TPU v7x, 256 devices: a whole 4x4x8 slice. The times are simulated.
256 devices in a mesh: section: 16 (over x, y), seq: 16 (over z, core).
Axes of the slice: x: 4, y: 4, z: 8, core: 2. Of those that a mesh axis runs over, the one named last changes fastest.
Arguments:
- inputs: bfloat16 [4, 8192, 1536], P(None, 'seq'), may hold values from -40 to 40
- weights: bfloat16 [2, 5, 1536, 1536], P(None, None, None, 'section'), may hold values from -0.0625 to 0.0625
- gains: float32 [2, 1536], replicated, may hold values from 0.1 to 1.9
Outputs:
- activations: bfloat16 [2, 4, 8192, 1536], P(None, None, 'seq', 'section')
All inputs are finite; a program needn't handle non-finite values.
Results may differ from a plain program's by a relative error of at most 0.0044.
Values may be sent and summed in bfloat16 or wider, within the bound.
No kernel may reach another device: no remote copies, remote signals or barrier semaphores. Data moves between devices by JAX's collectives and lax.ppermute only.
A program may use at most 128 MiB of HBM per device.

v0:
```python
import jax
import jax.numpy as jnp
from jax import lax
from jax.sharding import PartitionSpec as P


def with_halo(value, sides, width):
    for axis, dim in sides:
        count, length = (lax.axis_size(axis), value.shape[dim])
        up = [(i, (i + 1) % count) for i in range(count - 1)]
        down = [(j, i) for i, j in up]
        last = lax.slice_in_dim(value, length - width, length, axis=dim)
        initial = lax.slice_in_dim(value, 0, width, axis=dim)
        before = lax.ppermute(last, axis, up)
        after = lax.ppermute(initial, axis, down)
        value = jnp.concatenate([before, value, after], axis=dim)
    return value


def convolve(padded, kernel):
    count = padded.shape[1] - 4
    total = jnp.zeros((padded.shape[0], count, kernel.shape[2]), jnp.float32)
    for k in range(5):
        total = total + jnp.einsum(
            "brc,co->bro", padded[:, k : k + count], kernel[k], preferred_element_type=jnp.float32
        )
    return total


def normed(current, gain):
    values = current.astype(jnp.float32)
    scale = lax.rsqrt(jnp.mean(values * values, axis=-1, keepdims=True) + 1e-06)
    return jax.nn.gelu(values * scale * gain).astype(jnp.bfloat16)


def neighbours(hidden):
    return with_halo(hidden, (("seq", 1),), 2)


def local(inputs, weights, gains):
    share = weights.shape[3]
    begin = lax.axis_index("section") * share
    hidden = normed(inputs, gains[0])
    conv = convolve(neighbours(hidden), weights[0])
    own = lax.dynamic_slice_in_dim(inputs, begin, share, 2)
    current = (own.astype(jnp.float32) + conv).astype(jnp.bfloat16)
    results = [current]
    kernel = weights[1]
    whole = lax.all_gather(current, "section", axis=2, tiled=True)
    conv = convolve(neighbours(normed(whole, gains[1])), kernel)
    current = (current.astype(jnp.float32) + conv).astype(jnp.bfloat16)
    results.append(current)
    return jnp.stack(results, axis=0)


def solution(mesh):
    in_specs = (P(None, "seq", None), P(None, None, None, "section"), P())
    out_specs = P(None, None, "seq", "section")
    return jax.shard_map(local, mesh=mesh, in_specs=in_specs, out_specs=out_specs, check_vma=False)
```

profile of v0, /device:TPU:1, one launch (start us, length us, event | category | flops | bytes accessed | tf_op | source)
XLA Modules:
  0.0 165.4 jit_solution(3972784400976625223)
XLA Ops:
  6.5 4.2 %fusion = f32[4,512]{1,0:T(4,128)S(1)} fusion(bf16[4,512,1536]{2,1,0:T(8,128)(2,1)} %param.3), kind=kLoop, calls=%fused_computation.6 | loop fusion | flops 9435136 | bytes 6299648 | tf_op jit(solution)/shard_map/reduce_sum | solution.py:32
  10.8 0.3 copy-done.1
  11.2 5.8 %fusion.4 = bf16[4,512,1536]{2,1,0:T(8,128)(2,1)S(1)} fusion(bf16[4,512,1536]{2,1,0:T(8,128)(2,1)S(1)} %copy-done.1, f32[1536]{0:T(1024)S(1)} %get-tuple-element.6, f32[4,512]{1,0:T(4,128)S(1)} %add_rsqrt_fusion.1), kind=kLoop, calls=%fused_computation.10 | loop fusion | flops 37748736 | bytes 12597248 | tf_op jit(solution)/shard_map/convert_element_type | solution.py:33
  16.9 2.7 %copy-done.2 = bf16[4,512,1536]{2,1,0:T(8,128)(2,1)} copy-done((bf16[4,512,1536]{2,1,0:T(8,128)(2,1)}, bf16[4,512,1536]{2,1,0:T(8,128)(2,1)S(1)}, u32[]{:S(2)}) %copy-start.2) | copy-done | bytes 6291480
  19.6 4.9 %collective-permute-start = (bf16[4,2,1536]{2,1,0:T(2,128)(2,1)S(1)}, bf16[4,2,1536]{2,1,0:T(2,128)(2,1)S(1)}, u32[]{:S(2)}, u32[]{:S(2)}) collective-permute-start(bf16[4,2,1536]{2,1,0:T(2,128)(2,1)S(1)} %get-tuple-element.9), channel_id=1, source_target_pairs={{0,1},{1,2},{2,3},{3,4},{4,5},{5,6},{6,7},{7,8},{8,9},{9,10},{10,1... | collective-permute-start | bytes 73736 | tf_op jit(solution)/shard_map/ppermute | solution.py:14
  24.6 2.1 %collective-permute-start.1 = (bf16[4,2,1536]{2,1,0:T(2,128)(2,1)S(1)}, bf16[4,2,1536]{2,1,0:T(2,128)(2,1)S(1)}, u32[]{:S(2)}, u32[]{:S(2)}) collective-permute-start(bf16[4,2,1536]{2,1,0:T(2,128)(2,1)S(1)} %get-tuple-element.10), channel_id=1, source_target_pairs={{1,0},{2,1},{3,2},{4,3},{5,4},{6,5},{7,6},{8,7},{9,8},{10,9},{11,1... | collective-permute-start | bytes 73736 | tf_op jit(solution)/shard_map/ppermute | solution.py:15
  26.7 4.8 %fusion.83 = f32[4,512,96]{1,2,0:T(8,128)S(1)} fusion(bf16[4,512,1536]{2,1,0:T(8,128)(2,1)} %copy-done.2, bf16[2,5,1536,96]{2,3,1,0:T(8,128)(2,1)} %param.4), kind=kOutput, calls=%fused_computation.75 | convolution fusion | flops 603979776 | bytes 7372800 | tf_op jit(solution)/shard_map/brc,co->bro/dot_general | solution.py:24
  31.5 1.5 constant_dynamic-slice_fusion
  33.0 1.0 copy.18
  33.9 0.0 collective-permute-done.1
  33.9 4.8 %fusion.28 = f32[4,512,96]{1,2,0:T(8,128)S(1)} fusion(bf16[4,2,1536]{2,1,0:T(2,128)(2,1)S(1)} %collective-permute-done.1, bf16[4,512,1536]{2,1,0:T(8,128)(2,1)} %copy-done.2, bf16[2,5,1536,96]{2,3,1,0:T(8,128)(2,1)} %param.4), kind=kOutput, calls=%fused_computation.45 | convolution fusion | flops 616562688 | bytes 7397376 | tf_op jit(solution)/shard_map/brc,co->bro/dot_general | solution.py:24
  38.8 0.0 collective-permute-done
  38.8 3.0 %fusion.30 = f32[4,512,96]{1,2,0:T(8,128)S(1)} fusion(bf16[4,512,1536]{2,1,0:T(8,128)(2,1)S(1)} %bitcast.58, bf16[4,2,1536]{2,1,0:T(2,128)(2,1)S(1)} %collective-permute-done, bf16[2,5,1536,96]{2,3,1,0:T(8,128)(2,1)} %param.4), kind=kOutput, calls=%fused_computation.48 | convolution fusion | flops 616562688 | bytes 7397376 | tf_op jit(solution)/shard_map/brc,co->bro/dot_general | solution.py:24
  41.8 0.0 copy-start.3
  41.8 3.1 %fusion.64 = f32[4,512,96]{1,2,0:T(8,128)S(1)} fusion(f32[4,512,96]{1,2,0:T(8,128)S(1)} %fusion.83, f32[4,512,96]{1,2,0:T(8,128)S(1)} %fusion.30, bf16[4,2,1536]{2,1,0:T(2,128)(2,1)S(1)} %collective-permute-done, bf16[4,512,1536]{2,1,0:T(8,128)(2,1)S(1)} %bitcast.58, bf16[2,5,1536,96]{2,3,1,0:T(8,128)(2,1)} %param.4), kind=kOutput, calls=%fused_computation.62 | convolution fusion | flops 616955904 | bytes 8970240 | tf_op jit(solution)/shard_map/brc,co->bro/dot_general | solution.py:24
  44.9 3.5 %fusion.67 = bf16[4,512,96]{1,2,0:T(8,128)(2,1)S(1)} fusion(f32[4,512,96]{1,2,0:T(8,128)S(1)} %fusion.28, f32[4,512,96]{1,2,0:T(8,128)S(1)} %fusion.64, bf16[4,512,1536]{2,1,0:T(8,128)(2,1)S(1)} %bitcast.58, bf16[4,2,1536]{2,1,0:T(2,128)(2,1)S(1)} %collective-permute-done.1, bf16[4,512,96]{1,2,0:T(8,128)(2,1)S(1)} %copy-done.3, ...), kind=kOutput, calls=%fused_computation.63 | convolution fusion | flops 617545728 | bytes 8970240 | tf_op jit(solution)/shard_map/brc,co->bro/dot_general | solution.py:24
  48.4 1.1 copy.16
  49.5 0.0 all-gather.2.cloned.1.call-update
  49.5 70.2 %all-gather.2.cloned.1.call-done = bf16[4,512,1536]{1,0,2:T(4,128)(2,1)} async-done(((bf16[4,512,96]{1,0,2:T(4,128)(2,1)}), bf16[4,512,1536]{1,0,2:T(4,128)(2,1)}) %all-gather.2.cloned.1.call-update) | async-done | bytes 6291472 | tf_op jit(solution)/shard_map/all_gather | solution.py:49
  119.7 10.6 %copy.17 = bf16[4,512,1536]{2,1,0:T(8,128)(2,1)} copy(bf16[4,512,1536]{1,0,2:T(4,128)(2,1)} %all-gather.2.cloned.1.call-done) | data formatting | bytes 12582912 | tf_op jit(solution)/shard_map/all_gather | solution.py:49
  130.3 4.2 %fusion.9 = f32[4,512]{1,0:T(4,128)S(1)} fusion(bf16[4,512,1536]{2,1,0:T(8,128)(2,1)} %copy.17), kind=kLoop, calls=%fused_computation.15 | loop fusion | flops 9435136 | bytes 6299648 | tf_op jit(solution)/shard_map/reduce_sum | solution.py:32
  134.6 0.4 copy-done
  134.9 5.8 %fusion.13 = bf16[4,512,1536]{2,1,0:T(8,128)(2,1)S(1)} fusion(bf16[4,512,1536]{2,1,0:T(8,128)(2,1)S(1)} %copy-done, f32[1536]{0:T(1024)S(1)} %get-tuple-element.5, f32[4,512]{1,0:T(4,128)S(1)} %add_rsqrt_fusion), kind=kLoop, calls=%fused_computation.19 | loop fusion | flops 37748736 | bytes 12597248 | tf_op jit(solution)/shard_map/convert_element_type | solution.py:33
  140.8 2.6 %collective-permute-start.3 = (bf16[4,2,1536]{2,1,0:T(2,128)(2,1)S(1)}, bf16[4,2,1536]{2,1,0:T(2,128)(2,1)S(1)}, u32[]{:S(2)}, u32[]{:S(2)}) collective-permute-start(bf16[4,2,1536]{2,1,0:T(2,128)(2,1)S(1)} %get-tuple-element.8), channel_id=1, source_target_pairs={{1,0},{2,1},{3,2},{4,3},{5,4},{6,5},{7,6},{8,7},{9,8},{10,9},{11,1... | collective-permute-start | bytes 73736 | tf_op jit(solution)/shard_map/ppermute | solution.py:15
  143.4 2.0 %fusion.77 = f32[4,512,96]{1,2,0:T(8,128)S(1)} fusion(bf16[4,512,1536]{2,1,0:T(8,128)(2,1)S(1)} %fusion.13, bf16[2,5,1536,96]{2,3,1,0:T(8,128)(2,1)S(1)} %copy-done.4), kind=kOutput, calls=%fused_computation.69 | convolution fusion | flops 603979776 | bytes 7372800 | tf_op jit(solution)/shard_map/brc,co->bro/dot_general | solution.py:24
  145.4 3.3 %collective-permute-start.2 = (bf16[4,2,1536]{2,1,0:T(2,128)(2,1)S(1)}, bf16[4,2,1536]{2,1,0:T(2,128)(2,1)S(1)}, u32[]{:S(2)}, u32[]{:S(2)}) collective-permute-start(bf16[4,2,1536]{2,1,0:T(2,128)(2,1)S(1)} %get-tuple-element.7), channel_id=1, source_target_pairs={{0,1},{1,2},{2,3},{3,4},{4,5},{5,6},{6,7},{7,8},{8,9},{9,10},{10,1... | collective-permute-start | bytes 73736 | tf_op jit(solution)/shard_map/ppermute | solution.py:14
  148.7 2.1 %fusion.24 = f32[4,512,96]{1,2,0:T(8,128)S(1)} fusion(bf16[4,2,1536]{2,1,0:T(2,128)(2,1)S(1)} %collective-permute-done.3, bf16[4,512,1536]{2,1,0:T(8,128)(2,1)S(1)} %fusion.13, bf16[2,5,1536,96]{2,3,1,0:T(8,128)(2,1)S(1)} %copy-done.4), kind=kOutput, calls=%fused_computation.39 | convolution fusion | flops 616562688 | bytes 7397376 | tf_op jit(solution)/shard_map/brc,co->bro/dot_general | solution.py:24
  150.8 0.0 collective-permute-done.2
  150.8 2.1 %fusion.26 = f32[4,512,96]{1,2,0:T(8,128)S(1)} fusion(bf16[4,512,1536]{2,1,0:T(8,128)(2,1)S(1)} %fusion.13, bf16[4,2,1536]{2,1,0:T(2,128)(2,1)S(1)} %collective-permute-done.2, bf16[2,5,1536,96]{2,3,1,0:T(8,128)(2,1)S(1)} %copy-done.4), kind=kOutput, calls=%fused_computation.42 | convolution fusion | flops 616562688 | bytes 7397376 | tf_op jit(solution)/shard_map/brc,co->bro/dot_general | solution.py:24
  152.9 2.1 %fusion.49 = f32[4,512,96]{1,2,0:T(8,128)S(1)} fusion(f32[4,512,96]{1,2,0:T(8,128)S(1)} %fusion.77, f32[4,512,96]{1,2,0:T(8,128)S(1)} %fusion.26, bf16[4,2,1536]{2,1,0:T(2,128)(2,1)S(1)} %collective-permute-done.2, bf16[4,512,1536]{2,1,0:T(8,128)(2,1)S(1)} %fusion.13, bf16[2,5,1536,96]{2,3,1,0:T(8,128)(2,1)S(1)} %copy-done.4), kind=kOutput, calls=%fused_computation.57 | convolution fusion | flops 616955904 | bytes 8970240 | tf_op jit(solution)/shard_map/brc,co->bro/dot_general | solution.py:24
  155.0 2.6 %fusion.70 = bf16[1,4,512,96]{2,3,1,0:T(8,128)(2,1)S(1)} fusion(bf16[4,512,96]{1,2,0:T(8,128)(2,1)S(1)} %fusion.67, f32[4,512,96]{1,2,0:T(8,128)S(1)} %fusion.24, f32[4,512,96]{1,2,0:T(8,128)S(1)} %fusion.49, bf16[4,512,1536]{2,1,0:T(8,128)(2,1)S(1)} %fusion.13, bf16[4,2,1536]{2,1,0:T(2,128)(2,1)S(1)} %collective-permute-done.3, ...), kind=kOutput, calls=%fused_computation.66 | convolution fusion | flops 617545728 | bytes 8970240 | tf_op jit(solution)/shard_map/brc,co->bro/dot_general | solution.py:24
  157.6 0.9 pad_maximum_fusion.8
  (20 shorter events, 0.2 us)
Async XLA Ops:
  6.5 4.3 %copy-start.5 = (f32[2,1536]{1,0:T(2,128)S(1)}, f32[2,1536]{1,0:T(2,128)}, u32[]{:S(2)}) copy-start(f32[2,1536]{1,0:T(2,128)} %param.5) | copy-start | bytes 36868
  6.5 113.2 %all-gather.2.cloned.1.call-start = ((), (), s32[]{:S(2)}) async-start(), calls=%async_computation | async-start | bytes 6684672 | tf_op jit(solution)/shard_map/all_gather | solution.py:49
  6.5 4.6 %copy-start.1 = (bf16[4,512,1536]{2,1,0:T(8,128)(2,1)S(1)}, bf16[4,512,1536]{2,1,0:T(8,128)(2,1)}, u32[]{:S(2)}) copy-start(bf16[4,512,1536]{2,1,0:T(8,128)(2,1)} %param.3) | copy-start | bytes 18874372
  16.9 2.7 %copy-start.2 = (bf16[4,512,1536]{2,1,0:T(8,128)(2,1)}, bf16[4,512,1536]{2,1,0:T(8,128)(2,1)S(1)}, u32[]{:S(2)}) copy-start(bf16[4,512,1536]{2,1,0:T(8,128)(2,1)S(1)} %fusion.4) | copy-start | bytes 18874372
  19.6 19.1 %collective-permute-start = (bf16[4,2,1536]{2,1,0:T(2,128)(2,1)S(1)}, bf16[4,2,1536]{2,1,0:T(2,128)(2,1)S(1)}, u32[]{:S(2)}, u32[]{:S(2)}) collective-permute-start(bf16[4,2,1536]{2,1,0:T(2,128)(2,1)S(1)} %get-tuple-element.9), channel_id=1, source_target_pairs={{0,1},{1,2},{2,3},{3,4},{4,5},{5,6},{6,7},{7,8},{8,9},{9,10},{10,1... | collective-permute-start | bytes 73736 | tf_op jit(solution)/shard_map/ppermute | solution.py:14
  24.6 9.3 %collective-permute-start.1 = (bf16[4,2,1536]{2,1,0:T(2,128)(2,1)S(1)}, bf16[4,2,1536]{2,1,0:T(2,128)(2,1)S(1)}, u32[]{:S(2)}, u32[]{:S(2)}) collective-permute-start(bf16[4,2,1536]{2,1,0:T(2,128)(2,1)S(1)} %get-tuple-element.10), channel_id=1, source_target_pairs={{1,0},{2,1},{3,2},{4,3},{5,4},{6,5},{7,6},{8,7},{9,8},{10,9},{11,1... | collective-permute-start | bytes 73736 | tf_op jit(solution)/shard_map/ppermute | solution.py:15
  33.0 5.8 %slice-start = ((s8[6291456]{0:T(1024)(128)(4,1)}), s8[2097152]{0:T(1024)(128)(4,1)S(1)}, s32[]{:S(2)}) async-start(s8[6291456]{0:T(1024)(128)(4,1)} %bitcast.57), calls=%async_computation.1 | async-start | bytes 4194304
  33.9 4.9 %slice-start.1 = ((s8[6291456]{0:T(1024)(128)(4,1)}), s8[4194304]{0:T(1024)(128)(4,1)S(1)}, s32[]{:S(2)}) async-start(s8[6291456]{0:T(1024)(128)(4,1)} %bitcast.57), calls=%async_computation.2 | async-start | bytes 8388608
  41.8 3.1 %copy-start.3 = (bf16[4,512,96]{1,2,0:T(8,128)(2,1)S(1)}, bf16[4,512,96]{1,2,0:T(8,128)(2,1)}, u32[]{:S(2)}) copy-start(bf16[4,512,96]{1,2,0:T(8,128)(2,1)} %copy.18) | copy-start | bytes 1179652
  130.3 4.6 %copy-start = (bf16[4,512,1536]{2,1,0:T(8,128)(2,1)S(1)}, bf16[4,512,1536]{2,1,0:T(8,128)(2,1)}, u32[]{:S(2)}) copy-start(bf16[4,512,1536]{2,1,0:T(8,128)(2,1)} %copy.17) | copy-start | bytes 18874372
  134.9 8.4 %copy-start.4 = (bf16[2,5,1536,96]{2,3,1,0:T(8,128)(2,1)S(1)}, bf16[2,5,1536,96]{2,3,1,0:T(8,128)(2,1)}, u32[]{:S(2)}) copy-start(bf16[2,5,1536,96]{2,3,1,0:T(8,128)(2,1)} %param.4) | copy-start | bytes 8847364
  140.8 7.9 %collective-permute-start.3 = (bf16[4,2,1536]{2,1,0:T(2,128)(2,1)S(1)}, bf16[4,2,1536]{2,1,0:T(2,128)(2,1)S(1)}, u32[]{:S(2)}, u32[]{:S(2)}) collective-permute-start(bf16[4,2,1536]{2,1,0:T(2,128)(2,1)S(1)} %get-tuple-element.8), channel_id=1, source_target_pairs={{1,0},{2,1},{3,2},{4,3},{5,4},{6,5},{7,6},{8,7},{9,8},{10,9},{11,1... | collective-permute-start | bytes 73736 | tf_op jit(solution)/shard_map/ppermute | solution.py:15
  145.4 5.4 %collective-permute-start.2 = (bf16[4,2,1536]{2,1,0:T(2,128)(2,1)S(1)}, bf16[4,2,1536]{2,1,0:T(2,128)(2,1)S(1)}, u32[]{:S(2)}, u32[]{:S(2)}) collective-permute-start(bf16[4,2,1536]{2,1,0:T(2,128)(2,1)S(1)} %get-tuple-element.7), channel_id=1, source_target_pairs={{0,1},{1,2},{2,3},{3,4},{4,5},{5,6},{6,7},{7,8},{8,9},{9,10},{10,1... | collective-permute-start | bytes 73736 | tf_op jit(solution)/shard_map/ppermute | solution.py:14
Sparse Core Ops, SparseCore 0:
  49.6 70.0 all-gather.1
where the time goes:
time: 166 us; the launch traced here: 165 us
  waiting for transfers between devices  70.3 us (42%)
  matrix products  30.1 us (18%)
  other arithmetic  21 us (13%)
  local copies, waits for them, and re-layouts  17.5 us (11%)
  between operations  13.6 us (8%)
  starting transfers between devices  12.9 us (8%)
    all_gather x1, waiting for transfers between devices, local(): whole = lax.all_gather(current, 'section', axis=2, tiled=True)  70.2 us
    dot_general x10, matrix products, convolve(): jnp.einsum('brc,co->bro', padded[:, k:k + count], kernel[k], preferred_el...  30.1 us
    convert_element_type x2, other arithmetic, normed(): return jax.nn.gelu(values * scale * gain).astype(jnp.bfloat16)  11.5 us
    all_gather x1, local copies, waits for them, and re-layouts, local(): whole = lax.all_gather(current, 'section', axis=2, tiled=True)  10.6 us
    reduce_sum x2, other arithmetic, normed(): scale = lax.rsqrt(jnp.mean(values * values, axis=-1, keepdims=True) + 1e-06)  8.46 us
    ppermute x2, starting transfers between devices, with_halo(): before = lax.ppermute(last, axis, up)  8.24 us
    ppermute x2, starting transfers between devices, with_halo(): after = lax.ppermute(initial, axis, down)  4.68 us
    unnamed x17, local copies, waits for them, and re-layouts  4.3 us
  transfers between devices with their start and end apart: 5, of which 1 were waited for; matrix products, arithmetic and copies ran while one was open for 10% of the time, Pallas kernels for 0%

commit v1 on v0

v1 whole, which is shorter than its diff:
```python
import functools
import jax
import jax.numpy as jnp
from jax import lax
from jax.experimental import pallas as pl
from jax.experimental.pallas import tpu as pltpu
from jax.sharding import Mesh, PartitionSpec as P

C = 1536
T = 96
R = 480
S = 512
B = 208
NT = (((1,), (1,)), ((), ()))


def gelu(z):
    return 0.5 * z * (1.0 + jnp.tanh(0.7978845608028654 * (z + 0.044715 * z * z * z)))


def combine(wide):
    n = wide.shape[1]
    total = wide[2 * T : 3 * T]
    for k in (0, 1, 3, 4):
        total = total + pltpu.roll(wide[k * T : (k + 1) * T], (2 - k) % n, 1)
    return total


def first_kernel(info, x_ref, halo_ref, gain_ref, w_ref, o_ref, h_ref, y_ref, hy_ref, hr_ref, base):
    i = pl.program_id(0)
    start = pl.multiple_of(info[0] * 128, 128)
    off = info[1]
    row = lax.broadcasted_iota(jnp.int32, (T, 256), 0)
    col = lax.broadcasted_iota(jnp.int32, (T, 256), 1)
    pick = jnp.where(col == row + off, 1.0, 0.0).astype(jnp.bfloat16)

    def hidden(v):
        v = v.astype(jnp.float32)
        scale = lax.rsqrt(jnp.sum(v * v, axis=-1, keepdims=True) * (1.0 / C) + 1e-06)
        return gelu(v * scale * gain_ref[...]).astype(jnp.bfloat16)

    @pl.when(i == 0)
    def _():
        hh = hidden(halo_ref[...])
        hy_ref[...] = jnp.zeros_like(hy_ref)
        hr_ref[...] = jnp.zeros_like(hr_ref)
        hy = lax.dot_general(w_ref[...], hh, NT, preferred_element_type=jnp.float32)
        hx = lax.dot_general(pick, halo_ref[:, pl.ds(start, 256)], NT, preferred_element_type=jnp.float32)
        hy_ref[:, 0:32] = hy
        hy_ref[2 * T : 3 * T, 0:32] += hx

    def body(r, _):
        at = pl.ds(pl.multiple_of(r * 16, 16), 16)
        h_ref[at, :] = hidden(x_ref[0, at, :])
        return _

    lax.fori_loop(0, S // 16, body, 0, unroll=2)
    y_ref[:, 128 : 128 + S] = lax.dot_general(w_ref[...], h_ref[...], NT, preferred_element_type=jnp.float32)
    y_ref[2 * T : 3 * T, 128 : 128 + S] += lax.dot_general(
        pick, x_ref[0, :, pl.ds(start, 256)], NT, preferred_element_type=jnp.float32
    )
    b = base + i
    y_ref[:, 0:128] = pltpu.roll(hy_ref[...], lax.rem(124 - 8 * b + 128, 128), 1)
    y_ref[:, 128 + S :] = pltpu.roll(hy_ref[...], lax.rem(256 - 8 * b - 4, 128), 1)
    out = combine(y_ref[...])
    o_ref[pl.ds(pl.multiple_of(i * T, 16), T), :] = out[:, 128 : 128 + S].astype(jnp.bfloat16)
    pad = jnp.zeros((32, 128), jnp.float32)
    left = jnp.concatenate([out[:, 0:128], pad], 0).T
    right = jnp.concatenate([out[:, 128 + S :], pad], 0).T
    keep_left = (info[2] > 0).astype(jnp.float32)
    keep_right = (info[3] > 0).astype(jnp.float32)
    line = jnp.concatenate(
        [left[126:127] * keep_left, left[127:128] * keep_left, right[0:1] * keep_right, right[1:2] * keep_right], 1
    )
    hr_ref[pl.ds(i, 1), :] = line
    o_ref[2 * T :, :] = hr_ref[...].astype(jnp.bfloat16)


def first(x, halo, gain, w, info, base):
    return pl.pallas_call(
        functools.partial(first_kernel, base=base),
        grid_spec=pltpu.PrefetchScalarGridSpec(
            num_scalar_prefetch=1,
            grid=(2,),
            in_specs=[
                pl.BlockSpec((1, S, C), lambda i, info: (base + i, 0, 0)),
                pl.BlockSpec((32, C), lambda i, info: (0, 0)),
                pl.BlockSpec((1, C), lambda i, info: (0, 0)),
                pl.BlockSpec((R, C), lambda i, info: (0, 0)),
            ],
            out_specs=pl.BlockSpec((B, S), lambda i, info: (0, 0)),
            scratch_shapes=[
                pltpu.VMEM((S, C), jnp.bfloat16),
                pltpu.VMEM((R, S + 256), jnp.float32),
                pltpu.VMEM((R, 128), jnp.float32),
                pltpu.VMEM((16, S), jnp.float32),
            ],
        ),
        out_shape=jax.ShapeDtypeStruct((B, S), jnp.bfloat16),
        compiler_params=pltpu.CompilerParams(dimension_semantics=("arbitrary",), vmem_limit_bytes=40 << 20),
        cost_estimate=pl.CostEstimate(flops=4 * S * R * C, bytes_accessed=2 * S * C * 2 + R * C * 2, transcendentals=2 * S * C),
        name="first",
    )(info, x, halo, gain, w)


def second_kernel(order, a0, a1, a2, a3, a4, gain_ref, w_ref, o_ref, h_ref, y_ref, e_ref, sq_ref):
    refs = [(a0, 4, 0), (a1, 4, 4), (a2, 4, 8), (a3, 2, 12), (a4, 2, 14)]
    n = 2 * S + 128
    sq_ref[...] = jnp.zeros_like(sq_ref)

    for ref, count, at in refs:
        def gather(k, _, ref=ref, at=at):
            row = pl.multiple_of(k * B, 16)
            lines = ref[pl.ds(row + 2 * T, 16), :].astype(jnp.float32)
            tile = jnp.concatenate(
                [lines[j : j + 1, 128 * q : 128 * q + 128] for j in range(2) for q in range(4)]
                + [jnp.zeros((120, 128), jnp.float32)],
                0,
            )
            edge = tile.T[0:T]
            e_ref[pl.ds(pl.multiple_of((at + k) * T, 16), T), :] = edge
            sq = edge * edge
            acc = sq_ref[:, 2 * S :]
            for g in range(T // 8):
                acc = acc + sq[8 * g : 8 * g + 8]
            sq_ref[:, 2 * S :] = acc
            for j in range(2):
                v = ref[pl.ds(row + j * T, T), :].astype(jnp.float32)
                v = v * v
                acc = sq_ref[:, j * S : j * S + S]
                for g in range(T // 8):
                    acc = acc + v[8 * g : 8 * g + 8]
                sq_ref[:, j * S : j * S + S] = acc
            return _

        lax.fori_loop(0, count, gather, 0)

    total = jnp.sum(sq_ref[...], axis=0, keepdims=True)
    scale = lax.rsqrt(total * (1.0 / C) + 1e-06)
    sq_ref[...] = jnp.broadcast_to(scale, (8, n))

    for ref, count, at in refs:
        def apply(k, _, ref=ref, at=at):
            row = pl.multiple_of(k * B, 16)
            dest = pl.multiple_of(order[at + k] * T, 16)
            gain = gain_ref[pl.ds(dest, T), :]
            for j in range(2):
                for q in range(4):
                    lane = slice(j * S + 128 * q, j * S + 128 * q + 128)
                    v = ref[pl.ds(row + j * T, T), 128 * q : 128 * q + 128].astype(jnp.float32)
                    h_ref[pl.ds(dest, T), lane] = gelu(v * sq_ref[0:1, lane] * gain).astype(jnp.bfloat16)
            v = e_ref[pl.ds(pl.multiple_of((at + k) * T, 16), T), :]
            h_ref[pl.ds(dest, T), 2 * S :] = gelu(v * sq_ref[0:1, 2 * S :] * gain).astype(jnp.bfloat16)
            return _

        lax.fori_loop(0, count, apply, 0)

    y_ref[...] = jnp.dot(w_ref[...], h_ref[...], preferred_element_type=jnp.float32)
    for j in range(2):
        edge = y_ref[:, 2 * S :]
        wide = jnp.concatenate(
            [pltpu.roll(edge, 126 - 4 * j, 1), y_ref[:, j * S : j * S + S], pltpu.roll(edge, 126 - 4 * j, 1)], 1
        )
        out = combine(wide)[:, 128 : 128 + S] + a0[j * T : j * T + T, :].astype(jnp.float32)
        o_ref[j * T : j * T + T, :] = out.astype(jnp.bfloat16)


def second(parts, gain, w, order):
    vmem = pl.BlockSpec(memory_space=pltpu.VMEM)
    n = 2 * S + 128
    return pl.pallas_call(
        second_kernel,
        in_specs=[pl.BlockSpec(memory_space=pltpu.SMEM)] + [vmem] * 7,
        out_specs=vmem,
        out_shape=jax.ShapeDtypeStruct((2 * T, S), jnp.bfloat16),
        scratch_shapes=[
            pltpu.VMEM((C, n), jnp.bfloat16),
            pltpu.VMEM((R, n), jnp.float32),
            pltpu.VMEM((C, 128), jnp.float32),
            pltpu.VMEM((8, n), jnp.float32),
        ],
        compiler_params=pltpu.CompilerParams(vmem_limit_bytes=40 << 20),
        cost_estimate=pl.CostEstimate(flops=4 * S * R * C, bytes_accessed=2 * S * C * 2 + R * C * 2, transcendentals=2 * S * C),
        name="second",
    )(order, *parts, gain, w)


def shift(value, axis, d):
    return lax.ppermute(value, axis, [(i, (i + d) % 4) for i in range(4)])


def gather(block, f, s):
    below, above = shift(block, f, 1), shift(block, f, -1)
    far0, far1 = shift(below[:T], f, 1), shift(above[T:], f, -1)
    column = jnp.concatenate([block, below, above, far0, far1], 0)
    left, right = shift(column, s, 1), shift(column, s, -1)
    return [column, left, right, shift(left[: 2 * B], s, 1), shift(right[2 * B :], s, -1)]


def piece_order(f, s):
    def index(df, ds):
        at = {f: (lax.axis_index(f) + df) % 4, s: (lax.axis_index(s) + ds) % 4}
        return at["x"] * 4 + at["y"]

    rel = (0, -1, 1, 2)
    items = [index(r, d) for d in (0, -1, 1) for r in rel] + [index(r, 2) for r in rel]
    return jnp.stack(items).astype(jnp.int32)


def local(inputs, weights, gains):
    x, y = lax.axis_index("x"), lax.axis_index("y")
    sec = x * 4 + y
    seq = lax.axis_index("z") * 2 + lax.axis_index("core")
    w = weights.transpose(0, 1, 3, 2).reshape(2, R, C)
    up = [(i, i + 1) for i in range(15)]
    down = [(i + 1, i) for i in range(15)]
    before = lax.ppermute(inputs[:, S - 4 :], ("z", "core"), up)
    after = lax.ppermute(inputs[:, :4], ("z", "core"), down)
    halo = jnp.concatenate([before, after], 1).reshape(32, C)
    block = jnp.minimum(sec * T // 128, 10)
    info = jnp.stack([block, sec * T - block * 128, seq, 15 - seq]).astype(jnp.int32)
    g0 = gains[0:1]
    g1 = jnp.broadcast_to(gains[1][:, None], (C, 128))
    half0 = first(inputs, halo, g0, w[0], info, 0)
    half1 = first(inputs, halo, g0, w[0], info, 2)
    got0 = gather(half0, "y", "x")
    got1 = gather(half1, "x", "y")
    out0 = second(got0, g1, w[1], piece_order("y", "x"))
    out1 = second(got1, g1, w[1], piece_order("x", "y"))
    out = jnp.concatenate([half0[: 2 * T], half1[: 2 * T], out0, out1], 0)
    return out.reshape(2, 4, T, S).transpose(0, 1, 3, 2)


def solution(mesh):
    grid = Mesh(mesh.devices.reshape(4, 4, 8, 2), ("x", "y", "z", "core"))
    in_specs = (P(None, ("z", "core"), None), P(None, None, None, ("x", "y")), P())
    out_specs = P(None, None, ("z", "core"), ("x", "y"))
    return jax.shard_map(local, mesh=grid, in_specs=in_specs, out_specs=out_specs, check_vma=False)
```

time: 166 us -> 109 us (0.66)
  the two profiles are of different devices: /device:TPU:1 before, /device:TPU:96 now
where the time goes in v1:
time: 109 us
  Pallas kernels  35 us (32%)
  starting transfers between devices  29.9 us (27%)
  waiting for transfers between devices  28.9 us (27%)
  local copies, waits for them, and re-layouts  13.3 us (12%)
    ppermute x16, waiting for transfers between devices, shift(): return lax.ppermute(value, axis, [(i, (i + d) % 4) for i in range(4)])  28.9 us
    ppermute x16, starting transfers between devices, shift(): return lax.ppermute(value, axis, [(i, (i + d) % 4) for i in range(4)])  24.3 us
    pallas_call x2, Pallas kernels, first(): pl.pallas_call(functools.partial(first_kernel, base=base), grid_spec=pltp...  18.4 us
    pallas_call x2, Pallas kernels, second(): pl.pallas_call(second_kernel, in_specs=[pl.BlockSpec(memory_space=pltpu.S...  16.6 us
    unnamed x28, local copies, waits for them, and re-layouts  4.75 us
    ppermute x1, starting transfers between devices, local(): after = lax.ppermute(inputs[:, :4], ('z', 'core'), down)  3.64 us
  transfers between devices with their start and end apart: 18, of which 7 were waited for; matrix products, arithmetic and copies ran while one was open for 7% of the time, Pallas kernels for 8%

profile of v1, /device:TPU:96, one launch (start us, length us, event | category | flops | bytes accessed | tf_op | source)
XLA Modules:
  0.0 108.5 jit_solution(17139747052353912287)
XLA Ops:
  0.0 1.0 fusion
  1.0 1.9 %collective-permute-start = (bf16[4,4,1536]{2,1,0:T(4,128)(2,1)S(1)}, bf16[4,4,1536]{2,1,0:T(4,128)(2,1)S(1)}, u32[]{:S(2)}, u32[]{:S(2)}) collective-permute-start(bf16[4,4,1536]{2,1,0:T(4,128)(2,1)S(1)} %get-tuple-element.5), channel_id=1, source_target_pairs={{0,1},{1,2},{2,3},{3,4},{4,5},{5,6},{6,7},{7,8},{8,9},{9,10},{10,1... | collective-permute-start | bytes 147464 | tf_op jit(solution)/shard_map/ppermute | solution.py:217
  2.9 3.6 %collective-permute-start.1 = (bf16[4,4,1536]{2,1,0:T(4,128)(2,1)S(1)}, bf16[4,4,1536]{2,1,0:T(4,128)(2,1)S(1)}, u32[]{:S(2)}, u32[]{:S(2)}) collective-permute-start(bf16[4,4,1536]{2,1,0:T(4,128)(2,1)S(1)} %get-tuple-element.6), channel_id=1, source_target_pairs={{1,0},{2,1},{3,2},{4,3},{5,4},{6,5},{7,6},{8,7},{9,8},{10,9},{11,1... | collective-permute-start | bytes 147464 | tf_op jit(solution)/shard_map/ppermute | solution.py:218
  6.6 0.8 slice_reduce_fusion
  7.4 2.1 %fusion.1 = (bf16[1,5,96,1536]{3,2,1,0:T(8,128)(2,1)S(1)}, bf16[1,5,96,1536]{3,2,1,0:T(8,128)(2,1)S(1)}) fusion(bf16[2,5,96,1536]{3,2,1,0:T(8,128)(2,1)} %bitcast.32), kind=kLoop, calls=%fused_computation.15 | loop fusion | bytes 5898240 | tf_op jit(solution)/shard_map/slice | solution.py:228
  9.7 2.8 %copy-done = bf16[4,512,1536]{2,1,0:T(8,128)(2,1)S(1)} copy-done((bf16[4,512,1536]{2,1,0:T(8,128)(2,1)S(1)}, bf16[4,512,1536]{2,1,0:T(8,128)(2,1)}, u32[]{:S(2)}) %copy-start) | copy-done | bytes 6291480
  12.4 9.2 %first.3 = bf16[208,512]{1,0:T(8,128)(2,1)S(1)} custom-call(s32[4]{0:T(128)S(1)} %pad_add_fusion.info, bf16[4,512,1536]{2,1,0:T(8,128)(2,1)S(1)} %copy-done, bf16[32,1536]{1,0:T(8,128)(2,1)S(1)} %maximum_bitcast_fusion.halo_ref, f32[1,1536]{1,0:T(1,128)S(1)} %get-tuple-element.10.gain_ref, bf16[480,1536]{1,0:T(8,128)(2,1)S(1)} %bitcast.30), custom_call_target="tpu_custom_call" | custom-call | flops 1509949440 | bytes 4620288 | tf_op jit(solution)/shard_map/first/pallas_call | solution.py:80
  21.6 9.2 %first.2 = bf16[208,512]{1,0:T(8,128)(2,1)S(1)} custom-call(s32[4]{0:T(128)S(1)} %pad_add_fusion.info, bf16[4,512,1536]{2,1,0:T(8,128)(2,1)S(1)} %copy-done, bf16[32,1536]{1,0:T(8,128)(2,1)S(1)} %maximum_bitcast_fusion.halo_ref, f32[1,1536]{1,0:T(1,128)S(1)} %get-tuple-element.10.gain_ref, bf16[480,1536]{1,0:T(8,128)(2,1)S(1)} %bitcast.31), custom_call_target="tpu_custom_call" | custom-call | flops 1509949440 | bytes 4620288 | tf_op jit(solution)/shard_map/first/pallas_call | solution.py:80
  30.8 3.1 %collective-permute-start.3 = (bf16[208,512]{1,0:T(8,128)(2,1)S(1)}, bf16[208,512]{1,0:T(8,128)(2,1)S(1)}, u32[]{:S(2)}, u32[]{:S(2)}) collective-permute-start(bf16[208,512]{1,0:T(8,128)(2,1)S(1)} %first.2), channel_id=1, source_target_pairs={{0,48},{16,0},{32,16},{48,32},{1,49},{17,1},{33,17},{49,33},{2,50}... | collective-permute-start | bytes 638984 | tf_op jit(solution)/shard_map/ppermute | solution.py:189
  33.9 2.8 %collective-permute-start.11 = (bf16[208,512]{1,0:T(8,128)(2,1)S(1)}, bf16[208,512]{1,0:T(8,128)(2,1)S(1)}, u32[]{:S(2)}, u32[]{:S(2)}) collective-permute-start(bf16[208,512]{1,0:T(8,128)(2,1)S(1)} %first.3), channel_id=1, source_target_pairs={{0,192},{64,0},{128,64},{192,128},{1,193},{65,1},{129,65},{193,129... | collective-permute-start | bytes 638984 | tf_op jit(solution)/shard_map/ppermute | solution.py:189
  36.7 0.6 collective-permute-done.3
  37.3 3.8 %collective-permute-start.5 = (bf16[112,512]{1,0:T(8,128)(2,1)S(1)}, bf16[112,512]{1,0:T(8,128)(2,1)S(1)}, u32[]{:S(2)}, u32[]{:S(2)}) collective-permute-start(bf16[112,512]{1,0:T(8,128)(2,1)S(1)} %slice.72), channel_id=1, source_target_pairs={{0,48},{16,0},{32,16},{48,32},{1,49},{17,1},{33,17},{49,33},{2,50}... | collective-permute-start | bytes 344072 | tf_op jit(solution)/shard_map/ppermute | solution.py:189
  41.4 2.8 %collective-permute-start.13 = (bf16[112,512]{1,0:T(8,128)(2,1)S(1)}, bf16[112,512]{1,0:T(8,128)(2,1)S(1)}, u32[]{:S(2)}, u32[]{:S(2)}) collective-permute-start(bf16[112,512]{1,0:T(8,128)(2,1)S(1)} %slice.77), channel_id=1, source_target_pairs={{0,192},{64,0},{128,64},{192,128},{1,193},{65,1},{129,65},{193,129... | collective-permute-start | bytes 344072 | tf_op jit(solution)/shard_map/ppermute | solution.py:189
  44.5 6.2 %collective-permute-done.12 = bf16[96,512]{1,0:T(8,128)(2,1)S(1)} collective-permute-done((bf16[96,512]{1,0:T(8,128)(2,1)S(1)}, bf16[96,512]{1,0:T(8,128)(2,1)S(1)}, u32[]{:S(2)}, u32[]{:S(2)}) %collective-permute-start.12) | collective-permute-done | bytes 98336 | tf_op jit(solution)/shard_map/ppermute | solution.py:189
  50.8 3.9 %collective-permute-start.15 = (bf16[832,512]{1,0:T(8,128)(2,1)S(1)}, bf16[832,512]{1,0:T(8,128)(2,1)S(1)}, u32[]{:S(2)}, u32[]{:S(2)}) collective-permute-start(bf16[832,512]{1,0:T(8,128)(2,1)S(1)} %constant_dynamic-update-slice_fusion.5.a0), channel_id=1, source_target_pairs={{0,48},{16,0},{32,16},{48,32},{1,49},{17,1},{33,17},{49,33},{2,50}... | collective-permute-start | bytes 2555912 | tf_op jit(solution)/shard_map/ppermute | solution.py:189
  54.8 2.0 %collective-permute-start.6 = (bf16[832,512]{1,0:T(8,128)(2,1)S(1)}, bf16[832,512]{1,0:T(8,128)(2,1)S(1)}, u32[]{:S(2)}, u32[]{:S(2)}) collective-permute-start(bf16[832,512]{1,0:T(8,128)(2,1)S(1)} %constant_dynamic-update-slice_fusion.a0), channel_id=1, source_target_pairs={{0,64},{64,128},{128,192},{192,0},{1,65},{65,129},{129,193},{193,1... | collective-permute-start | bytes 2555912 | tf_op jit(solution)/shard_map/ppermute | solution.py:189
  56.8 16.3 %collective-permute-done.15.a2 = bf16[832,512]{1,0:T(8,128)(2,1)S(1)} collective-permute-done((bf16[832,512]{1,0:T(8,128)(2,1)S(1)}, bf16[832,512]{1,0:T(8,128)(2,1)S(1)}, u32[]{:S(2)}, u32[]{:S(2)}) %collective-permute-start.15) | collective-permute-done | bytes 852000 | tf_op jit(solution)/shard_map/ppermute | solution.py:189
  73.1 0.8 slice.79
  73.9 3.7 %collective-permute-start.17 = (bf16[416,512]{1,0:T(8,128)(2,1)}, bf16[416,512]{1,0:T(8,128)(2,1)}, u32[]{:S(2)}, u32[]{:S(2)}) collective-permute-start(bf16[416,512]{1,0:T(8,128)(2,1)} %slice.79), channel_id=1, source_target_pairs={{0,48},{16,0},{32,16},{48,32},{1,49},{17,1},{33,17},{49,33},{2,50}... | collective-permute-start | bytes 1277960 | tf_op jit(solution)/shard_map/ppermute | solution.py:189
  77.6 0.8 slice.78
  78.4 0.8 slice.74
  79.2 0.9 copy-done.1
  80.1 0.8 slice.73
  80.9 0.9 copy-done.3
  81.8 2.0 %collective-permute-start.8 = (bf16[416,512]{1,0:T(8,128)(2,1)}, bf16[416,512]{1,0:T(8,128)(2,1)}, u32[]{:S(2)}, u32[]{:S(2)}) collective-permute-start(bf16[416,512]{1,0:T(8,128)(2,1)} %slice.73), channel_id=1, source_target_pairs={{0,64},{64,128},{128,192},{192,0},{1,65},{65,129},{129,193},{193,1... | collective-permute-start | bytes 1277960 | tf_op jit(solution)/shard_map/ppermute | solution.py:189
  84.1 1.0 slice.69
  85.1 1.3 %collective-permute-done.17.a4 = bf16[416,512]{1,0:T(8,128)(2,1)} collective-permute-done((bf16[416,512]{1,0:T(8,128)(2,1)}, bf16[416,512]{1,0:T(8,128)(2,1)}, u32[]{:S(2)}, u32[]{:S(2)}) %collective-permute-start.17) | collective-permute-done | bytes 426016 | tf_op jit(solution)/shard_map/ppermute | solution.py:189
  86.4 4.2 %collective-permute-done.16.a3 = bf16[416,512]{1,0:T(8,128)(2,1)} collective-permute-done((bf16[416,512]{1,0:T(8,128)(2,1)}, bf16[416,512]{1,0:T(8,128)(2,1)}, u32[]{:S(2)}, u32[]{:S(2)}) %collective-permute-start.16) | collective-permute-done | bytes 426016 | tf_op jit(solution)/shard_map/ppermute | solution.py:189
  90.6 0.3 broadcast_in_dim.8.gain_ref
  90.9 8.4 %second.3 = bf16[192,512]{1,0:T(8,128)(2,1)S(1)} custom-call(s32[16]{0:T(128)S(1)} %stack.107.order, bf16[832,512]{1,0:T(8,128)(2,1)S(1)} %copy-done.7, bf16[832,512]{1,0:T(8,128)(2,1)S(1)} %collective-permute-done.14.a1, bf16[832,512]{1,0:T(8,128)(2,1)S(1)} %collective-permute-done.15.a2, bf16[416,512]{1,0:T(8,128)(2,1)} %collective-permute-done.16.a3, ...), custom_call_target="tpu_custom_call" | custom-call | flops 1509949440 | bytes 4620288 | tf_op jit(solution)/shard_map/second/pallas_call | solution.py:171
  99.4 8.2 %second.2 = bf16[192,512]{1,0:T(8,128)(2,1)S(1)} custom-call(s32[16]{0:T(128)S(1)} %stack.106.order, bf16[832,512]{1,0:T(8,128)(2,1)S(1)} %copy-done.9, bf16[832,512]{1,0:T(8,128)(2,1)S(1)} %copy-done.4, bf16[832,512]{1,0:T(8,128)(2,1)S(1)} %copy-done.2, bf16[416,512]{1,0:T(8,128)(2,1)} %collective-permute-done.8.a3, ...), custom_call_target="tpu_custom_call" | custom-call | flops 1509949440 | bytes 4620288 | tf_op jit(solution)/shard_map/second/pallas_call | solution.py:171
  107.6 0.9 pad_maximum_fusion
  (57 shorter events, 1.1 us)
Async XLA Ops:
  1.0 8.6 %collective-permute-start = (bf16[4,4,1536]{2,1,0:T(4,128)(2,1)S(1)}, bf16[4,4,1536]{2,1,0:T(4,128)(2,1)S(1)}, u32[]{:S(2)}, u32[]{:S(2)}) collective-permute-start(bf16[4,4,1536]{2,1,0:T(4,128)(2,1)S(1)} %get-tuple-element.5), channel_id=1, source_target_pairs={{0,1},{1,2},{2,3},{3,4},{4,5},{5,6},{6,7},{7,8},{8,9},{9,10},{10,1... | collective-permute-start | bytes 147464 | tf_op jit(solution)/shard_map/ppermute | solution.py:217
  2.9 6.7 %collective-permute-start.1 = (bf16[4,4,1536]{2,1,0:T(4,128)(2,1)S(1)}, bf16[4,4,1536]{2,1,0:T(4,128)(2,1)S(1)}, u32[]{:S(2)}, u32[]{:S(2)}) collective-permute-start(bf16[4,4,1536]{2,1,0:T(4,128)(2,1)S(1)} %get-tuple-element.6), channel_id=1, source_target_pairs={{1,0},{2,1},{3,2},{4,3},{5,4},{6,5},{7,6},{8,7},{9,8},{10,9},{11,1... | collective-permute-start | bytes 147464 | tf_op jit(solution)/shard_map/ppermute | solution.py:218
  9.6 2.8 %copy-start = (bf16[4,512,1536]{2,1,0:T(8,128)(2,1)S(1)}, bf16[4,512,1536]{2,1,0:T(8,128)(2,1)}, u32[]{:S(2)}) copy-start(bf16[4,512,1536]{2,1,0:T(8,128)(2,1)} %x_ref.3) | copy-start | bytes 18874372
  30.8 13.7 %copy-start.5 = (bf16[208,512]{1,0:T(8,128)(2,1)}, bf16[208,512]{1,0:T(8,128)(2,1)S(1)}, u32[]{:S(2)}) copy-start(bf16[208,512]{1,0:T(8,128)(2,1)S(1)} %first.2) | copy-start | bytes 638980
  30.8 6.5 %collective-permute-start.3 = (bf16[208,512]{1,0:T(8,128)(2,1)S(1)}, bf16[208,512]{1,0:T(8,128)(2,1)S(1)}, u32[]{:S(2)}, u32[]{:S(2)}) collective-permute-start(bf16[208,512]{1,0:T(8,128)(2,1)S(1)} %first.2), channel_id=1, source_target_pairs={{0,48},{16,0},{32,16},{48,32},{1,49},{17,1},{33,17},{49,33},{2,50}... | collective-permute-start | bytes 638984 | tf_op jit(solution)/shard_map/ppermute | solution.py:189
  33.9 7.3 %collective-permute-start.2 = (bf16[208,512]{1,0:T(8,128)(2,1)S(1)}, bf16[208,512]{1,0:T(8,128)(2,1)S(1)}, u32[]{:S(2)}, u32[]{:S(2)}) collective-permute-start(bf16[208,512]{1,0:T(8,128)(2,1)S(1)} %first.2), channel_id=1, source_target_pairs={{0,16},{16,32},{32,48},{48,0},{1,17},{17,33},{33,49},{49,1},{2,18}... | collective-permute-start | bytes 638984 | tf_op jit(solution)/shard_map/ppermute | solution.py:189
  33.9 7.4 %collective-permute-start.11 = (bf16[208,512]{1,0:T(8,128)(2,1)S(1)}, bf16[208,512]{1,0:T(8,128)(2,1)S(1)}, u32[]{:S(2)}, u32[]{:S(2)}) collective-permute-start(bf16[208,512]{1,0:T(8,128)(2,1)S(1)} %first.3), channel_id=1, source_target_pairs={{0,192},{64,0},{128,64},{192,128},{1,193},{65,1},{129,65},{193,129... | collective-permute-start | bytes 638984 | tf_op jit(solution)/shard_map/ppermute | solution.py:189
  36.7 7.6 %collective-permute-start.10 = (bf16[208,512]{1,0:T(8,128)(2,1)S(1)}, bf16[208,512]{1,0:T(8,128)(2,1)S(1)}, u32[]{:S(2)}, u32[]{:S(2)}) collective-permute-start(bf16[208,512]{1,0:T(8,128)(2,1)S(1)} %first.3), channel_id=1, source_target_pairs={{0,64},{64,128},{128,192},{192,0},{1,65},{65,129},{129,193},{193,1... | collective-permute-start | bytes 638984 | tf_op jit(solution)/shard_map/ppermute | solution.py:189
  37.3 17.4 %collective-permute-start.5 = (bf16[112,512]{1,0:T(8,128)(2,1)S(1)}, bf16[112,512]{1,0:T(8,128)(2,1)S(1)}, u32[]{:S(2)}, u32[]{:S(2)}) collective-permute-start(bf16[112,512]{1,0:T(8,128)(2,1)S(1)} %slice.72), channel_id=1, source_target_pairs={{0,48},{16,0},{32,16},{48,32},{1,49},{17,1},{33,17},{49,33},{2,50}... | collective-permute-start | bytes 344072 | tf_op jit(solution)/shard_map/ppermute | solution.py:189
  41.3 13.4 %collective-permute-start.4 = (bf16[96,512]{1,0:T(8,128)(2,1)S(1)}, bf16[96,512]{1,0:T(8,128)(2,1)S(1)}, u32[]{:S(2)}, u32[]{:S(2)}) collective-permute-start(bf16[96,512]{1,0:T(8,128)(2,1)S(1)} %slice.71), channel_id=1, source_target_pairs={{0,16},{16,32},{32,48},{48,0},{1,17},{17,33},{33,49},{49,1},{2,18}... | collective-permute-start | bytes 294920 | tf_op jit(solution)/shard_map/ppermute | solution.py:189
  41.4 9.4 %collective-permute-start.13 = (bf16[112,512]{1,0:T(8,128)(2,1)S(1)}, bf16[112,512]{1,0:T(8,128)(2,1)S(1)}, u32[]{:S(2)}, u32[]{:S(2)}) collective-permute-start(bf16[112,512]{1,0:T(8,128)(2,1)S(1)} %slice.77), channel_id=1, source_target_pairs={{0,192},{64,0},{128,64},{192,128},{1,193},{65,1},{129,65},{193,129... | collective-permute-start | bytes 344072 | tf_op jit(solution)/shard_map/ppermute | solution.py:189
  44.3 6.4 %collective-permute-start.12 = (bf16[96,512]{1,0:T(8,128)(2,1)S(1)}, bf16[96,512]{1,0:T(8,128)(2,1)S(1)}, u32[]{:S(2)}, u32[]{:S(2)}) collective-permute-start(bf16[96,512]{1,0:T(8,128)(2,1)S(1)} %slice.76), channel_id=1, source_target_pairs={{0,64},{64,128},{128,192},{192,0},{1,65},{65,129},{129,193},{193,1... | collective-permute-start | bytes 294920 | tf_op jit(solution)/shard_map/ppermute | solution.py:189
  50.8 30.2 %copy-start.6 = (bf16[832,512]{1,0:T(8,128)(2,1)}, bf16[832,512]{1,0:T(8,128)(2,1)S(1)}, u32[]{:S(2)}) copy-start(bf16[832,512]{1,0:T(8,128)(2,1)S(1)} %constant_dynamic-update-slice_fusion.5.a0) | copy-start | bytes 2555908
  50.8 22.3 %collective-permute-start.15 = (bf16[832,512]{1,0:T(8,128)(2,1)S(1)}, bf16[832,512]{1,0:T(8,128)(2,1)S(1)}, u32[]{:S(2)}, u32[]{:S(2)}) collective-permute-start(bf16[832,512]{1,0:T(8,128)(2,1)S(1)} %constant_dynamic-update-slice_fusion.5.a0), channel_id=1, source_target_pairs={{0,48},{16,0},{32,16},{48,32},{1,49},{17,1},{33,17},{49,33},{2,50}... | collective-permute-start | bytes 2555912 | tf_op jit(solution)/shard_map/ppermute | solution.py:189
  54.6 23.0 %collective-permute-start.14 = (bf16[832,512]{1,0:T(8,128)(2,1)S(1)}, bf16[832,512]{1,0:T(8,128)(2,1)S(1)}, u32[]{:S(2)}, u32[]{:S(2)}) collective-permute-start(bf16[832,512]{1,0:T(8,128)(2,1)S(1)} %constant_dynamic-update-slice_fusion.5.a0), channel_id=1, source_target_pairs={{0,16},{16,32},{32,48},{48,0},{1,17},{17,33},{33,49},{49,1},{2,18}... | collective-permute-start | bytes 2555912 | tf_op jit(solution)/shard_map/ppermute | solution.py:189
  54.7 26.3 %copy-start.8 = (bf16[832,512]{1,0:T(8,128)(2,1)}, bf16[832,512]{1,0:T(8,128)(2,1)S(1)}, u32[]{:S(2)}) copy-start(bf16[832,512]{1,0:T(8,128)(2,1)S(1)} %constant_dynamic-update-slice_fusion.a0) | copy-start | bytes 2555908
  54.7 23.7 %collective-permute-start.7 = (bf16[832,512]{1,0:T(8,128)(2,1)S(1)}, bf16[832,512]{1,0:T(8,128)(2,1)S(1)}, u32[]{:S(2)}, u32[]{:S(2)}) collective-permute-start(bf16[832,512]{1,0:T(8,128)(2,1)S(1)} %constant_dynamic-update-slice_fusion.a0), channel_id=1, source_target_pairs={{0,192},{64,0},{128,64},{192,128},{1,193},{65,1},{129,65},{193,129... | collective-permute-start | bytes 2555912 | tf_op jit(solution)/shard_map/ppermute | solution.py:189
  54.8 25.4 %collective-permute-start.6 = (bf16[832,512]{1,0:T(8,128)(2,1)S(1)}, bf16[832,512]{1,0:T(8,128)(2,1)S(1)}, u32[]{:S(2)}, u32[]{:S(2)}) collective-permute-start(bf16[832,512]{1,0:T(8,128)(2,1)S(1)} %constant_dynamic-update-slice_fusion.a0), channel_id=1, source_target_pairs={{0,64},{64,128},{128,192},{192,0},{1,65},{65,129},{129,193},{193,1... | collective-permute-start | bytes 2555912 | tf_op jit(solution)/shard_map/ppermute | solution.py:189
  73.9 12.5 %collective-permute-start.17 = (bf16[416,512]{1,0:T(8,128)(2,1)}, bf16[416,512]{1,0:T(8,128)(2,1)}, u32[]{:S(2)}, u32[]{:S(2)}) collective-permute-start(bf16[416,512]{1,0:T(8,128)(2,1)} %slice.79), channel_id=1, source_target_pairs={{0,48},{16,0},{32,16},{48,32},{1,49},{17,1},{33,17},{49,33},{2,50}... | collective-permute-start | bytes 1277960 | tf_op jit(solution)/shard_map/ppermute | solution.py:189
  78.4 12.2 %collective-permute-start.16 = (bf16[416,512]{1,0:T(8,128)(2,1)}, bf16[416,512]{1,0:T(8,128)(2,1)}, u32[]{:S(2)}, u32[]{:S(2)}) collective-permute-start(bf16[416,512]{1,0:T(8,128)(2,1)} %slice.78), channel_id=1, source_target_pairs={{0,16},{16,32},{32,48},{48,0},{1,17},{17,33},{33,49},{49,1},{2,18}... | collective-permute-start | bytes 1277960 | tf_op jit(solution)/shard_map/ppermute | solution.py:189
  79.2 0.9 copy-start.1
  80.1 19.2 %collective-permute-start.9 = (bf16[416,512]{1,0:T(8,128)(2,1)}, bf16[416,512]{1,0:T(8,128)(2,1)}, u32[]{:S(2)}, u32[]{:S(2)}) collective-permute-start(bf16[416,512]{1,0:T(8,128)(2,1)} %slice.74), channel_id=1, source_target_pairs={{0,192},{64,0},{128,64},{192,128},{1,193},{65,1},{129,65},{193,129... | collective-permute-start | bytes 1277960 | tf_op jit(solution)/shard_map/ppermute | solution.py:189
  80.9 0.9 copy-start.3
  81.8 17.5 %collective-permute-start.8 = (bf16[416,512]{1,0:T(8,128)(2,1)}, bf16[416,512]{1,0:T(8,128)(2,1)}, u32[]{:S(2)}, u32[]{:S(2)}) collective-permute-start(bf16[416,512]{1,0:T(8,128)(2,1)} %slice.73), channel_id=1, source_target_pairs={{0,64},{64,128},{128,192},{192,0},{1,65},{65,129},{129,193},{193,1... | collective-permute-start | bytes 1277960 | tf_op jit(solution)/shard_map/ppermute | solution.py:189
  84.0 6.8 %copy-start.7 = (bf16[832,512]{1,0:T(8,128)(2,1)S(1)}, bf16[832,512]{1,0:T(8,128)(2,1)}, u32[]{:S(2)}) copy-start(bf16[832,512]{1,0:T(8,128)(2,1)} %copy-done.6) | copy-start | bytes 2555908
  90.9 8.5 %copy-start.2 = (bf16[832,512]{1,0:T(8,128)(2,1)S(1)}, bf16[832,512]{1,0:T(8,128)(2,1)}, u32[]{:S(2)}) copy-start(bf16[832,512]{1,0:T(8,128)(2,1)} %copy-done.1) | copy-start | bytes 2555908
  90.9 8.5 %copy-start.4 = (bf16[832,512]{1,0:T(8,128)(2,1)S(1)}, bf16[832,512]{1,0:T(8,128)(2,1)}, u32[]{:S(2)}) copy-start(bf16[832,512]{1,0:T(8,128)(2,1)} %copy-done.3) | copy-start | bytes 2555908
  90.9 8.5 %copy-start.9 = (bf16[832,512]{1,0:T(8,128)(2,1)S(1)}, bf16[832,512]{1,0:T(8,128)(2,1)}, u32[]{:S(2)}) copy-start(bf16[832,512]{1,0:T(8,128)(2,1)} %copy-done.8) | copy-start | bytes 2555908

commit v2 on v1

v2 whole, which is shorter than its diff:
```python
import functools
import jax
import jax.numpy as jnp
from jax import lax
from jax.experimental import pallas as pl
from jax.experimental.pallas import tpu as pltpu
from jax.sharding import Mesh, PartitionSpec as P

C = 1536
T = 96
R = 480
S = 512
B = 208
Q = 384
N = 1152
NT = (((1,), (1,)), ((), ()))


def gelu(z):
    return 0.5 * z * (1.0 + jnp.tanh(0.7978845608028654 * (z + 0.044715 * z * z * z)))


def combine(wide):
    n = wide.shape[1]
    total = wide[2 * T : 3 * T]
    for k in (0, 1, 3, 4):
        total = total + pltpu.roll(wide[k * T : (k + 1) * T], (2 - k) % n, 1)
    return total


def first_kernel(info, x_ref, halo_ref, gain_ref, w_ref, o_ref, sq_ref, h_ref, y_ref, hy_ref, hr_ref, base):
    i = pl.program_id(0)
    start = pl.multiple_of(info[0] * 128, 128)
    off = info[1]
    row = lax.broadcasted_iota(jnp.int32, (T, 256), 0)
    col = lax.broadcasted_iota(jnp.int32, (T, 256), 1)
    pick = jnp.where(col == row + off, 1.0, 0.0).astype(jnp.bfloat16)

    def hidden(v):
        v = v.astype(jnp.float32)
        scale = lax.rsqrt(jnp.sum(v * v, axis=-1, keepdims=True) * (1.0 / C) + 1e-06)
        return gelu(v * scale * gain_ref[...]).astype(jnp.bfloat16)

    @pl.when(i == 0)
    def _():
        hh = hidden(halo_ref[...])
        hy_ref[...] = jnp.zeros_like(hy_ref)
        hr_ref[...] = jnp.zeros_like(hr_ref)
        sq_ref[...] = jnp.zeros_like(sq_ref)
        hy = lax.dot_general(w_ref[...], hh, NT, preferred_element_type=jnp.float32)
        hx = lax.dot_general(pick, halo_ref[:, pl.ds(start, 256)], NT, preferred_element_type=jnp.float32)
        hy_ref[:, 0:32] = hy
        hy_ref[2 * T : 3 * T, 0:32] += hx

    def body(r, _):
        at = pl.ds(pl.multiple_of(r * 16, 16), 16)
        h_ref[at, :] = hidden(x_ref[0, at, :])
        return _

    lax.fori_loop(0, S // 16, body, 0, unroll=2)
    y_ref[:, 128 : 128 + S] = lax.dot_general(w_ref[...], h_ref[...], NT, preferred_element_type=jnp.float32)
    y_ref[2 * T : 3 * T, 128 : 128 + S] += lax.dot_general(
        pick, x_ref[0, :, pl.ds(start, 256)], NT, preferred_element_type=jnp.float32
    )
    b = base + i
    y_ref[:, 0:128] = pltpu.roll(hy_ref[...], lax.rem(124 - 8 * b + 128, 128), 1)
    y_ref[:, 128 + S :] = pltpu.roll(hy_ref[...], lax.rem(256 - 8 * b - 4, 128), 1)
    out = combine(y_ref[...])
    out = out.astype(jnp.bfloat16)
    o_ref[pl.ds(pl.multiple_of(i * T, 16), T), :] = out[:, 128 : 128 + S]
    out = out.astype(jnp.float32)
    squares = jnp.sum(out * out, axis=0, keepdims=True)
    sq_ref[:, pl.ds(pl.multiple_of(i * S, 128), S)] = squares[:, 128 : 128 + S]
    pad = jnp.zeros((32, 128), jnp.float32)
    left = jnp.concatenate([out[:, 0:128], pad], 0).T
    right = jnp.concatenate([out[:, 128 + S :], pad], 0).T
    keep_left = (info[2] > 0).astype(jnp.float32)
    keep_right = (info[3] > 0).astype(jnp.float32)
    lane = lax.broadcasted_iota(jnp.int32, (1, 128), 1) - 4 * i
    turn = lax.rem(4 * i + 2, 128)
    edge = jnp.where((lane == 0) | (lane == 1), pltpu.roll(squares[:, 0:128], turn, 1) * keep_left, 0.0)
    edge += jnp.where((lane == 2) | (lane == 3), pltpu.roll(squares[:, 128 + S :], turn, 1) * keep_right, 0.0)
    sq_ref[:, 2 * S :] += edge
    line = jnp.concatenate(
        [left[126:127] * keep_left, left[127:128] * keep_left, right[0:1] * keep_right, right[1:2] * keep_right], 1
    )
    hr_ref[pl.ds(i, 1), :] = line
    o_ref[2 * T :, :] = hr_ref[...].astype(jnp.bfloat16)


def first(x, halo, gain, w, info, base):
    return pl.pallas_call(
        functools.partial(first_kernel, base=base),
        grid_spec=pltpu.PrefetchScalarGridSpec(
            num_scalar_prefetch=1,
            grid=(2,),
            in_specs=[
                pl.BlockSpec((1, S, C), lambda i, info: (base + i, 0, 0)),
                pl.BlockSpec((32, C), lambda i, info: (0, 0)),
                pl.BlockSpec((1, C), lambda i, info: (0, 0)),
                pl.BlockSpec((R, C), lambda i, info: (0, 0)),
            ],
            out_specs=[pl.BlockSpec((B, S), lambda i, info: (0, 0)), pl.BlockSpec((1, N), lambda i, info: (0, 0))],
            scratch_shapes=[
                pltpu.VMEM((S, C), jnp.bfloat16),
                pltpu.VMEM((R, S + 256), jnp.float32),
                pltpu.VMEM((R, 128), jnp.float32),
                pltpu.VMEM((16, S), jnp.float32),
            ],
        ),
        out_shape=[jax.ShapeDtypeStruct((B, S), jnp.bfloat16), jax.ShapeDtypeStruct((1, N), jnp.float32)],
        compiler_params=pltpu.CompilerParams(dimension_semantics=("arbitrary",), vmem_limit_bytes=40 << 20),
        cost_estimate=pl.CostEstimate(flops=4 * S * R * C, bytes_accessed=2 * S * C * 2 + R * C * 2, transcendentals=2 * S * C),
        name="first",
    )(info, x, halo, gain, w)


def prep_kernel(pos, w_ref, *refs):
    outs, perm = refs[:8], refs[8]
    for r in range(0, R, 96):
        v = w_ref[r : r + 96, :].astype(jnp.float32)
        cols = [v[:, (a * 4 + b) * T : (a * 4 + b) * T + T] for b in range(4) for a in range(4)]
        perm[r : r + 96, :] = jnp.concatenate(cols, 1).astype(jnp.bfloat16)
    for n, (src, at) in enumerate(((perm, pos[1]), (w_ref, pos[0]))):
        for m, d in enumerate((0, 1, 3, 2)):
            lane = pl.multiple_of(lax.rem(at + d, 4) * Q, 128)
            outs[n * 4 + m][...] = src[:, pl.ds(lane, Q)]


def prep(w, pos):
    vmem = pl.BlockSpec(memory_space=pltpu.VMEM)
    return pl.pallas_call(
        prep_kernel,
        in_specs=[pl.BlockSpec(memory_space=pltpu.SMEM), vmem],
        out_specs=[vmem] * 8,
        out_shape=[jax.ShapeDtypeStruct((R, Q), jnp.bfloat16)] * 8,
        scratch_shapes=[pltpu.VMEM((R, C), jnp.bfloat16)],
        compiler_params=pltpu.CompilerParams(vmem_limit_bytes=24 << 20),
        cost_estimate=pl.CostEstimate(flops=0, bytes_accessed=6 * R * C, transcendentals=0),
        name="prep",
    )(pos, w)


def partial_sum(w_ref, h_ref, y_ref):
    y_ref[...] = jnp.dot(w_ref[...], h_ref[...], preferred_element_type=jnp.float32)
    outs = []
    for j in range(2):
        edge = pltpu.roll(y_ref[:, 2 * S :], 126 - 4 * j, 1)
        wide = jnp.concatenate([edge, y_ref[:, j * S : j * S + S], edge], 1)
        outs.append(combine(wide)[:, 128 : 128 + S])
    return outs


def far_kernel(order, a0, a1, a2, a3, a4, sq_ref, gain_ref, w_ref, h_ref, far0_ref, far1_ref, y_ref, s_ref):
    s_ref[...] = jnp.broadcast_to(lax.rsqrt(sq_ref[...] * (1.0 / C) + 1e-06), s_ref.shape)

    def put(piece, halves, lines):
        dest = pl.multiple_of(order[piece] * T, 16)
        gain = gain_ref[pl.ds(dest, T), :]
        lines = lines.astype(jnp.float32)
        tile = jnp.concatenate(
            [lines[j : j + 1, 128 * q : 128 * q + 128] for j in range(2) for q in range(4)]
            + [jnp.zeros((120, 128), jnp.float32)],
            0,
        )
        h_ref[pl.ds(dest, T), 2 * S :] = gelu(tile.T[0:T] * s_ref[0:1, 2 * S :] * gain).astype(jnp.bfloat16)
        for j in range(2):
            for q in range(4):
                lane = slice(j * S + 128 * q, j * S + 128 * q + 128)
                v = halves[j][:, 128 * q : 128 * q + 128].astype(jnp.float32)
                h_ref[pl.ds(dest, T), lane] = gelu(v * s_ref[0:1, lane] * gain).astype(jnp.bfloat16)

    for piece, ref in enumerate((a0, a1, a2)):
        put(piece, (ref[0:T, :], ref[T : 2 * T, :]), ref[2 * T :, :])
    put(3, (a3[...], a4[0:T, :]), a4[T:, :])
    far0, far1 = partial_sum(w_ref, h_ref, y_ref)
    far0_ref[...] = far0.astype(jnp.bfloat16)
    far1_ref[...] = far1.astype(jnp.bfloat16)


def far_stage(order, parts, sq, gain, w):
    vmem = pl.BlockSpec(memory_space=pltpu.VMEM)
    return pl.pallas_call(
        far_kernel,
        in_specs=[pl.BlockSpec(memory_space=pltpu.SMEM)] + [vmem] * 8,
        out_specs=[vmem] * 3,
        out_shape=[
            jax.ShapeDtypeStruct((Q, N), jnp.bfloat16),
            jax.ShapeDtypeStruct((T, S), jnp.bfloat16),
            jax.ShapeDtypeStruct((T, S), jnp.bfloat16),
        ],
        scratch_shapes=[pltpu.VMEM((R, N), jnp.float32), pltpu.VMEM((8, N), jnp.float32)],
        compiler_params=pltpu.CompilerParams(vmem_limit_bytes=24 << 20),
        cost_estimate=pl.CostEstimate(flops=2 * R * Q * N, bytes_accessed=4 * Q * N, transcendentals=Q * N),
        name="far",
    )(order, *parts, sq, gain, w)


def near_kernel(h_ref, wp_ref, wm_ref, r0_ref, r1_ref, p_ref, m_ref, y_ref):
    out = partial_sum(wp_ref, h_ref, y_ref)
    p_ref[0:T, :] = (out[0] + r0_ref[...].astype(jnp.float32)).astype(jnp.bfloat16)
    p_ref[T:, :] = out[1].astype(jnp.bfloat16)
    out = partial_sum(wm_ref, h_ref, y_ref)
    m_ref[0:T, :] = out[0].astype(jnp.bfloat16)
    m_ref[T:, :] = (out[1] + r1_ref[...].astype(jnp.float32)).astype(jnp.bfloat16)


def near_stage(h, wp, wm, r0, r1):
    vmem = pl.BlockSpec(memory_space=pltpu.VMEM)
    return pl.pallas_call(
        near_kernel,
        in_specs=[vmem] * 5,
        out_specs=[vmem] * 2,
        out_shape=[jax.ShapeDtypeStruct((2 * T, S), jnp.bfloat16)] * 2,
        scratch_shapes=[pltpu.VMEM((R, N), jnp.float32)],
        compiler_params=pltpu.CompilerParams(vmem_limit_bytes=24 << 20),
        cost_estimate=pl.CostEstimate(flops=4 * R * Q * N, bytes_accessed=4 * Q * N, transcendentals=0),
        name="near",
    )(h, wp, wm, r0, r1)


def own_kernel(h_ref, w_ref, a_ref, o_ref, y_ref):
    out = partial_sum(w_ref, h_ref, y_ref)
    for j in range(2):
        o_ref[j * T : j * T + T, :] = out[j] + a_ref[j * T : j * T + T, :].astype(jnp.float32)


def own_stage(h, w, a):
    vmem = pl.BlockSpec(memory_space=pltpu.VMEM)
    return pl.pallas_call(
        own_kernel,
        in_specs=[vmem] * 3,
        out_specs=vmem,
        out_shape=jax.ShapeDtypeStruct((2 * T, S), jnp.float32),
        scratch_shapes=[pltpu.VMEM((R, N), jnp.float32)],
        compiler_params=pltpu.CompilerParams(vmem_limit_bytes=24 << 20),
        cost_estimate=pl.CostEstimate(flops=2 * R * Q * N, bytes_accessed=4 * Q * N, transcendentals=0),
        name="own",
    )(h, w, a)


def shift(value, axis, d):
    return lax.ppermute(value, axis, [(i, (i + d) % 4) for i in range(4)])


def gather(block, f):
    below, above = shift(block, f, 1), shift(block, f, -1)
    return [block, below, above, shift(below[:T], f, 1), shift(above[T:], f, -1)]


def spread(weights, g):
    return shift(weights[2], g, -1), shift(weights[1], g, 1), shift(weights[3], g, 2)


def local(inputs, weights, gains):
    x, y = lax.axis_index("x"), lax.axis_index("y")
    sec = x * 4 + y
    seq = lax.axis_index("z") * 2 + lax.axis_index("core")
    w = weights.transpose(0, 1, 3, 2).reshape(2, R, C)
    up = [(i, i + 1) for i in range(15)]
    down = [(i + 1, i) for i in range(15)]
    before = lax.ppermute(inputs[:, S - 4 :], ("z", "core"), up)
    after = lax.ppermute(inputs[:, :4], ("z", "core"), down)
    halo = jnp.concatenate([before, after], 1).reshape(32, C)
    send = prep(w[1], jnp.stack([x, y]).astype(jnp.int32))
    w_y = (send[0],) + spread(send[:4], "y")
    w_x = (send[4],) + spread(send[4:], "x")
    block = jnp.minimum(sec * T // 128, 10)
    info = jnp.stack([block, sec * T - block * 128, seq, 15 - seq]).astype(jnp.int32)
    g0 = gains[0:1]
    g1 = gains[1].reshape(4, 4, T)
    g_x = jnp.broadcast_to(lax.dynamic_index_in_dim(g1, y, 1, False).reshape(Q, 1), (Q, 128))
    g_y = jnp.broadcast_to(lax.dynamic_index_in_dim(g1, x, 0, False).reshape(Q, 1), (Q, 128))
    half0, sq0 = first(inputs, halo, g0, w[0], info, 0)
    half1, sq1 = first(inputs, halo, g0, w[0], info, 2)
    got0 = gather(half0, "x")
    got1 = gather(half1, "y")
    sq = jnp.concatenate([sq0, sq1], 0)
    for axis in ("x", "y"):
        sq = sq + lax.ppermute(sq, axis, [(i, i ^ 1) for i in range(4)])
        sq = sq + lax.ppermute(sq, axis, [(i, i ^ 2) for i in range(4)])
    outs = []
    for got, own, at, weight, gain, line, g in (
        (got0, half0, x, w_y, g_x, sq[0:1], "y"),
        (got1, half1, y, w_x, g_y, sq[1:2], "x"),
    ):
        order = jnp.stack([at, (at + 3) % 4, (at + 1) % 4, (at + 2) % 4]).astype(jnp.int32)
        h, far0, far1 = far_stage(order, got, line, gain, weight[3])
        plus, minus = near_stage(h, weight[1], weight[2], shift(far0, g, 1), shift(far1, g, -1))
        base = own_stage(h, weight[0], own[: 2 * T])
        total = base + shift(plus, g, 1).astype(jnp.float32) + shift(minus, g, -1).astype(jnp.float32)
        outs.append(total.astype(jnp.bfloat16))
    out = jnp.concatenate([half0[: 2 * T], half1[: 2 * T]] + outs, 0)
    return out.reshape(2, 4, T, S).transpose(0, 1, 3, 2)


def solution(mesh):
    grid = Mesh(mesh.devices.reshape(4, 4, 8, 2), ("x", "y", "z", "core"))
    in_specs = (P(None, ("z", "core"), None), P(None, None, None, ("x", "y")), P())
    out_specs = P(None, None, ("z", "core"), ("x", "y"))
    return jax.shard_map(local, mesh=grid, in_specs=in_specs, out_specs=out_specs, check_vma=False)
```

time: 109 us -> 126 us (1.16)
  starting transfers between devices: 29.9 us -> 43.1 us
  local copies, waits for them, and re-layouts: 13.3 us -> 19.2 us
  waiting for transfers between devices: 28.9 us -> 26.8 us
    ppermute x16 -> x22, waiting for transfers between devices: 28.9 us -> 13.1 us  [shift(): return lax.ppermute(value, axis, [(i, (i + d) % 4) for i in range(4)])]
    ppermute x0 -> x4, waiting for transfers between devices: none -> 13.7 us  [the longest x2 11.4 us: local(): sq = sq + lax.ppermute(sq, axis, [(i, i ^ 1) for i in range(4)])]
    unnamed x28 -> x32, local copies, waits for them, and re-layouts: 4.75 us -> 13.3 us
    ppermute x0 -> x4, starting transfers between devices: none -> 7.6 us  [the longest x2 4.96 us: local(): sq = sq + lax.ppermute(sq, axis, [(i, i ^ 2) for i in range(4)])]
    ppermute x16 -> x22, starting transfers between devices: 24.3 us -> 30 us  [shift(): return lax.ppermute(value, axis, [(i, (i + d) % 4) for i in range(4)])]
    slice x12 -> x9, local copies, waits for them, and re-layouts: 7.13 us -> 4.41 us  [the longest x1 2.12 us: local(): send = prep(w[1], jnp.stack([x, y]).astype(jnp.int32))]
    pallas_call x2 -> x7, Pallas kernels: 16.6 us -> 15.2 us  [the longest x2 6.18 us: far_stage(): pl.pallas_call(far_kernel, in_specs=[pl.BlockSpec(memory_space=pltpu.SMEM...]
  transfers between devices with their start and end apart: 18 -> 28, of which waited for: 7 -> 7; matrix products, arithmetic and copies ran while one was open for 7% -> 4% of each run, Pallas kernels for 8% -> 12%
where the time goes in v2:
time: 126 us; the launch traced here: 125 us
  starting transfers between devices  43.1 us (34%)
  Pallas kernels  34.4 us (27%)
  waiting for transfers between devices  26.8 us (21%)
  local copies, waits for them, and re-layouts  19.2 us (15%)
  other arithmetic  1.49 us (1%)
    ppermute x22, starting transfers between devices, shift(): return lax.ppermute(value, axis, [(i, (i + d) % 4) for i in range(4)])  30 us
    pallas_call x2, Pallas kernels, first(): pl.pallas_call(functools.partial(first_kernel, base=base), grid_spec=pltp...  19.2 us
    unnamed x32, local copies, waits for them, and re-layouts  13.3 us
    ppermute x22, waiting for transfers between devices, shift(): return lax.ppermute(value, axis, [(i, (i + d) % 4) for i in range(4)])  13.1 us
    ppermute x2, waiting for transfers between devices, local(): sq = sq + lax.ppermute(sq, axis, [(i, i ^ 1) for i in range(4)])  11.4 us
    pallas_call x2, Pallas kernels, far_stage(): pl.pallas_call(far_kernel, in_specs=[pl.BlockSpec(memory_space=pltpu.SMEM...  6.18 us
    ppermute x2, starting transfers between devices, local(): sq = sq + lax.ppermute(sq, axis, [(i, i ^ 2) for i in range(4)])  4.96 us
    pallas_call x2, Pallas kernels, near_stage(): pl.pallas_call(near_kernel, in_specs=[vmem] * 5, out_specs=[vmem] * 2, ou...  4.49 us
  transfers between devices with their start and end apart: 28, of which 7 were waited for; matrix products, arithmetic and copies ran while one was open for 4% of the time, Pallas kernels for 12%

profile of v2, /device:TPU:96, one launch (start us, length us, event | category | flops | bytes accessed | tf_op | source)
XLA Modules:
  0.0 125.3 jit_solution(16548725802464389439)
XLA Ops:
  1.0 1.9 %collective-permute-start = (bf16[4,4,1536]{2,1,0:T(4,128)(2,1)S(1)}, bf16[4,4,1536]{2,1,0:T(4,128)(2,1)S(1)}, u32[]{:S(2)}, u32[]{:S(2)}) collective-permute-start(bf16[4,4,1536]{2,1,0:T(4,128)(2,1)S(1)} %get-tuple-element.49), channel_id=1, source_target_pairs={{0,1},{1,2},{2,3},{3,4},{4,5},{5,6},{6,7},{7,8},{8,9},{9,10},{10,1... | collective-permute-start | bytes 147464 | tf_op jit(solution)/shard_map/ppermute | solution.py:262
  2.9 3.6 %collective-permute-start.1 = (bf16[4,4,1536]{2,1,0:T(4,128)(2,1)S(1)}, bf16[4,4,1536]{2,1,0:T(4,128)(2,1)S(1)}, u32[]{:S(2)}, u32[]{:S(2)}) collective-permute-start(bf16[4,4,1536]{2,1,0:T(4,128)(2,1)S(1)} %get-tuple-element.50), channel_id=1, source_target_pairs={{1,0},{2,1},{3,2},{4,3},{5,4},{6,5},{7,6},{8,7},{9,8},{10,9},{11,1... | collective-permute-start | bytes 147464 | tf_op jit(solution)/shard_map/ppermute | solution.py:263
  6.6 2.1 %fusion.2 = (bf16[1,5,96,1536]{3,2,1,0:T(8,128)(2,1)S(1)}, bf16[1,5,96,1536]{3,2,1,0:T(8,128)(2,1)S(1)}) fusion(bf16[2,5,96,1536]{3,2,1,0:T(8,128)(2,1)} %bitcast.23), kind=kLoop, calls=%fused_computation.14 | loop fusion | bytes 5898240 | tf_op jit(solution)/shard_map/slice | solution.py:265
  8.9 2.8 %copy-done = bf16[4,512,1536]{2,1,0:T(8,128)(2,1)S(1)} copy-done((bf16[4,512,1536]{2,1,0:T(8,128)(2,1)S(1)}, bf16[4,512,1536]{2,1,0:T(8,128)(2,1)}, u32[]{:S(2)}) %copy-start) | copy-done | bytes 6291480
  11.7 9.2 %first.2 = (bf16[208,512]{1,0:T(8,128)(2,1)S(1)}, f32[1,1152]{1,0:T(1,128)S(1)}) custom-call(s32[4]{0:T(128)S(1)} %pad_add_fusion.info, bf16[4,512,1536]{2,1,0:T(8,128)(2,1)S(1)} %copy-done, bf16[32,1536]{1,0:T(8,128)(2,1)S(1)} %maximum_bitcast_fusion.halo_ref, f32[1,1536]{1,0:T(1,128)S(1)} %get-tuple-element.54.gain_ref, bf16[480,1536]{1,0:T(8,128)(2,1)S(1)} %bitcast.20), custom_call_target="tpu_custom_call" | custom-call | flops 1509949440 | bytes 4620288 | tf_op jit(solution)/shard_map/first/pallas_call | solution.py:92
  21.0 9.9 %first.3 = (bf16[208,512]{1,0:T(8,128)(2,1)}, f32[1,1152]{1,0:T(1,128)S(1)}) custom-call(s32[4]{0:T(128)S(1)} %pad_add_fusion.info, bf16[4,512,1536]{2,1,0:T(8,128)(2,1)S(1)} %copy-done, bf16[32,1536]{1,0:T(8,128)(2,1)S(1)} %maximum_bitcast_fusion.halo_ref, f32[1,1536]{1,0:T(1,128)S(1)} %get-tuple-element.54.gain_ref, bf16[480,1536]{1,0:T(8,128)(2,1)S(1)} %bitcast.21), custom_call_target="tpu_custom_call" | custom-call | flops 1509949440 | bytes 4620288 | tf_op jit(solution)/shard_map/first/pallas_call | solution.py:92
  30.9 1.6 %collective-permute-start.6 = (f32[2,1152]{1,0:T(2,128)S(1)}, f32[2,1152]{1,0:T(2,128)S(1)}, u32[]{:S(2)}, u32[]{:S(2)}) collective-permute-start(f32[2,1152]{1,0:T(2,128)S(1)} %pad_maximum_fusion.1), channel_id=1, source_target_pairs={{0,64},{64,0},{128,192},{192,128},{1,65},{65,1},{129,193},{193,129... | collective-permute-start | bytes 27656 | tf_op jit(solution)/shard_map/ppermute | solution.py:280
  32.5 2.2 %collective-permute-done.6 = f32[2,1152]{1,0:T(2,128)S(1)} collective-permute-done((f32[2,1152]{1,0:T(2,128)S(1)}, f32[2,1152]{1,0:T(2,128)S(1)}, u32[]{:S(2)}, u32[]{:S(2)}) %collective-permute-start.6) | collective-permute-done | bytes 9248 | tf_op jit(solution)/shard_map/ppermute | solution.py:280
  34.7 3.1 %collective-permute-start.7 = (f32[2,1152]{1,0:T(2,128)S(1)}, f32[2,1152]{1,0:T(2,128)S(1)}, u32[]{:S(2)}, u32[]{:S(2)}) collective-permute-start(f32[2,1152]{1,0:T(2,128)S(1)} %fusion), channel_id=1, source_target_pairs={{0,128},{64,192},{128,0},{192,64},{1,129},{65,193},{129,1},{193,65... | collective-permute-start | bytes 27656 | tf_op jit(solution)/shard_map/ppermute | solution.py:281
  37.9 2.5 %prep.1 = (bf16[480,384]{1,0:T(8,128)(2,1)S(1)}, bf16[480,384]{1,0:T(8,128)(2,1)}, bf16[480,384]{1,0:T(8,128)(2,1)}, bf16[480,384]{1,0:T(8,128)(2,1)S(1)}, bf16[...) custom-call(s32[2]{0:T(128)S(1)} %pad_add_fusion.2.pos, ...), custom_call_target="tpu_custom_call" | custom-call | bytes 4423680 | tf_op jit(solution)/shard_map/prep/pallas_call | solution.py:132
  41.2 3.2 %collective-permute-start.10 = (bf16[480,384]{1,0:T(8,128)(2,1)S(1)}, bf16[480,384]{1,0:T(8,128)(2,1)S(1)}, u32[]{:S(2)}, u32[]{:S(2)}) collective-permute-start(bf16[480,384]{1,0:T(8,128)(2,1)S(1)} %get-tuple-element.31), channel_id=1, source_target_pairs={{0,32},{16,48},{32,0},{48,16},{1,33},{17,49},{33,1},{49,17},{2,34}... | collective-permute-start | bytes 1105928 | tf_op jit(solution)/shard_map/ppermute | solution.py:243
  44.4 1.1 collective-permute-start.3
  46.4 1.1 collective-permute-start.18
  47.5 1.1 collective-permute-start.8
  48.5 9.2 %collective-permute-done.8 = f32[2,1152]{1,0:T(2,128)S(1)} collective-permute-done((f32[2,1152]{1,0:T(2,128)S(1)}, f32[2,1152]{1,0:T(2,128)S(1)}, u32[]{:S(2)}, u32[]{:S(2)}) %collective-permute-start.8) | collective-permute-done | bytes 9248 | tf_op jit(solution)/shard_map/ppermute | solution.py:280
  57.7 1.8 %collective-permute-start.9 = (f32[2,1152]{1,0:T(2,128)S(1)}, f32[2,1152]{1,0:T(2,128)S(1)}, u32[]{:S(2)}, u32[]{:S(2)}) collective-permute-start(f32[2,1152]{1,0:T(2,128)S(1)} %add.86), channel_id=1, source_target_pairs={{0,32},{16,48},{32,0},{48,16},{1,33},{17,49},{33,1},{49,17},{2,34}... | collective-permute-start | bytes 27656 | tf_op jit(solution)/shard_map/ppermute | solution.py:281
  60.5 2.4 %collective-permute-done.9 = f32[2,1152]{1,0:T(2,128)S(1)} collective-permute-done((f32[2,1152]{1,0:T(2,128)S(1)}, f32[2,1152]{1,0:T(2,128)S(1)}, u32[]{:S(2)}, u32[]{:S(2)}) %collective-permute-start.9) | collective-permute-done | bytes 9248 | tf_op jit(solution)/shard_map/ppermute | solution.py:281
  62.9 2.1 %collective-permute-start.12 = (bf16[480,384]{1,0:T(8,128)(2,1)}, bf16[480,384]{1,0:T(8,128)(2,1)S(1)}, u32[]{:S(2)}, u32[]{:S(2)}) collective-permute-start(bf16[480,384]{1,0:T(8,128)(2,1)} %get-tuple-element.35), channel_id=1, source_target_pairs={{0,16},{16,32},{32,48},{48,0},{1,17},{17,33},{33,49},{49,1},{2,18}... | collective-permute-start | bytes 1105928 | tf_op jit(solution)/shard_map/ppermute | solution.py:243
  67.8 2.2 %collective-permute-start.5 = (bf16[112,512]{1,0:T(8,128)(2,1)S(1)}, bf16[112,512]{1,0:T(8,128)(2,1)S(1)}, u32[]{:S(2)}, u32[]{:S(2)}) collective-permute-start(bf16[112,512]{1,0:T(8,128)(2,1)S(1)} %slice.63), channel_id=1, source_target_pairs={{0,192},{64,0},{128,64},{192,128},{1,193},{65,1},{129,65},{193,129... | collective-permute-start | bytes 344072 | tf_op jit(solution)/shard_map/ppermute | solution.py:243
  70.0 8.1 %collective-permute-done.5.a4 = bf16[112,512]{1,0:T(8,128)(2,1)S(1)} collective-permute-done((bf16[112,512]{1,0:T(8,128)(2,1)S(1)}, bf16[112,512]{1,0:T(8,128)(2,1)S(1)}, u32[]{:S(2)}, u32[]{:S(2)}) %collective-permute-start.5) | collective-permute-done | bytes 114720 | tf_op jit(solution)/shard_map/ppermute | solution.py:243
  78.1 2.6 %collective-permute-start.22 = (bf16[480,384]{1,0:T(8,128)(2,1)}, bf16[480,384]{1,0:T(8,128)(2,1)S(1)}, u32[]{:S(2)}, u32[]{:S(2)}) collective-permute-start(bf16[480,384]{1,0:T(8,128)(2,1)} %get-tuple-element.43), channel_id=1, source_target_pairs={{0,192},{64,0},{128,64},{192,128},{1,193},{65,1},{129,65},{193,129... | collective-permute-start | bytes 1105928 | tf_op jit(solution)/shard_map/ppermute | solution.py:243
  82.8 3.1 %far.2 = (bf16[384,1152]{1,0:T(8,128)(2,1)S(1)}, bf16[96,512]{1,0:T(8,128)(2,1)}, bf16[96,512]{1,0:T(8,128)(2,1)}) custom-call(s32[4]{0:T(128)S(1)} %pad_add_fusion.1.order, bf16[208,512]{1,0:T(8,128)(2,1)S(1)} %get-tuple-element.27.a0, bf16[208,512]{1,0:T(8,128)(2,1)S(1)} %collective-permute-done.2.a1, bf16[208,512]{1,0:T(8,128)(2,1)S(1)} %collective-permute-done.3.a2, ...), custom_call_target="tpu_custom_call" | custom-call | flops 424673280 | bytes 1769472 | tf_op jit(solution)/shard_map/far/pallas_call | solution.py:183
  87.7 2.9 %collective-permute-start.14 = (bf16[96,512]{1,0:T(8,128)(2,1)}, bf16[96,512]{1,0:T(8,128)(2,1)S(1)}, u32[]{:S(2)}, u32[]{:S(2)}) collective-permute-start(bf16[96,512]{1,0:T(8,128)(2,1)} %get-tuple-element.37), channel_id=1, source_target_pairs={{0,48},{16,0},{32,16},{48,32},{1,49},{17,1},{33,17},{49,33},{2,50}... | collective-permute-start | bytes 294920 | tf_op jit(solution)/shard_map/ppermute | solution.py:243
  94.4 1.6 %collective-permute-start.19 = (bf16[96,512]{1,0:T(8,128)(2,1)}, bf16[96,512]{1,0:T(8,128)(2,1)}, u32[]{:S(2)}, u32[]{:S(2)}) collective-permute-start(bf16[96,512]{1,0:T(8,128)(2,1)} %slice.66), channel_id=1, source_target_pairs={{0,16},{16,32},{32,48},{48,0},{1,17},{17,33},{33,49},{49,1},{2,18}... | collective-permute-start | bytes 294920 | tf_op jit(solution)/shard_map/ppermute | solution.py:243
  99.9 1.8 %near.2 = (bf16[192,512]{1,0:T(8,128)(2,1)S(1)}, bf16[192,512]{1,0:T(8,128)(2,1)S(1)}) custom-call(bf16[384,1152]{1,0:T(8,128)(2,1)S(1)} %get-tuple-element.32.h_ref, bf16[480,384]{1,0:T(8,128)(2,1)S(1)} %copy-done.6, bf16[480,384]{1,0:T(8,128)(2,1)S(1)} %copy-done.8, bf16[96,512]{1,0:T(8,128)(2,1)S(1)} %copy-done.10, bf16[96,512]{1,0:T(8,128)(2,1)S(1)} %copy-done.12), custom_call_target="tpu_custom_call" | custom-call | flops 849346560 | bytes 1769472 | tf_op jit(solution)/shard_map/near/pallas_call | solution.py:210
  101.8 3.2 %collective-permute-start.16 = (bf16[192,512]{1,0:T(8,128)(2,1)S(1)}, bf16[192,512]{1,0:T(8,128)(2,1)S(1)}, u32[]{:S(2)}, u32[]{:S(2)}) collective-permute-start(bf16[192,512]{1,0:T(8,128)(2,1)S(1)} %get-tuple-element.39), channel_id=1, source_target_pairs={{0,48},{16,0},{32,16},{48,32},{1,49},{17,1},{33,17},{49,33},{2,50}... | collective-permute-start | bytes 589832 | tf_op jit(solution)/shard_map/ppermute | solution.py:243
  105.2 3.1 %far.3 = (bf16[384,1152]{1,0:T(8,128)(2,1)S(1)}, bf16[96,512]{1,0:T(8,128)(2,1)S(1)}, bf16[96,512]{1,0:T(8,128)(2,1)S(1)}) custom-call(s32[4]{0:T(128)S(1)} %pad_add_fusion.3.order, bf16[208,512]{1,0:T(8,128)(2,1)} %get-tuple-element.28.a0, bf16[208,512]{1,0:T(8,128)(2,1)S(1)} %collective-permute-done.17.a1, ...), custom_call_target="tpu_custom_call" | custom-call | flops 424673280 | bytes 1769472 | tf_op jit(solution)/shard_map/far/pallas_call | solution.py:183
  108.2 1.5 %collective-permute-start.24 = (bf16[96,512]{1,0:T(8,128)(2,1)S(1)}, bf16[96,512]{1,0:T(8,128)(2,1)S(1)}, u32[]{:S(2)}, u32[]{:S(2)}) collective-permute-start(bf16[96,512]{1,0:T(8,128)(2,1)S(1)} %get-tuple-element.45), channel_id=1, source_target_pairs={{0,64},{64,128},{128,192},{192,0},{1,65},{65,129},{129,193},{193,1... | collective-permute-start | bytes 294920 | tf_op jit(solution)/shard_map/ppermute | solution.py:243
  109.8 1.8 %collective-permute-start.25 = (bf16[96,512]{1,0:T(8,128)(2,1)S(1)}, bf16[96,512]{1,0:T(8,128)(2,1)S(1)}, u32[]{:S(2)}, u32[]{:S(2)}) collective-permute-start(bf16[96,512]{1,0:T(8,128)(2,1)S(1)} %get-tuple-element.46), channel_id=1, source_target_pairs={{0,192},{64,0},{128,64},{192,128},{1,193},{65,1},{129,65},{193,129... | collective-permute-start | bytes 294920 | tf_op jit(solution)/shard_map/ppermute | solution.py:243
  114.6 2.7 %near.3 = (bf16[192,512]{1,0:T(8,128)(2,1)S(1)}, bf16[192,512]{1,0:T(8,128)(2,1)S(1)}) custom-call(bf16[384,1152]{1,0:T(8,128)(2,1)S(1)} %get-tuple-element.41.h_ref, bf16[480,384]{1,0:T(8,128)(2,1)S(1)} %collective-permute-done.22.wp_ref, bf16[480,384]{1,0:T(8,128)(2,1)} %collective-permute-done.23.wm_ref, ...), custom_call_target="tpu_custom_call" | custom-call | flops 849346560 | bytes 1769472 | tf_op jit(solution)/shard_map/near/pallas_call | solution.py:210
  118.4 2.3 %collective-permute-start.27 = (bf16[192,512]{1,0:T(8,128)(2,1)S(1)}, bf16[192,512]{1,0:T(8,128)(2,1)S(1)}, u32[]{:S(2)}, u32[]{:S(2)}) collective-permute-start(bf16[192,512]{1,0:T(8,128)(2,1)S(1)} %get-tuple-element.48), channel_id=1, source_target_pairs={{0,192},{64,0},{128,64},{192,128},{1,193},{65,1},{129,65},{193,129... | collective-permute-start | bytes 589832 | tf_op jit(solution)/shard_map/ppermute | solution.py:243
  120.8 3.6 %collective-permute-done.26 = bf16[192,512]{1,0:T(8,128)(2,1)S(1)} collective-permute-done((bf16[192,512]{1,0:T(8,128)(2,1)S(1)}, bf16[192,512]{1,0:T(8,128)(2,1)S(1)}, u32[]{:S(2)}, u32[]{:S(2)}) %collective-permute-start.26) | collective-permute-done | bytes 196640 | tf_op jit(solution)/shard_map/ppermute | solution.py:243
  (95 shorter events, 23.4 us)
Async XLA Ops:
  1.0 7.9 %collective-permute-start = (bf16[4,4,1536]{2,1,0:T(4,128)(2,1)S(1)}, bf16[4,4,1536]{2,1,0:T(4,128)(2,1)S(1)}, u32[]{:S(2)}, u32[]{:S(2)}) collective-permute-start(bf16[4,4,1536]{2,1,0:T(4,128)(2,1)S(1)} %get-tuple-element.49), channel_id=1, source_target_pairs={{0,1},{1,2},{2,3},{3,4},{4,5},{5,6},{6,7},{7,8},{8,9},{9,10},{10,1... | collective-permute-start | bytes 147464 | tf_op jit(solution)/shard_map/ppermute | solution.py:262
  2.9 6.0 %collective-permute-start.1 = (bf16[4,4,1536]{2,1,0:T(4,128)(2,1)S(1)}, bf16[4,4,1536]{2,1,0:T(4,128)(2,1)S(1)}, u32[]{:S(2)}, u32[]{:S(2)}) collective-permute-start(bf16[4,4,1536]{2,1,0:T(4,128)(2,1)S(1)} %get-tuple-element.50), channel_id=1, source_target_pairs={{1,0},{2,1},{3,2},{4,3},{5,4},{6,5},{7,6},{8,7},{9,8},{10,9},{11,1... | collective-permute-start | bytes 147464 | tf_op jit(solution)/shard_map/ppermute | solution.py:263
  6.6 2.1 %copy-start.15 = (f32[2,1536]{1,0:T(2,128)S(1)}, f32[2,1536]{1,0:T(2,128)}, u32[]{:S(2)}) copy-start(f32[2,1536]{1,0:T(2,128)} %param.5) | copy-start | bytes 36868
  8.9 2.8 %copy-start = (bf16[4,512,1536]{2,1,0:T(8,128)(2,1)S(1)}, bf16[4,512,1536]{2,1,0:T(8,128)(2,1)}, u32[]{:S(2)}) copy-start(bf16[4,512,1536]{2,1,0:T(8,128)(2,1)} %x_ref.3) | copy-start | bytes 18874372
  30.9 3.7 %collective-permute-start.6 = (f32[2,1152]{1,0:T(2,128)S(1)}, f32[2,1152]{1,0:T(2,128)S(1)}, u32[]{:S(2)}, u32[]{:S(2)}) collective-permute-start(f32[2,1152]{1,0:T(2,128)S(1)} %pad_maximum_fusion.1), channel_id=1, source_target_pairs={{0,64},{64,0},{128,192},{192,128},{1,65},{65,1},{129,193},{193,129... | collective-permute-start | bytes 27656 | tf_op jit(solution)/shard_map/ppermute | solution.py:280
  34.7 12.8 %collective-permute-start.7 = (f32[2,1152]{1,0:T(2,128)S(1)}, f32[2,1152]{1,0:T(2,128)S(1)}, u32[]{:S(2)}, u32[]{:S(2)}) collective-permute-start(f32[2,1152]{1,0:T(2,128)S(1)} %fusion), channel_id=1, source_target_pairs={{0,128},{64,192},{128,0},{192,64},{1,129},{65,193},{129,1},{193,65... | collective-permute-start | bytes 27656 | tf_op jit(solution)/shard_map/ppermute | solution.py:281
  41.2 44.7 %copy-start.2 = (bf16[480,384]{1,0:T(8,128)(2,1)S(1)}, bf16[480,384]{1,0:T(8,128)(2,1)}, u32[]{:S(2)}) copy-start(bf16[480,384]{1,0:T(8,128)(2,1)} %copy-done.1) | copy-start | bytes 1105924
  41.2 25.9 %collective-permute-start.10 = (bf16[480,384]{1,0:T(8,128)(2,1)S(1)}, bf16[480,384]{1,0:T(8,128)(2,1)S(1)}, u32[]{:S(2)}, u32[]{:S(2)}) collective-permute-start(bf16[480,384]{1,0:T(8,128)(2,1)S(1)} %get-tuple-element.31), channel_id=1, source_target_pairs={{0,32},{16,48},{32,0},{48,16},{1,33},{17,49},{33,1},{49,17},{2,34}... | collective-permute-start | bytes 1105928 | tf_op jit(solution)/shard_map/ppermute | solution.py:243
  44.4 18.5 %collective-permute-start.3 = (bf16[208,512]{1,0:T(8,128)(2,1)S(1)}, bf16[208,512]{1,0:T(8,128)(2,1)S(1)}, u32[]{:S(2)}, u32[]{:S(2)}) collective-permute-start(bf16[208,512]{1,0:T(8,128)(2,1)S(1)} %get-tuple-element.27.a0), channel_id=1, source_target_pairs={{0,192},{64,0},{128,64},{192,128},{1,193},{65,1},{129,65},{193,129... | collective-permute-start | bytes 638984 | tf_op jit(solution)/shard_map/ppermute | solution.py:243
  45.5 14.1 %collective-permute-start.2 = (bf16[208,512]{1,0:T(8,128)(2,1)S(1)}, bf16[208,512]{1,0:T(8,128)(2,1)S(1)}, u32[]{:S(2)}, u32[]{:S(2)}) collective-permute-start(bf16[208,512]{1,0:T(8,128)(2,1)S(1)} %get-tuple-element.27.a0), channel_id=1, source_target_pairs={{0,64},{64,128},{128,192},{192,0},{1,65},{65,129},{129,193},{193,1... | collective-permute-start | bytes 638984 | tf_op jit(solution)/shard_map/ppermute | solution.py:243
  46.4 18.6 %collective-permute-start.18 = (bf16[208,512]{1,0:T(8,128)(2,1)}, bf16[208,512]{1,0:T(8,128)(2,1)S(1)}, u32[]{:S(2)}, u32[]{:S(2)}) collective-permute-start(bf16[208,512]{1,0:T(8,128)(2,1)} %get-tuple-element.28.a0), channel_id=1, source_target_pairs={{0,48},{16,0},{32,16},{48,32},{1,49},{17,1},{33,17},{49,33},{2,50}... | collective-permute-start | bytes 638984 | tf_op jit(solution)/shard_map/ppermute | solution.py:243
  47.5 10.2 %collective-permute-start.8 = (f32[2,1152]{1,0:T(2,128)S(1)}, f32[2,1152]{1,0:T(2,128)S(1)}, u32[]{:S(2)}, u32[]{:S(2)}) collective-permute-start(f32[2,1152]{1,0:T(2,128)S(1)} %fusion.4), channel_id=1, source_target_pairs={{0,16},{16,0},{32,48},{48,32},{1,17},{17,1},{33,49},{49,33},{2,18}... | collective-permute-start | bytes 27656 | tf_op jit(solution)/shard_map/ppermute | solution.py:280
  57.7 5.2 %collective-permute-start.9 = (f32[2,1152]{1,0:T(2,128)S(1)}, f32[2,1152]{1,0:T(2,128)S(1)}, u32[]{:S(2)}, u32[]{:S(2)}) collective-permute-start(f32[2,1152]{1,0:T(2,128)S(1)} %add.86), channel_id=1, source_target_pairs={{0,32},{16,48},{32,0},{48,16},{1,33},{17,49},{33,1},{49,17},{2,34}... | collective-permute-start | bytes 27656 | tf_op jit(solution)/shard_map/ppermute | solution.py:281
  59.6 6.8 %collective-permute-start.4 = (bf16[96,512]{1,0:T(8,128)(2,1)S(1)}, bf16[96,512]{1,0:T(8,128)(2,1)S(1)}, u32[]{:S(2)}, u32[]{:S(2)}) collective-permute-start(bf16[96,512]{1,0:T(8,128)(2,1)S(1)} %slice.62), channel_id=1, source_target_pairs={{0,64},{64,128},{128,192},{192,0},{1,65},{65,129},{129,193},{193,1... | collective-permute-start | bytes 294920 | tf_op jit(solution)/shard_map/ppermute | solution.py:243
  62.9 23.1 %collective-permute-start.11 = (bf16[480,384]{1,0:T(8,128)(2,1)}, bf16[480,384]{1,0:T(8,128)(2,1)S(1)}, u32[]{:S(2)}, u32[]{:S(2)}) collective-permute-start(bf16[480,384]{1,0:T(8,128)(2,1)} %get-tuple-element.34), channel_id=1, source_target_pairs={{0,48},{16,0},{32,16},{48,32},{1,49},{17,1},{33,17},{49,33},{2,50}... | collective-permute-start | bytes 1105928 | tf_op jit(solution)/shard_map/ppermute | solution.py:243
  62.9 24.1 %collective-permute-start.12 = (bf16[480,384]{1,0:T(8,128)(2,1)}, bf16[480,384]{1,0:T(8,128)(2,1)S(1)}, u32[]{:S(2)}, u32[]{:S(2)}) collective-permute-start(bf16[480,384]{1,0:T(8,128)(2,1)} %get-tuple-element.35), channel_id=1, source_target_pairs={{0,16},{16,32},{32,48},{48,0},{1,17},{17,33},{33,49},{49,1},{2,18}... | collective-permute-start | bytes 1105928 | tf_op jit(solution)/shard_map/ppermute | solution.py:243
  65.0 36.8 %collective-permute-start.21 = (bf16[480,384]{1,0:T(8,128)(2,1)}, bf16[480,384]{1,0:T(8,128)(2,1)}, u32[]{:S(2)}, u32[]{:S(2)}) collective-permute-start(bf16[480,384]{1,0:T(8,128)(2,1)} %get-tuple-element.40), channel_id=1, source_target_pairs={{0,128},{64,192},{128,0},{192,64},{1,129},{65,193},{129,1},{193,65... | collective-permute-start | bytes 1105928 | tf_op jit(solution)/shard_map/ppermute | solution.py:243
  67.0 18.8 %collective-permute-start.17 = (bf16[208,512]{1,0:T(8,128)(2,1)}, bf16[208,512]{1,0:T(8,128)(2,1)S(1)}, u32[]{:S(2)}, u32[]{:S(2)}) collective-permute-start(bf16[208,512]{1,0:T(8,128)(2,1)} %get-tuple-element.28.a0), channel_id=1, source_target_pairs={{0,16},{16,32},{32,48},{48,0},{1,17},{17,33},{33,49},{49,1},{2,18}... | collective-permute-start | bytes 638984 | tf_op jit(solution)/shard_map/ppermute | solution.py:243
  67.8 10.3 %collective-permute-start.5 = (bf16[112,512]{1,0:T(8,128)(2,1)S(1)}, bf16[112,512]{1,0:T(8,128)(2,1)S(1)}, u32[]{:S(2)}, u32[]{:S(2)}) collective-permute-start(bf16[112,512]{1,0:T(8,128)(2,1)S(1)} %slice.63), channel_id=1, source_target_pairs={{0,192},{64,0},{128,64},{192,128},{1,193},{65,1},{129,65},{193,129... | collective-permute-start | bytes 344072 | tf_op jit(solution)/shard_map/ppermute | solution.py:243
  78.1 31.6 %collective-permute-start.22 = (bf16[480,384]{1,0:T(8,128)(2,1)}, bf16[480,384]{1,0:T(8,128)(2,1)S(1)}, u32[]{:S(2)}, u32[]{:S(2)}) collective-permute-start(bf16[480,384]{1,0:T(8,128)(2,1)} %get-tuple-element.43), channel_id=1, source_target_pairs={{0,192},{64,0},{128,64},{192,128},{1,193},{65,1},{129,65},{193,129... | collective-permute-start | bytes 1105928 | tf_op jit(solution)/shard_map/ppermute | solution.py:243
  80.9 1.0 copy-start.4
  85.9 28.7 %collective-permute-start.23 = (bf16[480,384]{1,0:T(8,128)(2,1)S(1)}, bf16[480,384]{1,0:T(8,128)(2,1)}, u32[]{:S(2)}, u32[]{:S(2)}) collective-permute-start(bf16[480,384]{1,0:T(8,128)(2,1)S(1)} %copy-done.2), channel_id=1, source_target_pairs={{0,64},{64,128},{128,192},{192,0},{1,65},{65,129},{129,193},{193,1... | collective-permute-start | bytes 1105928 | tf_op jit(solution)/shard_map/ppermute | solution.py:243
  86.7 6.0 %collective-permute-start.13 = (bf16[96,512]{1,0:T(8,128)(2,1)}, bf16[96,512]{1,0:T(8,128)(2,1)S(1)}, u32[]{:S(2)}, u32[]{:S(2)}) collective-permute-start(bf16[96,512]{1,0:T(8,128)(2,1)} %get-tuple-element.36), channel_id=1, source_target_pairs={{0,16},{16,32},{32,48},{48,0},{1,17},{17,33},{33,49},{49,1},{2,18}... | collective-permute-start | bytes 294920 | tf_op jit(solution)/shard_map/ppermute | solution.py:243
  87.7 6.1 %collective-permute-start.14 = (bf16[96,512]{1,0:T(8,128)(2,1)}, bf16[96,512]{1,0:T(8,128)(2,1)S(1)}, u32[]{:S(2)}, u32[]{:S(2)}) collective-permute-start(bf16[96,512]{1,0:T(8,128)(2,1)} %get-tuple-element.37), channel_id=1, source_target_pairs={{0,48},{16,0},{32,16},{48,32},{1,49},{17,1},{33,17},{49,33},{2,50}... | collective-permute-start | bytes 294920 | tf_op jit(solution)/shard_map/ppermute | solution.py:243
  93.4 11.7 %collective-permute-start.20 = (bf16[112,512]{1,0:T(8,128)(2,1)}, bf16[112,512]{1,0:T(8,128)(2,1)}, u32[]{:S(2)}, u32[]{:S(2)}) collective-permute-start(bf16[112,512]{1,0:T(8,128)(2,1)} %slice.67), channel_id=1, source_target_pairs={{0,48},{16,0},{32,16},{48,32},{1,49},{17,1},{33,17},{49,33},{2,50}... | collective-permute-start | bytes 344072 | tf_op jit(solution)/shard_map/ppermute | solution.py:243
  94.4 7.3 %collective-permute-start.19 = (bf16[96,512]{1,0:T(8,128)(2,1)}, bf16[96,512]{1,0:T(8,128)(2,1)}, u32[]{:S(2)}, u32[]{:S(2)}) collective-permute-start(bf16[96,512]{1,0:T(8,128)(2,1)} %slice.66), channel_id=1, source_target_pairs={{0,16},{16,32},{32,48},{48,0},{1,17},{17,33},{33,49},{49,1},{2,18}... | collective-permute-start | bytes 294920 | tf_op jit(solution)/shard_map/ppermute | solution.py:243
  101.7 19.0 %collective-permute-start.15 = (bf16[192,512]{1,0:T(8,128)(2,1)S(1)}, bf16[192,512]{1,0:T(8,128)(2,1)S(1)}, u32[]{:S(2)}, u32[]{:S(2)}) collective-permute-start(bf16[192,512]{1,0:T(8,128)(2,1)S(1)} %get-tuple-element.38), channel_id=1, source_target_pairs={{0,16},{16,32},{32,48},{48,0},{1,17},{17,33},{33,49},{49,1},{2,18}... | collective-permute-start | bytes 589832 | tf_op jit(solution)/shard_map/ppermute | solution.py:243
  101.8 18.9 %collective-permute-start.16 = (bf16[192,512]{1,0:T(8,128)(2,1)S(1)}, bf16[192,512]{1,0:T(8,128)(2,1)S(1)}, u32[]{:S(2)}, u32[]{:S(2)}) collective-permute-start(bf16[192,512]{1,0:T(8,128)(2,1)S(1)} %get-tuple-element.39), channel_id=1, source_target_pairs={{0,48},{16,0},{32,16},{48,32},{1,49},{17,1},{33,17},{49,33},{2,50}... | collective-permute-start | bytes 589832 | tf_op jit(solution)/shard_map/ppermute | solution.py:243
  108.2 6.4 %collective-permute-start.24 = (bf16[96,512]{1,0:T(8,128)(2,1)S(1)}, bf16[96,512]{1,0:T(8,128)(2,1)S(1)}, u32[]{:S(2)}, u32[]{:S(2)}) collective-permute-start(bf16[96,512]{1,0:T(8,128)(2,1)S(1)} %get-tuple-element.45), channel_id=1, source_target_pairs={{0,64},{64,128},{128,192},{192,0},{1,65},{65,129},{129,193},{193,1... | collective-permute-start | bytes 294920 | tf_op jit(solution)/shard_map/ppermute | solution.py:243
  109.8 4.8 %collective-permute-start.25 = (bf16[96,512]{1,0:T(8,128)(2,1)S(1)}, bf16[96,512]{1,0:T(8,128)(2,1)S(1)}, u32[]{:S(2)}, u32[]{:S(2)}) collective-permute-start(bf16[96,512]{1,0:T(8,128)(2,1)S(1)} %get-tuple-element.46), channel_id=1, source_target_pairs={{0,192},{64,0},{128,64},{192,128},{1,193},{65,1},{129,65},{193,129... | collective-permute-start | bytes 294920 | tf_op jit(solution)/shard_map/ppermute | solution.py:243
  117.4 7.0 %collective-permute-start.26 = (bf16[192,512]{1,0:T(8,128)(2,1)S(1)}, bf16[192,512]{1,0:T(8,128)(2,1)S(1)}, u32[]{:S(2)}, u32[]{:S(2)}) collective-permute-start(bf16[192,512]{1,0:T(8,128)(2,1)S(1)} %get-tuple-element.47), channel_id=1, source_target_pairs={{0,64},{64,128},{128,192},{192,0},{1,65},{65,129},{129,193},{193,1... | collective-permute-start | bytes 589832 | tf_op jit(solution)/shard_map/ppermute | solution.py:243
  118.4 6.0 %collective-permute-start.27 = (bf16[192,512]{1,0:T(8,128)(2,1)S(1)}, bf16[192,512]{1,0:T(8,128)(2,1)S(1)}, u32[]{:S(2)}, u32[]{:S(2)}) collective-permute-start(bf16[192,512]{1,0:T(8,128)(2,1)S(1)} %get-tuple-element.48), channel_id=1, source_target_pairs={{0,192},{64,0},{128,64},{192,128},{1,193},{65,1},{129,65},{193,129... | collective-permute-start | bytes 589832 | tf_op jit(solution)/shard_map/ppermute | solution.py:243
  (12 other events, 9.6 us)

commit v3 on v2

v3 whole, which is shorter than its diff:
```python
import functools
import jax
import jax.numpy as jnp
from jax import lax
from jax.experimental import pallas as pl
from jax.experimental.pallas import tpu as pltpu
from jax.sharding import Mesh, PartitionSpec as P

C = 1536
T = 96
R = 480
S = 512
M = 4
B = 400
HB = 192
Q = 384
HR = 240
N = M * S + 128
NT = (((1,), (1,)), ((), ()))


def whole(*shape):
    return pl.BlockSpec(shape, lambda i, *_: (0,) * len(shape))


def gelu(z):
    half = 0.5 * z
    return half + half * jnp.tanh(z * (0.7978845608028654 + 0.035677408136300125 * (z * z)))


def combine(wide):
    n = wide.shape[1]
    total = wide[2 * T : 3 * T]
    for k in (0, 1, 3, 4):
        total = total + pltpu.roll(wide[k * T : (k + 1) * T], (2 - k) % n, 1)
    return total


def first_kernel(info, x_ref, halo_ref, gain_ref, w_ref, o_ref, sq_ref, h_ref, y_ref, hy_ref, hr_ref):
    i = pl.program_id(0)
    start = pl.multiple_of(info[0] * 128, 128)
    off = info[1]
    row = lax.broadcasted_iota(jnp.int32, (T, 256), 0)
    col = lax.broadcasted_iota(jnp.int32, (T, 256), 1)
    pick = jnp.where(col == row + off, 1.0, 0.0).astype(jnp.bfloat16)

    def hidden(v):
        v = v.astype(jnp.float32)
        scale = lax.rsqrt(jnp.sum(v * v, axis=-1, keepdims=True) * (1.0 / C) + 1e-06)
        return gelu(v * scale * gain_ref[...]).astype(jnp.bfloat16)

    @pl.when(i == 0)
    def _():
        hh = hidden(halo_ref[...])
        hy_ref[...] = jnp.zeros_like(hy_ref)
        hr_ref[...] = jnp.zeros_like(hr_ref)
        sq_ref[...] = jnp.zeros_like(sq_ref)
        hy = lax.dot_general(w_ref[...], hh, NT, preferred_element_type=jnp.float32)
        hx = lax.dot_general(pick, halo_ref[:, pl.ds(start, 256)], NT, preferred_element_type=jnp.float32)
        hy_ref[:, 0:32] = hy
        hy_ref[2 * T : 3 * T, 0:32] += hx

    window = pl.ds(start, 256)
    for c in range(2):
        for r in range(c * 256, c * 256 + 256, 16):
            h_ref[r : r + 16, :] = hidden(x_ref[0, r : r + 16, :])
        at = slice(c * 256, c * 256 + 256)
        to = slice(128 + c * 256, 384 + c * 256)
        y_ref[:, to] = lax.dot_general(w_ref[...], h_ref[at, :], NT, preferred_element_type=jnp.float32)
        y_ref[2 * T : 3 * T, to] += lax.dot_general(
            pick, x_ref[0, at, window], NT, preferred_element_type=jnp.float32
        )
    y_ref[:, 0:128] = pltpu.roll(hy_ref[...], lax.rem(252 - 8 * i, 128), 1)
    y_ref[:, 128 + S :] = pltpu.roll(hy_ref[...], lax.rem(252 - 8 * i, 128), 1)
    out = combine(y_ref[...])
    out = out.astype(jnp.bfloat16)
    o_ref[pl.ds(pl.multiple_of(i * T, 16), T), :] = out[:, 128 : 128 + S]
    out = out.astype(jnp.float32)
    squares = jnp.sum(out * out, axis=0, keepdims=True)
    sq_ref[:, pl.ds(pl.multiple_of(i * S, 128), S)] = squares[:, 128 : 128 + S]
    pad = jnp.zeros((32, 128), jnp.float32)
    left = jnp.concatenate([out[:, 0:128], pad], 0).T
    right = jnp.concatenate([out[:, 128 + S :], pad], 0).T
    keep_left = (info[2] > 0).astype(jnp.float32)
    keep_right = (info[3] > 0).astype(jnp.float32)
    lane = lax.broadcasted_iota(jnp.int32, (1, 128), 1) - 4 * i
    turn = lax.rem(4 * i + 2, 128)
    edge = jnp.where((lane == 0) | (lane == 1), pltpu.roll(squares[:, 0:128], turn, 1) * keep_left, 0.0)
    edge += jnp.where((lane == 2) | (lane == 3), pltpu.roll(squares[:, 128 + S :], turn, 1) * keep_right, 0.0)
    sq_ref[:, M * S :] += edge
    line = jnp.concatenate(
        [left[126:127] * keep_left, left[127:128] * keep_left, right[0:1] * keep_right, right[1:2] * keep_right], 1
    )
    hr_ref[pl.ds(i, 1), :] = line
    o_ref[M * T :, :] = hr_ref[...].astype(jnp.bfloat16)


def first(x, halo, gain, w, info):
    return pl.pallas_call(
        first_kernel,
        grid_spec=pltpu.PrefetchScalarGridSpec(
            num_scalar_prefetch=1,
            grid=(M,),
            in_specs=[
                pl.BlockSpec((1, S, C), lambda i, info: (i, 0, 0)),
                whole(32, C),
                whole(1, C),
                pl.BlockSpec((None, R, C), lambda i, info: (0, 0, 0)),
            ],
            out_specs=[whole(B, S), whole(1, N)],
            scratch_shapes=[
                pltpu.VMEM((S, C), jnp.bfloat16),
                pltpu.VMEM((R, S + 256), jnp.float32),
                pltpu.VMEM((R, 128), jnp.float32),
                pltpu.VMEM((16, S), jnp.float32),
            ],
        ),
        out_shape=[jax.ShapeDtypeStruct((B, S), jnp.bfloat16), jax.ShapeDtypeStruct((1, N), jnp.float32)],
        compiler_params=pltpu.CompilerParams(dimension_semantics=("arbitrary",), vmem_limit_bytes=32 << 20),
        cost_estimate=pl.CostEstimate(flops=2 * M * S * R * C, bytes_accessed=2 * M * S * C, transcendentals=M * S * C),
        name="first",
    )(info, x, halo, gain, w)


def prep_kernel(core, w_ref, o_ref):
    for r in range(0, HR, 80):
        v = w_ref[r : r + 80, :].astype(jnp.float32)
        for b in range(4):
            cols = [v[:, (a * 4 + b) * T : (a * 4 + b) * T + T] for a in range(4)]
            o_ref[b, r : r + 80, :] = jnp.concatenate(cols, 1).astype(jnp.bfloat16)


def prep(core, w):
    return pl.pallas_call(
        prep_kernel,
        grid_spec=pltpu.PrefetchScalarGridSpec(
            num_scalar_prefetch=1,
            grid=(1,),
            in_specs=[pl.BlockSpec((None, HR, C), lambda i, core: (1, core[0], 0))],
            out_specs=whole(4, HR, Q),
        ),
        out_shape=jax.ShapeDtypeStruct((4, HR, Q), jnp.bfloat16),
        compiler_params=pltpu.CompilerParams(vmem_limit_bytes=16 << 20),
        cost_estimate=pl.CostEstimate(flops=0, bytes_accessed=4 * HR * C, transcendentals=0),
        name="prep",
    )(core, w)


def partial_sum(core, mine_ref, other_ref, h_ref, y_ref):
    at = pl.multiple_of(core * HR, 16)
    y_ref[pl.ds(at, HR), :] = jnp.dot(mine_ref[...], h_ref[...], preferred_element_type=jnp.float32)
    at = pl.multiple_of(HR - core * HR, 16)
    y_ref[pl.ds(at, HR), :] = jnp.dot(other_ref[...], h_ref[...], preferred_element_type=jnp.float32)
    outs = []
    for j in range(M):
        edge = pltpu.roll(y_ref[:, M * S :], 126 - 4 * j, 1)
        wide = jnp.concatenate([edge, y_ref[:, j * S : j * S + S], edge], 1)
        outs.append(combine(wide)[:, 128 : 128 + S])
    return outs


def far_kernel(order, a0, a1, a2, a3, a4, sq_ref, gain_ref, wa_ref, wb_ref, h_ref, far0_ref, far1_ref, y_ref, s_ref):
    s_ref[...] = jnp.broadcast_to(lax.rsqrt(sq_ref[...] * (1.0 / C) + 1e-06), s_ref.shape)

    def put(piece, parts, lines):
        dest = pl.multiple_of(order[piece] * T, 16)
        gain = gain_ref[pl.ds(dest, T), :]
        lines = lines.astype(jnp.float32)
        tile = jnp.concatenate(
            [lines[j : j + 1, 128 * q : 128 * q + 128] for j in range(M) for q in range(4)]
            + [jnp.zeros((112, 128), jnp.float32)],
            0,
        )
        h_ref[pl.ds(dest, T), M * S :] = gelu(tile.T[0:T] * s_ref[0:1, M * S :] * gain).astype(jnp.bfloat16)
        for j in range(M):
            ref, row = parts[j]
            for q in range(4):
                lane = slice(j * S + 128 * q, j * S + 128 * q + 128)
                v = ref[row : row + T, 128 * q : 128 * q + 128].astype(jnp.float32)
                h_ref[pl.ds(dest, T), lane] = gelu(v * s_ref[0:1, lane] * gain).astype(jnp.bfloat16)

    for piece, ref in enumerate((a0, a1, a2)):
        put(piece, [(ref, j * T) for j in range(M)], ref[M * T :, :])
    put(3, [(a3, 0), (a3, T), (a4, 0), (a4, T)], a4[HB:, :])
    out = partial_sum(order[8], wa_ref, wb_ref, h_ref, y_ref)
    for j in range(2):
        far0_ref[j * T : j * T + T, :] = out[j].astype(jnp.bfloat16)
        far1_ref[j * T : j * T + T, :] = out[j + 2].astype(jnp.bfloat16)


def picked(k):
    return [pl.BlockSpec((None, HR, Q), lambda i, order: (order[k], 0, 0))] * 2


def stage(kernel, order, args, in_specs, outs, scratch, flops, name):
    return pl.pallas_call(
        kernel,
        grid_spec=pltpu.PrefetchScalarGridSpec(
            num_scalar_prefetch=1,
            grid=(1,),
            in_specs=in_specs,
            out_specs=[whole(*o.shape) for o in outs],
            scratch_shapes=[pltpu.VMEM((R, N), jnp.float32)] + scratch,
        ),
        out_shape=outs,
        compiler_params=pltpu.CompilerParams(vmem_limit_bytes=32 << 20),
        cost_estimate=pl.CostEstimate(flops=flops, bytes_accessed=4 * Q * N, transcendentals=0),
        name=name,
    )(order, *args)


def near_kernel(order, h_ref, pa_ref, pb_ref, ma_ref, mb_ref, r0_ref, r1_ref, p_ref, m_ref, y_ref):
    out = partial_sum(order[8], pa_ref, pb_ref, h_ref, y_ref)
    for j in range(M):
        at = slice(j * T, j * T + T)
        value = out[j] + r0_ref[at, :].astype(jnp.float32) if j < 2 else out[j]
        p_ref[at, :] = value.astype(jnp.bfloat16)
    out = partial_sum(order[8], ma_ref, mb_ref, h_ref, y_ref)
    for j in range(M):
        at = slice(j * T, j * T + T)
        value = out[j] + r1_ref[j * T - HB : j * T - HB + T, :].astype(jnp.float32) if j >= 2 else out[j]
        m_ref[at, :] = value.astype(jnp.bfloat16)


def own_kernel(order, h_ref, wa_ref, wb_ref, a_ref, o_ref, y_ref):
    out = partial_sum(order[8], wa_ref, wb_ref, h_ref, y_ref)
    for j in range(M):
        at = slice(j * T, j * T + T)
        o_ref[at, :] = out[j] + a_ref[at, :].astype(jnp.float32)


def shift(value, axis, d):
    return lax.ppermute(value, axis, [(i, (i + d) % 4) for i in range(4)])


def local(inputs, weights, gains):
    x, y, core = lax.axis_index("x"), lax.axis_index("y"), lax.axis_index("core")
    sec = x * 4 + y
    seq = lax.axis_index("z") * 2 + core
    w = weights.transpose(0, 1, 3, 2).reshape(2, R, C)
    up = [(i, i + 1) for i in range(15)]
    down = [(i + 1, i) for i in range(15)]
    before = lax.ppermute(inputs[:, S - 4 :], ("z", "core"), up)
    after = lax.ppermute(inputs[:, :4], ("z", "core"), down)
    halo = jnp.concatenate([before, after], 1).reshape(32, C)
    send = prep(core.reshape(1).astype(jnp.int32), w)
    block = jnp.minimum(sec * T // 128, 10)
    info = jnp.stack([block, sec * T - block * 128, seq, 15 - seq]).astype(jnp.int32)
    info, send = lax.optimization_barrier((info, send))
    mine = lax.all_to_all(send, "y", 0, 0, tiled=True)
    gain = lax.dynamic_index_in_dim(gains[1].reshape(4, 4, T), y, 1, False).reshape(Q, 1)
    gain = jnp.broadcast_to(gain, (Q, 128))
    block, sq = first(inputs, halo, gains[0:1], w, info)
    block, sq, mine = lax.optimization_barrier((block, sq, mine))
    other = lax.ppermute(mine, "core", [(0, 1), (1, 0)])
    below, above = shift(block, "x", 1), shift(block, "x", -1)
    got = [block, below, above, shift(below[:HB], "x", 1), shift(above[HB:], "x", -1)]
    for axis in ("x", "y"):
        sq = sq + lax.ppermute(sq, axis, [(i, i ^ 1) for i in range(4)])
        sq = sq + lax.ppermute(sq, axis, [(i, i ^ 2) for i in range(4)])
    rel = [x, x + 3, x + 1, x + 2, y, y + 3, y + 1, y + 2]
    order = jnp.concatenate([jnp.stack(rel) % 4, core.reshape(1)]).astype(jnp.int32)
    half = jax.ShapeDtypeStruct((HB, S), jnp.bfloat16)
    full = jax.ShapeDtypeStruct((M * T, S), jnp.bfloat16)
    h, far0, far1 = stage(
        far_kernel,
        order,
        (*got, sq, gain, mine, other),
        [whole(B, S)] * 3 + [whole(HB, S), whole(B - HB, S), whole(1, N), whole(Q, 128)] + picked(7),
        [jax.ShapeDtypeStruct((Q, N), jnp.bfloat16), half, half],
        [pltpu.VMEM((8, N), jnp.float32)],
        4 * R * Q * N,
        "far",
    )
    r0, r1 = shift(far0, "y", 1), shift(far1, "y", -1)
    plus, minus = stage(
        near_kernel,
        order,
        (h, mine, other, mine, other, r0, r1),
        [whole(Q, N)] + picked(6) + picked(5) + [whole(HB, S)] * 2,
        [full, full],
        [],
        4 * R * Q * N,
        "near",
    )
    plus, minus, h = lax.optimization_barrier((plus, minus, h))
    (base,) = stage(
        own_kernel,
        order,
        (h, mine, other, block),
        [whole(Q, N)] + picked(4) + [whole(B, S)],
        [jax.ShapeDtypeStruct((M * T, S), jnp.float32)],
        [],
        2 * R * Q * N,
        "own",
    )
    total = base + shift(plus, "y", 1).astype(jnp.float32) + shift(minus, "y", -1).astype(jnp.float32)
    out = jnp.concatenate([block[: M * T], total.astype(jnp.bfloat16)], 0)
    return out.reshape(2, M, T, S).transpose(0, 1, 3, 2)


def solution(mesh):
    grid = Mesh(mesh.devices.reshape(4, 4, 8, 2), ("x", "y", "z", "core"))
    in_specs = (P(None, ("z", "core"), None), P(None, None, None, ("x", "y")), P())
    out_specs = P(None, None, ("z", "core"), ("x", "y"))
    return jax.shard_map(local, mesh=grid, in_specs=in_specs, out_specs=out_specs, check_vma=False)
```

time: 126 us -> 86.5 us (0.69)
  local copies, waits for them, and re-layouts: 19.2 us -> 7.88 us
  starting transfers between devices: 43.1 us -> 32.3 us
  Pallas kernels: 34.4 us -> 23.6 us
  waiting for transfers between devices: 26.8 us -> 19.9 us
    ppermute x22 -> x8, starting transfers between devices: 30 us -> 12.7 us  [shift(): return lax.ppermute(value, axis, [(i, (i + d) % 4) for i in range(4)])]
    pallas_call x9 -> x5, Pallas kernels: 34.4 us -> 23.6 us  [the longest x3 12.8 us: stage(): pl.pallas_call(kernel, grid_spec=pltpu.PrefetchScalarGridSpec(num_scalar_...]
    unnamed x32 -> x8, local copies, waits for them, and re-layouts: 13.3 us -> 6.44 us
    ppermute x22 -> x8, waiting for transfers between devices: 13.1 us -> 6.88 us  [shift(): return lax.ppermute(value, axis, [(i, (i + d) % 4) for i in range(4)])]
    all_to_all x0 -> x1, starting transfers between devices: none -> 4.46 us  [local(): mine = lax.all_to_all(send, 'y', 0, 0, tiled=True)]
    slice x9 -> x4, local copies, waits for them, and re-layouts: 4.41 us -> 0.08 us  [the longest x1 0.03 us: local(): out = jnp.concatenate([block[:M * T], total.astype(jnp.bfloat16)], 0)]
    ppermute x2, waiting for transfers between devices: 11.4 us -> 8.37 us  [local(): sq = sq + lax.ppermute(sq, axis, [(i, i ^ 1) for i in range(4)])]
    ppermute x2, waiting for transfers between devices: 2.35 us -> 4.66 us  [local(): sq = sq + lax.ppermute(sq, axis, [(i, i ^ 2) for i in range(4)])]
  transfers between devices with their start and end apart: 28 -> 16, of which waited for: 7 -> 7; matrix products, arithmetic and copies ran while one was open for 4% -> 2% of each run, Pallas kernels for 12% -> 16%
where the time goes in v3:
time: 86.5 us; the launch traced here: 86 us
  starting transfers between devices  32.3 us (37%)
  Pallas kernels  23.6 us (27%)
  waiting for transfers between devices  19.9 us (23%)
  local copies, waits for them, and re-layouts  7.88 us (9%)
  other arithmetic  2.07 us (2%)
    pallas_call x3, Pallas kernels, stage(): pl.pallas_call(kernel, grid_spec=pltpu.PrefetchScalarGridSpec(num_scalar_...  12.8 us
    ppermute x8, starting transfers between devices, shift(): return lax.ppermute(value, axis, [(i, (i + d) % 4) for i in range(4)])  12.7 us
    pallas_call x1, Pallas kernels, first(): pl.pallas_call(first_kernel, grid_spec=pltpu.PrefetchScalarGridSpec(num_s...  9.55 us
    ppermute x2, waiting for transfers between devices, local(): sq = sq + lax.ppermute(sq, axis, [(i, i ^ 1) for i in range(4)])  8.37 us
    ppermute x8, waiting for transfers between devices, shift(): return lax.ppermute(value, axis, [(i, (i + d) % 4) for i in range(4)])  6.88 us
    unnamed x8, local copies, waits for them, and re-layouts  6.44 us
    ppermute x2, starting transfers between devices, local(): sq = sq + lax.ppermute(sq, axis, [(i, i ^ 2) for i in range(4)])  5.77 us
    ppermute x2, waiting for transfers between devices, local(): sq = sq + lax.ppermute(sq, axis, [(i, i ^ 2) for i in range(4)])  4.66 us
  transfers between devices with their start and end apart: 16, of which 7 were waited for; matrix products, arithmetic and copies ran while one was open for 2% of the time, Pallas kernels for 16%

profile of v3, /device:TPU:96, one launch (start us, length us, event | category | flops | bytes accessed | tf_op | source)
XLA Modules:
  0.0 86.0 jit_solution(14541341055648324213)
XLA Ops:
  0.0 1.0 %fusion.1 = (bf16[4,4,1536]{2,1,0:T(4,128)(2,1)S(1)}, bf16[4,4,1536]{2,1,0:T(4,128)(2,1)S(1)}) fusion(bf16[4,512,1536]{2,1,0:T(8,128)(2,1)} %x_ref.1), kind=kLoop, calls=%fused_computation.11 | loop fusion | bytes 196608 | tf_op jit(solution)/shard_map/slice | solution.py:243
  1.0 1.9 %collective-permute-start = (bf16[4,4,1536]{2,1,0:T(4,128)(2,1)S(1)}, bf16[4,4,1536]{2,1,0:T(4,128)(2,1)S(1)}, u32[]{:S(2)}, u32[]{:S(2)}) collective-permute-start(bf16[4,4,1536]{2,1,0:T(4,128)(2,1)S(1)} %get-tuple-element.35), channel_id=1, source_target_pairs={{0,1},{1,2},{2,3},{3,4},{4,5},{5,6},{6,7},{7,8},{8,9},{9,10},{10,1... | collective-permute-start | bytes 147464 | tf_op jit(solution)/shard_map/ppermute | solution.py:243
  2.9 3.6 %collective-permute-start.1 = (bf16[4,4,1536]{2,1,0:T(4,128)(2,1)S(1)}, bf16[4,4,1536]{2,1,0:T(4,128)(2,1)S(1)}, u32[]{:S(2)}, u32[]{:S(2)}) collective-permute-start(bf16[4,4,1536]{2,1,0:T(4,128)(2,1)S(1)} %get-tuple-element.36), channel_id=1, source_target_pairs={{1,0},{2,1},{3,2},{4,3},{5,4},{6,5},{7,6},{8,7},{9,8},{10,9},{11,1... | collective-permute-start | bytes 147464 | tf_op jit(solution)/shard_map/ppermute | solution.py:244
  6.6 1.8 %copy-done = bf16[2,5,1536,96]{2,3,1,0:T(8,128)(2,1)S(1)} copy-done((bf16[2,5,1536,96]{2,3,1,0:T(8,128)(2,1)S(1)}, bf16[2,5,1536,96]{2,3,1,0:T(8,128)(2,1)}, u32[]{:S(2)}) %copy-start) | copy-done | bytes 2949144
  8.4 1.2 %prep.1 = bf16[4,240,384]{2,1,0:T(8,128)(2,1)} custom-call(s32[1]{0:T(128)} %bitcast.4.core, bf16[2,480,1536]{2,1,0:T(8,128)(2,1)S(1)} %bitcast.21), custom_call_target="tpu_custom_call" | custom-call | bytes 1474560 | tf_op jit(solution)/shard_map/prep/pallas_call | solution.py:134
  9.7 4.5 %all-to-all-start = ((bf16[4,240,384]{2,1,0:T(8,128)(2,1)}), bf16[4,240,384]{2,1,0:T(8,128)(2,1)S(1)}, u32[]{:S(2)}, u32[]{:S(2)}) async-start(bf16[4,240,384]{2,1,0:T(8,128)(2,1)} %prep.1), calls=%async_computation | async-start | bytes 1474560 | tf_op jit(solution)/shard_map/all_to_all | solution.py:250
  14.3 1.8 %copy-done.1 = bf16[2,5,1536,96]{2,3,1,0:T(8,128)(2,1)S(1)} copy-done((bf16[2,5,1536,96]{2,3,1,0:T(8,128)(2,1)S(1)}, bf16[2,5,1536,96]{2,3,1,0:T(8,128)(2,1)}, u32[]{:S(2)}) %copy-start.1) | copy-done | bytes 2949144
  16.2 2.8 %copy-done.2 = bf16[4,512,1536]{2,1,0:T(8,128)(2,1)S(1)} copy-done((bf16[4,512,1536]{2,1,0:T(8,128)(2,1)S(1)}, bf16[4,512,1536]{2,1,0:T(8,128)(2,1)}, u32[]{:S(2)}) %copy-start.2) | copy-done | bytes 6291480
  18.9 9.6 %first.1 = (bf16[400,512]{1,0:T(8,128)(2,1)S(1)}, f32[1,2176]{1,0:T(1,128)S(1)}) custom-call(s32[4]{0:T(128)S(1)} %pad_add_fusion.info, bf16[4,512,1536]{2,1,0:T(8,128)(2,1)S(1)} %copy-done.2, bf16[32,1536]{1,0:T(8,128)(2,1)S(1)} %maximum_bitcast_fusion.halo_ref, f32[1,1536]{1,0:T(1,128)S(1)} %get-tuple-element.38.gain_ref, bf16[2,480,1536]{2,1,0:T(8,128)(2,1)S(1)} %bitcast.22), custom_call_target="tpu_custom_call" | custom-call | flops 3019898880 | bytes 6291456 | tf_op jit(solution)/shard_map/first/pallas_call | solution.py:99
  28.5 2.8 %collective-permute-start.3 = (bf16[400,512]{1,0:T(8,128)(2,1)S(1)}, bf16[400,512]{1,0:T(8,128)(2,1)S(1)}, u32[]{:S(2)}, u32[]{:S(2)}) collective-permute-start(bf16[400,512]{1,0:T(8,128)(2,1)S(1)} %get-tuple-element.24.a0.a_ref), channel_id=1, source_target_pairs={{0,192},{64,0},{128,64},{192,128},{1,193},{65,1},{129,65},{193,129... | collective-permute-start | bytes 1228808 | tf_op jit(solution)/shard_map/ppermute | solution.py:233
  31.4 0.9 %collective-permute-start.10 = (bf16[4,240,384]{2,1,0:T(8,128)(2,1)S(1)}, bf16[4,240,384]{2,1,0:T(8,128)(2,1)S(1)}, u32[]{:S(2)}, u32[]{:S(2)}) collective-permute-start(bf16[4,240,384]{2,1,0:T(8,128)(2,1)S(1)} %all-to-all-done.wa_ref.pa_ref.ma_ref), channel_id=1, source_target_pairs={{0,1},{1,0},{2,3},{3,2},{4,5},{5,4},{6,7},{7,6},{8,9},{9,8},{10,11... | collective-permute-start | bytes 2211848 | tf_op jit(solution)/shard_map/ppermute | solution.py:255
  32.3 0.5 collective-permute-start.6
  32.8 8.4 %collective-permute-done.6 = f32[1,2176]{1,0:T(1,128)S(1)} collective-permute-done((f32[1,2176]{1,0:T(1,128)S(1)}, f32[1,2176]{1,0:T(1,128)S(1)}, u32[]{:S(2)}, u32[]{:S(2)}) %collective-permute-start.6) | collective-permute-done | bytes 8736 | tf_op jit(solution)/shard_map/ppermute | solution.py:259
  41.2 2.9 %collective-permute-start.7 = (f32[1,2176]{1,0:T(1,128)S(1)}, f32[1,2176]{1,0:T(1,128)S(1)}, u32[]{:S(2)}, u32[]{:S(2)}) collective-permute-start(f32[1,2176]{1,0:T(1,128)S(1)} %add.62), channel_id=1, source_target_pairs={{0,128},{64,192},{128,0},{192,64},{1,129},{65,193},{129,1},{193,65... | collective-permute-start | bytes 26120 | tf_op jit(solution)/shard_map/ppermute | solution.py:260
  44.1 2.3 %collective-permute-done.7 = f32[1,2176]{1,0:T(1,128)S(1)} collective-permute-done((f32[1,2176]{1,0:T(1,128)S(1)}, f32[1,2176]{1,0:T(1,128)S(1)}, u32[]{:S(2)}, u32[]{:S(2)}) %collective-permute-start.7) | collective-permute-done | bytes 8736 | tf_op jit(solution)/shard_map/ppermute | solution.py:260
  46.4 2.4 %collective-permute-start.8 = (f32[1,2176]{1,0:T(1,128)S(1)}, f32[1,2176]{1,0:T(1,128)S(1)}, u32[]{:S(2)}, u32[]{:S(2)}) collective-permute-start(f32[1,2176]{1,0:T(1,128)S(1)} %add.63), channel_id=1, source_target_pairs={{0,16},{16,0},{32,48},{48,32},{1,17},{17,1},{33,49},{49,33},{2,18}... | collective-permute-start | bytes 26120 | tf_op jit(solution)/shard_map/ppermute | solution.py:259
  48.8 3.1 %collective-permute-start.5 = (bf16[208,512]{1,0:T(8,128)(2,1)S(1)}, bf16[208,512]{1,0:T(8,128)(2,1)S(1)}, u32[]{:S(2)}, u32[]{:S(2)}) collective-permute-start(bf16[208,512]{1,0:T(8,128)(2,1)S(1)} %slice.29), channel_id=1, source_target_pairs={{0,192},{64,0},{128,64},{192,128},{1,193},{65,1},{129,65},{193,129... | collective-permute-start | bytes 638984 | tf_op jit(solution)/shard_map/ppermute | solution.py:233
  52.1 2.9 %collective-permute-start.9 = (f32[1,2176]{1,0:T(1,128)S(1)}, f32[1,2176]{1,0:T(1,128)}, u32[]{:S(2)}, u32[]{:S(2)}) collective-permute-start(f32[1,2176]{1,0:T(1,128)S(1)} %add.64), channel_id=1, source_target_pairs={{0,32},{16,48},{32,0},{48,16},{1,33},{17,49},{33,1},{49,17},{2,34}... | collective-permute-start | bytes 26120 | tf_op jit(solution)/shard_map/ppermute | solution.py:260
  55.3 2.4 %collective-permute-done.9 = f32[1,2176]{1,0:T(1,128)} collective-permute-done((f32[1,2176]{1,0:T(1,128)S(1)}, f32[1,2176]{1,0:T(1,128)}, u32[]{:S(2)}, u32[]{:S(2)}) %collective-permute-start.9) | collective-permute-done | bytes 8736 | tf_op jit(solution)/shard_map/ppermute | solution.py:260
  57.6 0.7 add.65.sq_ref
  58.3 0.6 collective-permute-done.4.a3
  59.0 4.7 %far.1 = (bf16[384,2176]{1,0:T(8,128)(2,1)S(1)}, bf16[192,512]{1,0:T(8,128)(2,1)S(1)}, bf16[192,512]{1,0:T(8,128)(2,1)S(1)}) custom-call(s32[9]{0:T(128)S(1)} %pad_add_fusion.1.order, bf16[400,512]{1,0:T(8,128)(2,1)S(1)} %get-tuple-element.24.a0.a_ref, bf16[400,512]{1,0:T(8,128)(2,1)S(1)} %collective-permute-done.2.a1, ...), custom_call_target="tpu_custom_call" | custom-call | flops 1604321280 | bytes 3342336 | tf_op jit(solution)/shard_map/far/pallas_call | solution.py:196
  63.8 0.4 collective-permute-start.11
  64.1 3.0 %collective-permute-start.12 = (bf16[192,512]{1,0:T(8,128)(2,1)S(1)}, bf16[192,512]{1,0:T(8,128)(2,1)S(1)}, u32[]{:S(2)}, u32[]{:S(2)}) collective-permute-start(bf16[192,512]{1,0:T(8,128)(2,1)S(1)} %get-tuple-element.29), channel_id=1, source_target_pairs={{0,48},{16,0},{32,16},{48,32},{1,49},{17,1},{33,17},{49,33},{2,50}... | collective-permute-start | bytes 589832 | tf_op jit(solution)/shard_map/ppermute | solution.py:233
  67.1 3.6 %collective-permute-done.11.r0_ref = bf16[192,512]{1,0:T(8,128)(2,1)S(1)} collective-permute-done((bf16[192,512]{1,0:T(8,128)(2,1)S(1)}, bf16[192,512]{1,0:T(8,128)(2,1)S(1)}, u32[]{:S(2)}, u32[]{:S(2)}) %collective-permute-start.11) | collective-permute-done | bytes 196640 | tf_op jit(solution)/shard_map/ppermute | solution.py:233
  70.7 5.0 %near.1 = (bf16[384,512]{1,0:T(8,128)(2,1)S(1)}, bf16[384,512]{1,0:T(8,128)(2,1)S(1)}) custom-call(s32[9]{0:T(128)S(1)} %pad_add_fusion.1.order, bf16[384,2176]{1,0:T(8,128)(2,1)S(1)} %get-tuple-element.32.h_ref, bf16[4,240,384]{2,1,0:T(8,128)(2,1)S(1)} %all-to-all-done.wa_ref.pa_ref.ma_ref, ...), custom_call_target="tpu_custom_call" | custom-call | flops 1604321280 | bytes 3342336 | tf_op jit(solution)/shard_map/near/pallas_call | solution.py:196
  75.7 1.4 %collective-permute-start.13 = (bf16[384,512]{1,0:T(8,128)(2,1)S(1)}, bf16[384,512]{1,0:T(8,128)(2,1)S(1)}, u32[]{:S(2)}, u32[]{:S(2)}) collective-permute-start(bf16[384,512]{1,0:T(8,128)(2,1)S(1)} %get-tuple-element.33), channel_id=1, source_target_pairs={{0,16},{16,32},{32,48},{48,0},{1,17},{17,33},{33,49},{49,1},{2,18}... | collective-permute-start | bytes 1179656 | tf_op jit(solution)/shard_map/ppermute | solution.py:233
  77.1 1.9 %collective-permute-start.14 = (bf16[384,512]{1,0:T(8,128)(2,1)S(1)}, bf16[384,512]{1,0:T(8,128)(2,1)S(1)}, u32[]{:S(2)}, u32[]{:S(2)}) collective-permute-start(bf16[384,512]{1,0:T(8,128)(2,1)S(1)} %get-tuple-element.34), channel_id=1, source_target_pairs={{0,48},{16,0},{32,16},{48,32},{1,49},{17,1},{33,17},{49,33},{2,50}... | collective-permute-start | bytes 1179656 | tf_op jit(solution)/shard_map/ppermute | solution.py:233
  79.0 3.1 %own.1 = f32[384,512]{1,0:T(8,128)S(1)} custom-call(s32[9]{0:T(128)S(1)} %pad_add_fusion.1.order, bf16[384,2176]{1,0:T(8,128)(2,1)S(1)} %get-tuple-element.32.h_ref, bf16[4,240,384]{2,1,0:T(8,128)(2,1)S(1)} %all-to-all-done.wa_ref.pa_ref.ma_ref, bf16[4,240,384]{2,1,0:T(8,128)(2,1)S(1)} %collective-permute-done.10.wb_ref.pb_ref.mb_ref, ...), custom_call_target="tpu_custom_call" | custom-call | flops 802160640 | bytes 3342336 | tf_op jit(solution)/shard_map/own/pallas_call | solution.py:196
  82.2 2.6 %collective-permute-done.13 = bf16[384,512]{1,0:T(8,128)(2,1)S(1)} collective-permute-done((bf16[384,512]{1,0:T(8,128)(2,1)S(1)}, bf16[384,512]{1,0:T(8,128)(2,1)S(1)}, u32[]{:S(2)}, u32[]{:S(2)}) %collective-permute-start.13) | collective-permute-done | bytes 393248 | tf_op jit(solution)/shard_map/ppermute | solution.py:233
  84.8 0.2 add_convert_fusion
  85.0 0.9 %pad_maximum_fusion = bf16[768,512]{1,0:T(8,128)(2,1)} fusion(bf16[384,512]{1,0:T(8,128)(2,1)S(1)} %add_convert_fusion, bf16[384,512]{1,0:T(8,128)(2,1)S(1)} %slice.24), kind=kLoop, calls=%fused_computation | loop fusion | flops 1572864 | bytes 1572864 | tf_op jit(solution)/shard_map/concatenate | solution.py:298
  (33 shorter events, 0.9 us)
Async XLA Ops:
  1.0 13.3 %collective-permute-start = (bf16[4,4,1536]{2,1,0:T(4,128)(2,1)S(1)}, bf16[4,4,1536]{2,1,0:T(4,128)(2,1)S(1)}, u32[]{:S(2)}, u32[]{:S(2)}) collective-permute-start(bf16[4,4,1536]{2,1,0:T(4,128)(2,1)S(1)} %get-tuple-element.35), channel_id=1, source_target_pairs={{0,1},{1,2},{2,3},{3,4},{4,5},{5,6},{6,7},{7,8},{8,9},{9,10},{10,1... | collective-permute-start | bytes 147464 | tf_op jit(solution)/shard_map/ppermute | solution.py:243
  2.9 11.3 %collective-permute-start.1 = (bf16[4,4,1536]{2,1,0:T(4,128)(2,1)S(1)}, bf16[4,4,1536]{2,1,0:T(4,128)(2,1)S(1)}, u32[]{:S(2)}, u32[]{:S(2)}) collective-permute-start(bf16[4,4,1536]{2,1,0:T(4,128)(2,1)S(1)} %get-tuple-element.36), channel_id=1, source_target_pairs={{1,0},{2,1},{3,2},{4,3},{5,4},{6,5},{7,6},{8,7},{9,8},{10,9},{11,1... | collective-permute-start | bytes 147464 | tf_op jit(solution)/shard_map/ppermute | solution.py:244
  6.6 1.8 %copy-start = (bf16[2,5,1536,96]{2,3,1,0:T(8,128)(2,1)S(1)}, bf16[2,5,1536,96]{2,3,1,0:T(8,128)(2,1)}, u32[]{:S(2)}) copy-start(bf16[2,5,1536,96]{2,3,1,0:T(8,128)(2,1)} %param.4) | copy-start | bytes 8847364
  8.4 5.8 %copy-start.3 = (f32[2,1536]{1,0:T(2,128)S(1)}, f32[2,1536]{1,0:T(2,128)}, u32[]{:S(2)}) copy-start(f32[2,1536]{1,0:T(2,128)} %param.5) | copy-start | bytes 36868
  9.7 18.8 %all-to-all-start = ((bf16[4,240,384]{2,1,0:T(8,128)(2,1)}), bf16[4,240,384]{2,1,0:T(8,128)(2,1)S(1)}, u32[]{:S(2)}, u32[]{:S(2)}) async-start(bf16[4,240,384]{2,1,0:T(8,128)(2,1)} %prep.1), calls=%async_computation | async-start | bytes 1474560 | tf_op jit(solution)/shard_map/all_to_all | solution.py:250
  14.3 1.8 %copy-start.1 = (bf16[2,5,1536,96]{2,3,1,0:T(8,128)(2,1)S(1)}, bf16[2,5,1536,96]{2,3,1,0:T(8,128)(2,1)}, u32[]{:S(2)}) copy-start(bf16[2,5,1536,96]{2,3,1,0:T(8,128)(2,1)} %param.4) | copy-start | bytes 8847364
  16.2 2.8 %copy-start.2 = (bf16[4,512,1536]{2,1,0:T(8,128)(2,1)S(1)}, bf16[4,512,1536]{2,1,0:T(8,128)(2,1)}, u32[]{:S(2)}) copy-start(bf16[4,512,1536]{2,1,0:T(8,128)(2,1)} %x_ref.1) | copy-start | bytes 18874372
  28.5 20.3 %collective-permute-start.3 = (bf16[400,512]{1,0:T(8,128)(2,1)S(1)}, bf16[400,512]{1,0:T(8,128)(2,1)S(1)}, u32[]{:S(2)}, u32[]{:S(2)}) collective-permute-start(bf16[400,512]{1,0:T(8,128)(2,1)S(1)} %get-tuple-element.24.a0.a_ref), channel_id=1, source_target_pairs={{0,192},{64,0},{128,64},{192,128},{1,193},{65,1},{129,65},{193,129... | collective-permute-start | bytes 1228808 | tf_op jit(solution)/shard_map/ppermute | solution.py:233
  31.4 20.6 %collective-permute-start.2 = (bf16[400,512]{1,0:T(8,128)(2,1)S(1)}, bf16[400,512]{1,0:T(8,128)(2,1)S(1)}, u32[]{:S(2)}, u32[]{:S(2)}) collective-permute-start(bf16[400,512]{1,0:T(8,128)(2,1)S(1)} %get-tuple-element.24.a0.a_ref), channel_id=1, source_target_pairs={{0,64},{64,128},{128,192},{192,0},{1,65},{65,129},{129,193},{193,1... | collective-permute-start | bytes 1228808 | tf_op jit(solution)/shard_map/ppermute | solution.py:233
  31.4 27.5 %collective-permute-start.10 = (bf16[4,240,384]{2,1,0:T(8,128)(2,1)S(1)}, bf16[4,240,384]{2,1,0:T(8,128)(2,1)S(1)}, u32[]{:S(2)}, u32[]{:S(2)}) collective-permute-start(bf16[4,240,384]{2,1,0:T(8,128)(2,1)S(1)} %all-to-all-done.wa_ref.pa_ref.ma_ref), channel_id=1, source_target_pairs={{0,1},{1,0},{2,3},{3,2},{4,5},{5,4},{6,7},{7,6},{8,9},{9,8},{10,11... | collective-permute-start | bytes 2211848 | tf_op jit(solution)/shard_map/ppermute | solution.py:255
  32.3 8.8 %collective-permute-start.6 = (f32[1,2176]{1,0:T(1,128)S(1)}, f32[1,2176]{1,0:T(1,128)S(1)}, u32[]{:S(2)}, u32[]{:S(2)}) collective-permute-start(f32[1,2176]{1,0:T(1,128)S(1)} %get-tuple-element.25), channel_id=1, source_target_pairs={{0,64},{64,0},{128,192},{192,128},{1,65},{65,1},{129,193},{193,129... | collective-permute-start | bytes 26120 | tf_op jit(solution)/shard_map/ppermute | solution.py:259
  41.2 5.2 %collective-permute-start.7 = (f32[1,2176]{1,0:T(1,128)S(1)}, f32[1,2176]{1,0:T(1,128)S(1)}, u32[]{:S(2)}, u32[]{:S(2)}) collective-permute-start(f32[1,2176]{1,0:T(1,128)S(1)} %add.62), channel_id=1, source_target_pairs={{0,128},{64,192},{128,0},{192,64},{1,129},{65,193},{129,1},{193,65... | collective-permute-start | bytes 26120 | tf_op jit(solution)/shard_map/ppermute | solution.py:260
  46.4 5.6 %collective-permute-start.8 = (f32[1,2176]{1,0:T(1,128)S(1)}, f32[1,2176]{1,0:T(1,128)S(1)}, u32[]{:S(2)}, u32[]{:S(2)}) collective-permute-start(f32[1,2176]{1,0:T(1,128)S(1)} %add.63), channel_id=1, source_target_pairs={{0,16},{16,0},{32,48},{48,32},{1,17},{17,1},{33,49},{49,33},{2,18}... | collective-permute-start | bytes 26120 | tf_op jit(solution)/shard_map/ppermute | solution.py:259
  48.8 10.1 %collective-permute-start.5 = (bf16[208,512]{1,0:T(8,128)(2,1)S(1)}, bf16[208,512]{1,0:T(8,128)(2,1)S(1)}, u32[]{:S(2)}, u32[]{:S(2)}) collective-permute-start(bf16[208,512]{1,0:T(8,128)(2,1)S(1)} %slice.29), channel_id=1, source_target_pairs={{0,192},{64,0},{128,64},{192,128},{1,193},{65,1},{129,65},{193,129... | collective-permute-start | bytes 638984 | tf_op jit(solution)/shard_map/ppermute | solution.py:233
  51.9 7.0 %collective-permute-start.4 = (bf16[192,512]{1,0:T(8,128)(2,1)S(1)}, bf16[192,512]{1,0:T(8,128)(2,1)S(1)}, u32[]{:S(2)}, u32[]{:S(2)}) collective-permute-start(bf16[192,512]{1,0:T(8,128)(2,1)S(1)} %slice.28), channel_id=1, source_target_pairs={{0,64},{64,128},{128,192},{192,0},{1,65},{65,129},{129,193},{193,1... | collective-permute-start | bytes 589832 | tf_op jit(solution)/shard_map/ppermute | solution.py:233
  52.1 5.5 %collective-permute-start.9 = (f32[1,2176]{1,0:T(1,128)S(1)}, f32[1,2176]{1,0:T(1,128)}, u32[]{:S(2)}, u32[]{:S(2)}) collective-permute-start(f32[1,2176]{1,0:T(1,128)S(1)} %add.64), channel_id=1, source_target_pairs={{0,32},{16,48},{32,0},{48,16},{1,33},{17,49},{33,1},{49,17},{2,34}... | collective-permute-start | bytes 26120 | tf_op jit(solution)/shard_map/ppermute | solution.py:260
  63.8 7.0 %collective-permute-start.11 = (bf16[192,512]{1,0:T(8,128)(2,1)S(1)}, bf16[192,512]{1,0:T(8,128)(2,1)S(1)}, u32[]{:S(2)}, u32[]{:S(2)}) collective-permute-start(bf16[192,512]{1,0:T(8,128)(2,1)S(1)} %get-tuple-element.28), channel_id=1, source_target_pairs={{0,16},{16,32},{32,48},{48,0},{1,17},{17,33},{33,49},{49,1},{2,18}... | collective-permute-start | bytes 589832 | tf_op jit(solution)/shard_map/ppermute | solution.py:233
  64.1 6.6 %collective-permute-start.12 = (bf16[192,512]{1,0:T(8,128)(2,1)S(1)}, bf16[192,512]{1,0:T(8,128)(2,1)S(1)}, u32[]{:S(2)}, u32[]{:S(2)}) collective-permute-start(bf16[192,512]{1,0:T(8,128)(2,1)S(1)} %get-tuple-element.29), channel_id=1, source_target_pairs={{0,48},{16,0},{32,16},{48,32},{1,49},{17,1},{33,17},{49,33},{2,50}... | collective-permute-start | bytes 589832 | tf_op jit(solution)/shard_map/ppermute | solution.py:233
  75.7 9.1 %collective-permute-start.13 = (bf16[384,512]{1,0:T(8,128)(2,1)S(1)}, bf16[384,512]{1,0:T(8,128)(2,1)S(1)}, u32[]{:S(2)}, u32[]{:S(2)}) collective-permute-start(bf16[384,512]{1,0:T(8,128)(2,1)S(1)} %get-tuple-element.33), channel_id=1, source_target_pairs={{0,16},{16,32},{32,48},{48,0},{1,17},{17,33},{33,49},{49,1},{2,18}... | collective-permute-start | bytes 1179656 | tf_op jit(solution)/shard_map/ppermute | solution.py:233
  77.1 7.8 %collective-permute-start.14 = (bf16[384,512]{1,0:T(8,128)(2,1)S(1)}, bf16[384,512]{1,0:T(8,128)(2,1)S(1)}, u32[]{:S(2)}, u32[]{:S(2)}) collective-permute-start(bf16[384,512]{1,0:T(8,128)(2,1)S(1)} %get-tuple-element.34), channel_id=1, source_target_pairs={{0,48},{16,0},{32,16},{48,32},{1,49},{17,1},{33,17},{49,33},{2,50}... | collective-permute-start | bytes 1179656 | tf_op jit(solution)/shard_map/ppermute | solution.py:233

commit v4 on v3

--- a/solution.py
+++ b/solution.py
@@ -146,20 +146,21 @@
     )(core, w)
 
 
-def partial_sum(core, mine_ref, other_ref, h_ref, y_ref):
-    at = pl.multiple_of(core * HR, 16)
-    y_ref[pl.ds(at, HR), :] = jnp.dot(mine_ref[...], h_ref[...], preferred_element_type=jnp.float32)
-    at = pl.multiple_of(HR - core * HR, 16)
-    y_ref[pl.ds(at, HR), :] = jnp.dot(other_ref[...], h_ref[...], preferred_element_type=jnp.float32)
-    outs = []
-    for j in range(M):
-        edge = pltpu.roll(y_ref[:, M * S :], 126 - 4 * j, 1)
-        wide = jnp.concatenate([edge, y_ref[:, j * S : j * S + S], edge], 1)
-        outs.append(combine(wide)[:, 128 : 128 + S])
-    return outs
-
-
-def far_kernel(order, a0, a1, a2, a3, a4, sq_ref, gain_ref, wa_ref, wb_ref, h_ref, far0_ref, far1_ref, y_ref, s_ref):
+def join(core, pairs, v_ref):
+    for k, (mine_ref, other_ref) in enumerate(pairs):
+        v_ref[pl.ds(pl.multiple_of(k * R + core * HR, 16), HR), :] = mine_ref[...]
+        v_ref[pl.ds(pl.multiple_of(k * R + HR - core * HR, 16), HR), :] = other_ref[...]
+
+
+def taps(y_ref, k, j):
+    rows = slice(k * R, k * R + R)
+    edge = pltpu.roll(y_ref[rows, M * S :], 126 - 4 * j, 1)
+    wide = jnp.concatenate([edge, y_ref[rows, j * S : j * S + S], edge], 1)
+    return combine(wide)[:, 128 : 128 + S]
+
+
+def far_kernel(order, a0, a1, a2, a3, a4, sq_ref, gain_ref, wa_ref, wb_ref, h_ref, far0_ref, far1_ref, y_ref, v_ref, s_ref):
+    join(order[8], [(wa_ref, wb_ref)], v_ref)
     s_ref[...] = jnp.broadcast_to(lax.rsqrt(sq_ref[...] * (1.0 / C) + 1e-06), s_ref.shape)
 
     def put(piece, parts, lines):
@@ -182,17 +183,17 @@
     for piece, ref in enumerate((a0, a1, a2)):
         put(piece, [(ref, j * T) for j in range(M)], ref[M * T :, :])
     put(3, [(a3, 0), (a3, T), (a4, 0), (a4, T)], a4[HB:, :])
-    out = partial_sum(order[8], wa_ref, wb_ref, h_ref, y_ref)
+    y_ref[...] = jnp.dot(v_ref[...], h_ref[...], preferred_element_type=jnp.float32)
     for j in range(2):
-        far0_ref[j * T : j * T + T, :] = out[j].astype(jnp.bfloat16)
-        far1_ref[j * T : j * T + T, :] = out[j + 2].astype(jnp.bfloat16)
+        far0_ref[j * T : j * T + T, :] = taps(y_ref, 0, j).astype(jnp.bfloat16)
+        far1_ref[j * T : j * T + T, :] = taps(y_ref, 0, j + 2).astype(jnp.bfloat16)
 
 
 def picked(k):
     return [pl.BlockSpec((None, HR, Q), lambda i, order: (order[k], 0, 0))] * 2
 
 
-def stage(kernel, order, args, in_specs, outs, scratch, flops, name):
+def stage(kernel, order, args, in_specs, outs, scratch, count, name):
     return pl.pallas_call(
         kernel,
         grid_spec=pltpu.PrefetchScalarGridSpec(
@@ -200,33 +201,29 @@
             grid=(1,),
             in_specs=in_specs,
             out_specs=[whole(*o.shape) for o in outs],
-            scratch_shapes=[pltpu.VMEM((R, N), jnp.float32)] + scratch,
+            scratch_shapes=[pltpu.VMEM((count * R, N), jnp.float32), pltpu.VMEM((count * R, Q), jnp.bfloat16)] + scratch,
         ),
         out_shape=outs,
-        compiler_params=pltpu.CompilerParams(vmem_limit_bytes=32 << 20),
-        cost_estimate=pl.CostEstimate(flops=flops, bytes_accessed=4 * Q * N, transcendentals=0),
+        compiler_params=pltpu.CompilerParams(vmem_limit_bytes=40 << 20),
+        cost_estimate=pl.CostEstimate(flops=2 * count * R * Q * N, bytes_accessed=4 * Q * N, transcendentals=0),
         name=name,
     )(order, *args)
 
 
-def near_kernel(order, h_ref, pa_ref, pb_ref, ma_ref, mb_ref, r0_ref, r1_ref, p_ref, m_ref, y_ref):
-    out = partial_sum(order[8], pa_ref, pb_ref, h_ref, y_ref)
+def near_kernel(order, h_ref, pa_ref, pb_ref, ma_ref, mb_ref, p_ref, m_ref, y_ref, v_ref):
+    join(order[8], [(pa_ref, pb_ref), (ma_ref, mb_ref)], v_ref)
+    y_ref[...] = jnp.dot(v_ref[...], h_ref[...], preferred_element_type=jnp.float32)
+    for j in range(M):
+        p_ref[j * T : j * T + T, :] = taps(y_ref, 0, j)
+        m_ref[j * T : j * T + T, :] = taps(y_ref, 1, j)
+
+
+def own_kernel(order, h_ref, wa_ref, wb_ref, a_ref, o_ref, y_ref, v_ref):
+    join(order[8], [(wa_ref, wb_ref)], v_ref)
+    y_ref[...] = jnp.dot(v_ref[...], h_ref[...], preferred_element_type=jnp.float32)
     for j in range(M):
         at = slice(j * T, j * T + T)
-        value = out[j] + r0_ref[at, :].astype(jnp.float32) if j < 2 else out[j]
-        p_ref[at, :] = value.astype(jnp.bfloat16)
-    out = partial_sum(order[8], ma_ref, mb_ref, h_ref, y_ref)
-    for j in range(M):
-        at = slice(j * T, j * T + T)
-        value = out[j] + r1_ref[j * T - HB : j * T - HB + T, :].astype(jnp.float32) if j >= 2 else out[j]
-        m_ref[at, :] = value.astype(jnp.bfloat16)
-
-
-def own_kernel(order, h_ref, wa_ref, wb_ref, a_ref, o_ref, y_ref):
-    out = partial_sum(order[8], wa_ref, wb_ref, h_ref, y_ref)
-    for j in range(M):
-        at = slice(j * T, j * T + T)
-        o_ref[at, :] = out[j] + a_ref[at, :].astype(jnp.float32)
+        o_ref[at, :] = taps(y_ref, 0, j) + a_ref[at, :].astype(jnp.float32)
 
 
 def shift(value, axis, d):
@@ -237,7 +234,8 @@
     x, y, core = lax.axis_index("x"), lax.axis_index("y"), lax.axis_index("core")
     sec = x * 4 + y
     seq = lax.axis_index("z") * 2 + core
-    w = weights.transpose(0, 1, 3, 2).reshape(2, R, C)
+    w = pltpu.with_memory_space_constraint(weights.transpose(0, 1, 3, 2).reshape(2, R, C), pltpu.HBM)
+    held = pltpu.with_memory_space_constraint(inputs, pltpu.HBM)
     up = [(i, i + 1) for i in range(15)]
     down = [(i + 1, i) for i in range(15)]
     before = lax.ppermute(inputs[:, S - 4 :], ("z", "core"), up)
@@ -250,18 +248,17 @@
     mine = lax.all_to_all(send, "y", 0, 0, tiled=True)
     gain = lax.dynamic_index_in_dim(gains[1].reshape(4, 4, T), y, 1, False).reshape(Q, 1)
     gain = jnp.broadcast_to(gain, (Q, 128))
-    block, sq = first(inputs, halo, gains[0:1], w, info)
+    block, sq = first(held, halo, gains[0:1], w, info)
     block, sq, mine = lax.optimization_barrier((block, sq, mine))
     other = lax.ppermute(mine, "core", [(0, 1), (1, 0)])
     below, above = shift(block, "x", 1), shift(block, "x", -1)
     got = [block, below, above, shift(below[:HB], "x", 1), shift(above[HB:], "x", -1)]
-    for axis in ("x", "y"):
+    for axis in ("y", "x"):
         sq = sq + lax.ppermute(sq, axis, [(i, i ^ 1) for i in range(4)])
         sq = sq + lax.ppermute(sq, axis, [(i, i ^ 2) for i in range(4)])
     rel = [x, x + 3, x + 1, x + 2, y, y + 3, y + 1, y + 2]
     order = jnp.concatenate([jnp.stack(rel) % 4, core.reshape(1)]).astype(jnp.int32)
     half = jax.ShapeDtypeStruct((HB, S), jnp.bfloat16)
-    full = jax.ShapeDtypeStruct((M * T, S), jnp.bfloat16)
     h, far0, far1 = stage(
         far_kernel,
         order,
@@ -269,29 +266,33 @@
         [whole(B, S)] * 3 + [whole(HB, S), whole(B - HB, S), whole(1, N), whole(Q, 128)] + picked(7),
         [jax.ShapeDtypeStruct((Q, N), jnp.bfloat16), half, half],
         [pltpu.VMEM((8, N), jnp.float32)],
-        4 * R * Q * N,
+        1,
         "far",
     )
     r0, r1 = shift(far0, "y", 1), shift(far1, "y", -1)
+    one = jax.ShapeDtypeStruct((M * T, S), jnp.float32)
     plus, minus = stage(
         near_kernel,
         order,
-        (h, mine, other, mine, other, r0, r1),
-        [whole(Q, N)] + picked(6) + picked(5) + [whole(HB, S)] * 2,
-        [full, full],
+        (h, mine, other, mine, other),
+        [whole(Q, N)] + picked(6) + picked(5),
+        [one, one],
         [],
-        4 * R * Q * N,
+        2,
         "near",
     )
+    plus, minus, r0, r1 = lax.optimization_barrier((plus, minus, r0, r1))
+    plus = jnp.concatenate([plus[:HB] + r0.astype(jnp.float32), plus[HB:]], 0).astype(jnp.bfloat16)
+    minus = jnp.concatenate([minus[:HB], minus[HB:] + r1.astype(jnp.float32)], 0).astype(jnp.bfloat16)
     plus, minus, h = lax.optimization_barrier((plus, minus, h))
     (base,) = stage(
         own_kernel,
         order,
         (h, mine, other, block),
         [whole(Q, N)] + picked(4) + [whole(B, S)],
-        [jax.ShapeDtypeStruct((M * T, S), jnp.float32)],
+        [one],
         [],
-        2 * R * Q * N,
+        1,
         "own",
     )
     total = base + shift(plus, "y", 1).astype(jnp.float32) + shift(minus, "y", -1).astype(jnp.float32)

time: 86.5 us -> 73.5 us (0.85)
  local copies, waits for them, and re-layouts: 7.88 us -> 1.5 us
  waiting for transfers between devices: 19.9 us -> 14.7 us
  starting transfers between devices: 32.3 us -> 30.8 us
    unnamed x8 -> x2, local copies, waits for them, and re-layouts: 6.44 us -> 0.01 us
    ppermute x2, waiting for transfers between devices: 8.37 us -> 2.36 us  [local(): sq = sq + lax.ppermute(sq, axis, [(i, i ^ 1) for i in range(4)])]
    pallas_call x3, Pallas kernels: 12.8 us -> 10 us  [stage(): pl.pallas_call(kernel, grid_spec=pltpu.PrefetchScalarGridSpec(num_scalar_...]
    pallas_call x1, Pallas kernels: 9.55 us -> 11.3 us  [first(): pl.pallas_call(first_kernel, grid_spec=pltpu.PrefetchScalarGridSpec(num_s...]
    ppermute x8, waiting for transfers between devices: 6.88 us -> 5.21 us  [shift(): return lax.ppermute(value, axis, [(i, (i + d) % 4) for i in range(4)])]
    all_to_all x1, waiting for transfers between devices: 0.01 us -> 1.49 us  [local(): mine = lax.all_to_all(send, 'y', 0, 0, tiled=True)]
    pallas_call x1, Pallas kernels: 1.24 us -> 2.36 us  [prep(): pl.pallas_call(prep_kernel, grid_spec=pltpu.PrefetchScalarGridSpec(num_sc...]
    ppermute x2, waiting for transfers between devices: 4.66 us -> 5.65 us  [local(): sq = sq + lax.ppermute(sq, axis, [(i, i ^ 2) for i in range(4)])]
  transfers between devices with their start and end apart: 16 -> 16, of which waited for: 7 -> 6; matrix products, arithmetic and copies ran while one was open for 2% -> 2% of each run, Pallas kernels for 16% -> 27%
where the time goes in v4:
time: 73.5 us; the launch traced here: 73.2 us
  starting transfers between devices  30.8 us (42%)
  Pallas kernels  23.7 us (32%)
  waiting for transfers between devices  14.7 us (20%)
  other arithmetic  2.29 us (3%)
  local copies, waits for them, and re-layouts  1.5 us (2%)
    ppermute x8, starting transfers between devices, shift(): return lax.ppermute(value, axis, [(i, (i + d) % 4) for i in range(4)])  12.5 us
    pallas_call x1, Pallas kernels, first(): pl.pallas_call(first_kernel, grid_spec=pltpu.PrefetchScalarGridSpec(num_s...  11.3 us
    pallas_call x3, Pallas kernels, stage(): pl.pallas_call(kernel, grid_spec=pltpu.PrefetchScalarGridSpec(num_scalar_...  10 us
    ppermute x2, starting transfers between devices, local(): sq = sq + lax.ppermute(sq, axis, [(i, i ^ 2) for i in range(4)])  6.19 us
    ppermute x2, waiting for transfers between devices, local(): sq = sq + lax.ppermute(sq, axis, [(i, i ^ 2) for i in range(4)])  5.65 us
    ppermute x8, waiting for transfers between devices, shift(): return lax.ppermute(value, axis, [(i, (i + d) % 4) for i in range(4)])  5.21 us
    all_to_all x1, starting transfers between devices, local(): mine = lax.all_to_all(send, 'y', 0, 0, tiled=True)  4.46 us
    ppermute x1, starting transfers between devices, local(): after = lax.ppermute(inputs[:, :4], ('z', 'core'), down)  3.64 us
  transfers between devices with their start and end apart: 16, of which 6 were waited for; matrix products, arithmetic and copies ran while one was open for 2% of the time, Pallas kernels for 27%

profile of v4, /device:TPU:96, one launch (start us, length us, event | category | flops | bytes accessed | tf_op | source)
XLA Modules:
  0.0 73.2 jit_solution(323965863882477123)
XLA Ops:
  0.0 1.0 %fusion.1 = (bf16[4,4,1536]{2,1,0:T(4,128)(2,1)S(1)}, bf16[4,4,1536]{2,1,0:T(4,128)(2,1)S(1)}) fusion(bf16[4,512,1536]{2,1,0:T(8,128)(2,1)} %x_ref.1), kind=kLoop, calls=%fused_computation.17 | loop fusion | bytes 196608 | tf_op jit(solution)/shard_map/slice | solution.py:241
  1.0 1.9 %collective-permute-start = (bf16[4,4,1536]{2,1,0:T(4,128)(2,1)S(1)}, bf16[4,4,1536]{2,1,0:T(4,128)(2,1)S(1)}, u32[]{:S(2)}, u32[]{:S(2)}) collective-permute-start(bf16[4,4,1536]{2,1,0:T(4,128)(2,1)S(1)} %get-tuple-element.43), channel_id=1, source_target_pairs={{0,1},{1,2},{2,3},{3,4},{4,5},{5,6},{6,7},{7,8},{8,9},{9,10},{10,1... | collective-permute-start | bytes 147464 | tf_op jit(solution)/shard_map/ppermute | solution.py:241
  2.9 3.6 %collective-permute-start.1 = (bf16[4,4,1536]{2,1,0:T(4,128)(2,1)S(1)}, bf16[4,4,1536]{2,1,0:T(4,128)(2,1)S(1)}, u32[]{:S(2)}, u32[]{:S(2)}) collective-permute-start(bf16[4,4,1536]{2,1,0:T(4,128)(2,1)S(1)} %get-tuple-element.44), channel_id=1, source_target_pairs={{1,0},{2,1},{3,2},{4,3},{5,4},{6,5},{7,6},{8,7},{9,8},{10,9},{11,1... | collective-permute-start | bytes 147464 | tf_op jit(solution)/shard_map/ppermute | solution.py:242
  6.6 2.4 %prep.1 = bf16[4,240,384]{2,1,0:T(8,128)(2,1)} custom-call(s32[1]{0:T(128)} %bitcast.4.core, bf16[2,480,1536]{2,1,0:T(8,128)(2,1)} %bitcast.21), custom_call_target="tpu_custom_call" | custom-call | bytes 1474560 | tf_op jit(solution)/shard_map/prep/pallas_call | solution.py:134
  9.0 4.5 %all-to-all-start = ((bf16[4,240,384]{2,1,0:T(8,128)(2,1)}), bf16[4,240,384]{2,1,0:T(8,128)(2,1)S(1)}, u32[]{:S(2)}, u32[]{:S(2)}) async-start(bf16[4,240,384]{2,1,0:T(8,128)(2,1)} %prep.1), calls=%async_computation | async-start | bytes 1474560 | tf_op jit(solution)/shard_map/all_to_all | solution.py:248
  13.6 11.3 %first.1 = (bf16[400,512]{1,0:T(8,128)(2,1)S(1)}, f32[1,2176]{1,0:T(1,128)S(1)}) custom-call(s32[4]{0:T(128)S(1)} %pad_add_fusion.info, bf16[4,512,1536]{2,1,0:T(8,128)(2,1)} %x_ref.1, bf16[32,1536]{1,0:T(8,128)(2,1)S(1)} %maximum_bitcast_fusion.halo_ref, f32[1,1536]{1,0:T(1,128)S(1)} %get-tuple-element.46.gain_ref, bf16[2,480,1536]{2,1,0:T(8,128)(2,1)} %bitcast.22), custom_call_target="tpu_custom_call" | custom-call | flops 3019898880 | bytes 6291456 | tf_op jit(solution)/shard_map/first/pallas_call | solution.py:99
  24.9 1.5 %all-to-all-done.wa_ref.pa_ref.ma_ref = bf16[4,240,384]{2,1,0:T(8,128)(2,1)S(1)} async-done(((bf16[4,240,384]{2,1,0:T(8,128)(2,1)}), bf16[4,240,384]{2,1,0:T(8,128)(2,1)S(1)}, u32[]{:S(2)}, u32[]{:S(2)}) %all-to-all-start) | async-done | bytes 737312 | tf_op jit(solution)/shard_map/all_to_all | solution.py:248
  26.4 2.8 %collective-permute-start.3 = (bf16[400,512]{1,0:T(8,128)(2,1)S(1)}, bf16[400,512]{1,0:T(8,128)(2,1)S(1)}, u32[]{:S(2)}, u32[]{:S(2)}) collective-permute-start(bf16[400,512]{1,0:T(8,128)(2,1)S(1)} %get-tuple-element.28.a0.a_ref), channel_id=1, source_target_pairs={{0,192},{64,0},{128,64},{192,128},{1,193},{65,1},{129,65},{193,129... | collective-permute-start | bytes 1228808 | tf_op jit(solution)/shard_map/ppermute | solution.py:230
  29.2 1.3 %collective-permute-start.6 = (f32[1,2176]{1,0:T(1,128)S(1)}, f32[1,2176]{1,0:T(1,128)S(1)}, u32[]{:S(2)}, u32[]{:S(2)}) collective-permute-start(f32[1,2176]{1,0:T(1,128)S(1)} %get-tuple-element.29), channel_id=1, source_target_pairs={{0,16},{16,0},{32,48},{48,32},{1,17},{17,1},{33,49},{49,33},{2,18}... | collective-permute-start | bytes 26120 | tf_op jit(solution)/shard_map/ppermute | solution.py:257
  30.5 2.4 %collective-permute-done.6 = f32[1,2176]{1,0:T(1,128)S(1)} collective-permute-done((f32[1,2176]{1,0:T(1,128)S(1)}, f32[1,2176]{1,0:T(1,128)S(1)}, u32[]{:S(2)}, u32[]{:S(2)}) %collective-permute-start.6) | collective-permute-done | bytes 8736 | tf_op jit(solution)/shard_map/ppermute | solution.py:257
  32.9 2.9 %collective-permute-start.7 = (f32[1,2176]{1,0:T(1,128)S(1)}, f32[1,2176]{1,0:T(1,128)S(1)}, u32[]{:S(2)}, u32[]{:S(2)}) collective-permute-start(f32[1,2176]{1,0:T(1,128)S(1)} %add.68), channel_id=1, source_target_pairs={{0,32},{16,48},{32,0},{48,16},{1,33},{17,49},{33,1},{49,17},{2,34}... | collective-permute-start | bytes 26120 | tf_op jit(solution)/shard_map/ppermute | solution.py:258
  35.8 0.1 stack.55
  35.8 2.3 %collective-permute-done.7 = f32[1,2176]{1,0:T(1,128)S(1)} collective-permute-done((f32[1,2176]{1,0:T(1,128)S(1)}, f32[1,2176]{1,0:T(1,128)S(1)}, u32[]{:S(2)}, u32[]{:S(2)}) %collective-permute-start.7) | collective-permute-done | bytes 8736 | tf_op jit(solution)/shard_map/ppermute | solution.py:258
  38.1 0.8 %collective-permute-start.8 = (f32[1,2176]{1,0:T(1,128)S(1)}, f32[1,2176]{1,0:T(1,128)S(1)}, u32[]{:S(2)}, u32[]{:S(2)}) collective-permute-start(f32[1,2176]{1,0:T(1,128)S(1)} %add.69), channel_id=1, source_target_pairs={{0,64},{64,0},{128,192},{192,128},{1,65},{65,1},{129,193},{193,129... | collective-permute-start | bytes 26120 | tf_op jit(solution)/shard_map/ppermute | solution.py:257
  39.0 3.0 %collective-permute-start.5 = (bf16[208,512]{1,0:T(8,128)(2,1)S(1)}, bf16[208,512]{1,0:T(8,128)(2,1)S(1)}, u32[]{:S(2)}, u32[]{:S(2)}) collective-permute-start(bf16[208,512]{1,0:T(8,128)(2,1)S(1)} %slice.47), channel_id=1, source_target_pairs={{0,192},{64,0},{128,64},{192,128},{1,193},{65,1},{129,65},{193,129... | collective-permute-start | bytes 638984 | tf_op jit(solution)/shard_map/ppermute | solution.py:230
  42.1 3.3 %collective-permute-start.9 = (f32[1,2176]{1,0:T(1,128)S(1)}, f32[1,2176]{1,0:T(1,128)}, u32[]{:S(2)}, u32[]{:S(2)}) collective-permute-start(f32[1,2176]{1,0:T(1,128)S(1)} %add.70), channel_id=1, source_target_pairs={{0,128},{64,192},{128,0},{192,64},{1,129},{65,193},{129,1},{193,65... | collective-permute-start | bytes 26120 | tf_op jit(solution)/shard_map/ppermute | solution.py:258
  45.6 0.1 broadcast_in_dim.7
  45.7 3.4 %collective-permute-done.9 = f32[1,2176]{1,0:T(1,128)} collective-permute-done((f32[1,2176]{1,0:T(1,128)S(1)}, f32[1,2176]{1,0:T(1,128)}, u32[]{:S(2)}, u32[]{:S(2)}) %collective-permute-start.9) | collective-permute-done | bytes 8736 | tf_op jit(solution)/shard_map/ppermute | solution.py:258
  49.1 0.7 add.71.sq_ref
  49.8 0.1 broadcast_in_dim.8.gain_ref
  49.9 3.9 %far.1 = (bf16[384,2176]{1,0:T(8,128)(2,1)S(1)}, bf16[192,512]{1,0:T(8,128)(2,1)S(1)}, bf16[192,512]{1,0:T(8,128)(2,1)S(1)}) custom-call(s32[9]{0:T(128)S(1)} %pad_add_fusion.1.order, bf16[400,512]{1,0:T(8,128)(2,1)S(1)} %get-tuple-element.28.a0.a_ref, bf16[400,512]{1,0:T(8,128)(2,1)S(1)} %collective-permute-done.2.a1, ...), custom_call_target="tpu_custom_call" | custom-call | flops 802160640 | bytes 3342336 | tf_op jit(solution)/shard_map/far/pallas_call | solution.py:197
  53.8 1.8 %collective-permute-start.11 = (bf16[192,512]{1,0:T(8,128)(2,1)S(1)}, bf16[192,512]{1,0:T(8,128)(2,1)S(1)}, u32[]{:S(2)}, u32[]{:S(2)}) collective-permute-start(bf16[192,512]{1,0:T(8,128)(2,1)S(1)} %get-tuple-element.34), channel_id=1, source_target_pairs={{0,16},{16,32},{32,48},{48,0},{1,17},{17,33},{33,49},{49,1},{2,18}... | collective-permute-start | bytes 589832 | tf_op jit(solution)/shard_map/ppermute | solution.py:230
  55.6 1.5 %collective-permute-start.12 = (bf16[192,512]{1,0:T(8,128)(2,1)S(1)}, bf16[192,512]{1,0:T(8,128)(2,1)S(1)}, u32[]{:S(2)}, u32[]{:S(2)}) collective-permute-start(bf16[192,512]{1,0:T(8,128)(2,1)S(1)} %get-tuple-element.35), channel_id=1, source_target_pairs={{0,48},{16,0},{32,16},{48,32},{1,49},{17,1},{33,17},{49,33},{2,50}... | collective-permute-start | bytes 589832 | tf_op jit(solution)/shard_map/ppermute | solution.py:230
  57.1 3.8 %near.1 = (f32[384,512]{1,0:T(8,128)S(1)}, f32[384,512]{1,0:T(8,128)S(1)}) custom-call(s32[9]{0:T(128)S(1)} %pad_add_fusion.1.order, bf16[384,2176]{1,0:T(8,128)(2,1)S(1)} %get-tuple-element.40.h_ref, bf16[4,240,384]{2,1,0:T(8,128)(2,1)S(1)} %all-to-all-done.wa_ref.pa_ref.ma_ref, bf16[4,240,384]{2,1,0:T(8,128)(2,1)S(1)} %collective-permute-done.10.wb_ref.pb_ref.mb_ref, ...), custom_call_target="tpu_custom_call" | custom-call | flops 1604321280 | bytes 3342336 | tf_op jit(solution)/shard_map/near/pallas_call | solution.py:197
  60.9 0.3 collective-permute-done.12
  61.3 0.1 add_convert_fusion.1
  61.6 1.5 %collective-permute-start.13 = (bf16[384,512]{1,0:T(8,128)(2,1)S(1)}, bf16[384,512]{1,0:T(8,128)(2,1)S(1)}, u32[]{:S(2)}, u32[]{:S(2)}) collective-permute-start(bf16[384,512]{1,0:T(8,128)(2,1)S(1)} %pad_maximum_fusion.1), channel_id=1, source_target_pairs={{0,16},{16,32},{32,48},{48,0},{1,17},{17,33},{33,49},{49,1},{2,18}... | collective-permute-start | bytes 1179656 | tf_op jit(solution)/shard_map/ppermute | solution.py:230
  63.1 1.8 %collective-permute-start.14 = (bf16[384,512]{1,0:T(8,128)(2,1)S(1)}, bf16[384,512]{1,0:T(8,128)(2,1)S(1)}, u32[]{:S(2)}, u32[]{:S(2)}) collective-permute-start(bf16[384,512]{1,0:T(8,128)(2,1)S(1)} %pad_maximum_fusion.2), channel_id=1, source_target_pairs={{0,48},{16,0},{32,16},{48,32},{1,49},{17,1},{33,17},{49,33},{2,50}... | collective-permute-start | bytes 1179656 | tf_op jit(solution)/shard_map/ppermute | solution.py:230
  64.9 2.3 %own.1 = f32[384,512]{1,0:T(8,128)S(1)} custom-call(s32[9]{0:T(128)S(1)} %pad_add_fusion.1.order, bf16[384,2176]{1,0:T(8,128)(2,1)S(1)} %get-tuple-element.40.h_ref, bf16[4,240,384]{2,1,0:T(8,128)(2,1)S(1)} %all-to-all-done.wa_ref.pa_ref.ma_ref, bf16[4,240,384]{2,1,0:T(8,128)(2,1)S(1)} %collective-permute-done.10.wb_ref.pb_ref.mb_ref, ...), custom_call_target="tpu_custom_call" | custom-call | flops 802160640 | bytes 3342336 | tf_op jit(solution)/shard_map/own/pallas_call | solution.py:197
  67.2 4.9 %collective-permute-done.13 = bf16[384,512]{1,0:T(8,128)(2,1)S(1)} collective-permute-done((bf16[384,512]{1,0:T(8,128)(2,1)S(1)}, bf16[384,512]{1,0:T(8,128)(2,1)S(1)}, u32[]{:S(2)}, u32[]{:S(2)}) %collective-permute-start.13) | collective-permute-done | bytes 393248 | tf_op jit(solution)/shard_map/ppermute | solution.py:230
  72.1 0.2 add_convert_fusion
  72.3 0.9 %pad_maximum_fusion = bf16[768,512]{1,0:T(8,128)(2,1)} fusion(bf16[384,512]{1,0:T(8,128)(2,1)S(1)} %add_convert_fusion, bf16[384,512]{1,0:T(8,128)(2,1)S(1)} %slice.38), kind=kLoop, calls=%fused_computation | loop fusion | flops 1572864 | bytes 1572864 | tf_op jit(solution)/shard_map/concatenate | solution.py:299
  (32 shorter events, 0.7 us)
Async XLA Ops:
  1.0 12.6 %collective-permute-start = (bf16[4,4,1536]{2,1,0:T(4,128)(2,1)S(1)}, bf16[4,4,1536]{2,1,0:T(4,128)(2,1)S(1)}, u32[]{:S(2)}, u32[]{:S(2)}) collective-permute-start(bf16[4,4,1536]{2,1,0:T(4,128)(2,1)S(1)} %get-tuple-element.43), channel_id=1, source_target_pairs={{0,1},{1,2},{2,3},{3,4},{4,5},{5,6},{6,7},{7,8},{8,9},{9,10},{10,1... | collective-permute-start | bytes 147464 | tf_op jit(solution)/shard_map/ppermute | solution.py:241
  2.9 10.6 %collective-permute-start.1 = (bf16[4,4,1536]{2,1,0:T(4,128)(2,1)S(1)}, bf16[4,4,1536]{2,1,0:T(4,128)(2,1)S(1)}, u32[]{:S(2)}, u32[]{:S(2)}) collective-permute-start(bf16[4,4,1536]{2,1,0:T(4,128)(2,1)S(1)} %get-tuple-element.44), channel_id=1, source_target_pairs={{1,0},{2,1},{3,2},{4,3},{5,4},{6,5},{7,6},{8,7},{9,8},{10,9},{11,1... | collective-permute-start | bytes 147464 | tf_op jit(solution)/shard_map/ppermute | solution.py:242
  6.6 6.9 %copy-start = (f32[2,1536]{1,0:T(2,128)S(1)}, f32[2,1536]{1,0:T(2,128)}, u32[]{:S(2)}) copy-start(f32[2,1536]{1,0:T(2,128)} %param.5) | copy-start | bytes 36868
  9.0 17.4 %all-to-all-start = ((bf16[4,240,384]{2,1,0:T(8,128)(2,1)}), bf16[4,240,384]{2,1,0:T(8,128)(2,1)S(1)}, u32[]{:S(2)}, u32[]{:S(2)}) async-start(bf16[4,240,384]{2,1,0:T(8,128)(2,1)} %prep.1), calls=%async_computation | async-start | bytes 1474560 | tf_op jit(solution)/shard_map/all_to_all | solution.py:248
  26.4 12.5 %collective-permute-start.3 = (bf16[400,512]{1,0:T(8,128)(2,1)S(1)}, bf16[400,512]{1,0:T(8,128)(2,1)S(1)}, u32[]{:S(2)}, u32[]{:S(2)}) collective-permute-start(bf16[400,512]{1,0:T(8,128)(2,1)S(1)} %get-tuple-element.28.a0.a_ref), channel_id=1, source_target_pairs={{0,192},{64,0},{128,64},{192,128},{1,193},{65,1},{129,65},{193,129... | collective-permute-start | bytes 1228808 | tf_op jit(solution)/shard_map/ppermute | solution.py:230
  29.2 12.8 %collective-permute-start.2 = (bf16[400,512]{1,0:T(8,128)(2,1)S(1)}, bf16[400,512]{1,0:T(8,128)(2,1)S(1)}, u32[]{:S(2)}, u32[]{:S(2)}) collective-permute-start(bf16[400,512]{1,0:T(8,128)(2,1)S(1)} %get-tuple-element.28.a0.a_ref), channel_id=1, source_target_pairs={{0,64},{64,128},{128,192},{192,0},{1,65},{65,129},{129,193},{193,1... | collective-permute-start | bytes 1228808 | tf_op jit(solution)/shard_map/ppermute | solution.py:230
  29.2 20.6 %collective-permute-start.10 = (bf16[4,240,384]{2,1,0:T(8,128)(2,1)S(1)}, bf16[4,240,384]{2,1,0:T(8,128)(2,1)S(1)}, u32[]{:S(2)}, u32[]{:S(2)}) collective-permute-start(bf16[4,240,384]{2,1,0:T(8,128)(2,1)S(1)} %all-to-all-done.wa_ref.pa_ref.ma_ref), channel_id=1, source_target_pairs={{0,1},{1,0},{2,3},{3,2},{4,5},{5,4},{6,7},{7,6},{8,9},{9,8},{10,11... | collective-permute-start | bytes 2211848 | tf_op jit(solution)/shard_map/ppermute | solution.py:253
  29.2 3.7 %collective-permute-start.6 = (f32[1,2176]{1,0:T(1,128)S(1)}, f32[1,2176]{1,0:T(1,128)S(1)}, u32[]{:S(2)}, u32[]{:S(2)}) collective-permute-start(f32[1,2176]{1,0:T(1,128)S(1)} %get-tuple-element.29), channel_id=1, source_target_pairs={{0,16},{16,0},{32,48},{48,32},{1,17},{17,1},{33,49},{49,33},{2,18}... | collective-permute-start | bytes 26120 | tf_op jit(solution)/shard_map/ppermute | solution.py:257
  32.9 5.2 %collective-permute-start.7 = (f32[1,2176]{1,0:T(1,128)S(1)}, f32[1,2176]{1,0:T(1,128)S(1)}, u32[]{:S(2)}, u32[]{:S(2)}) collective-permute-start(f32[1,2176]{1,0:T(1,128)S(1)} %add.68), channel_id=1, source_target_pairs={{0,32},{16,48},{32,0},{48,16},{1,33},{17,49},{33,1},{49,17},{2,34}... | collective-permute-start | bytes 26120 | tf_op jit(solution)/shard_map/ppermute | solution.py:258
  38.1 4.0 %collective-permute-start.8 = (f32[1,2176]{1,0:T(1,128)S(1)}, f32[1,2176]{1,0:T(1,128)S(1)}, u32[]{:S(2)}, u32[]{:S(2)}) collective-permute-start(f32[1,2176]{1,0:T(1,128)S(1)} %add.69), channel_id=1, source_target_pairs={{0,64},{64,0},{128,192},{192,128},{1,65},{65,1},{129,193},{193,129... | collective-permute-start | bytes 26120 | tf_op jit(solution)/shard_map/ppermute | solution.py:257
  39.0 10.8 %collective-permute-start.5 = (bf16[208,512]{1,0:T(8,128)(2,1)S(1)}, bf16[208,512]{1,0:T(8,128)(2,1)S(1)}, u32[]{:S(2)}, u32[]{:S(2)}) collective-permute-start(bf16[208,512]{1,0:T(8,128)(2,1)S(1)} %slice.47), channel_id=1, source_target_pairs={{0,192},{64,0},{128,64},{192,128},{1,193},{65,1},{129,65},{193,129... | collective-permute-start | bytes 638984 | tf_op jit(solution)/shard_map/ppermute | solution.py:230
  42.0 7.8 %collective-permute-start.4 = (bf16[192,512]{1,0:T(8,128)(2,1)S(1)}, bf16[192,512]{1,0:T(8,128)(2,1)S(1)}, u32[]{:S(2)}, u32[]{:S(2)}) collective-permute-start(bf16[192,512]{1,0:T(8,128)(2,1)S(1)} %slice.46), channel_id=1, source_target_pairs={{0,64},{64,128},{128,192},{192,0},{1,65},{65,129},{129,193},{193,1... | collective-permute-start | bytes 589832 | tf_op jit(solution)/shard_map/ppermute | solution.py:230
  42.1 6.9 %collective-permute-start.9 = (f32[1,2176]{1,0:T(1,128)S(1)}, f32[1,2176]{1,0:T(1,128)}, u32[]{:S(2)}, u32[]{:S(2)}) collective-permute-start(f32[1,2176]{1,0:T(1,128)S(1)} %add.70), channel_id=1, source_target_pairs={{0,128},{64,192},{128,0},{192,64},{1,129},{65,193},{129,1},{193,65... | collective-permute-start | bytes 26120 | tf_op jit(solution)/shard_map/ppermute | solution.py:258
  53.8 7.1 %collective-permute-start.11 = (bf16[192,512]{1,0:T(8,128)(2,1)S(1)}, bf16[192,512]{1,0:T(8,128)(2,1)S(1)}, u32[]{:S(2)}, u32[]{:S(2)}) collective-permute-start(bf16[192,512]{1,0:T(8,128)(2,1)S(1)} %get-tuple-element.34), channel_id=1, source_target_pairs={{0,16},{16,32},{32,48},{48,0},{1,17},{17,33},{33,49},{49,1},{2,18}... | collective-permute-start | bytes 589832 | tf_op jit(solution)/shard_map/ppermute | solution.py:230
  55.6 5.7 %collective-permute-start.12 = (bf16[192,512]{1,0:T(8,128)(2,1)S(1)}, bf16[192,512]{1,0:T(8,128)(2,1)S(1)}, u32[]{:S(2)}, u32[]{:S(2)}) collective-permute-start(bf16[192,512]{1,0:T(8,128)(2,1)S(1)} %get-tuple-element.35), channel_id=1, source_target_pairs={{0,48},{16,0},{32,16},{48,32},{1,49},{17,1},{33,17},{49,33},{2,50}... | collective-permute-start | bytes 589832 | tf_op jit(solution)/shard_map/ppermute | solution.py:230
  61.6 10.5 %collective-permute-start.13 = (bf16[384,512]{1,0:T(8,128)(2,1)S(1)}, bf16[384,512]{1,0:T(8,128)(2,1)S(1)}, u32[]{:S(2)}, u32[]{:S(2)}) collective-permute-start(bf16[384,512]{1,0:T(8,128)(2,1)S(1)} %pad_maximum_fusion.1), channel_id=1, source_target_pairs={{0,16},{16,32},{32,48},{48,0},{1,17},{17,33},{33,49},{49,1},{2,18}... | collective-permute-start | bytes 1179656 | tf_op jit(solution)/shard_map/ppermute | solution.py:230
  63.1 9.0 %collective-permute-start.14 = (bf16[384,512]{1,0:T(8,128)(2,1)S(1)}, bf16[384,512]{1,0:T(8,128)(2,1)S(1)}, u32[]{:S(2)}, u32[]{:S(2)}) collective-permute-start(bf16[384,512]{1,0:T(8,128)(2,1)S(1)} %pad_maximum_fusion.2), channel_id=1, source_target_pairs={{0,48},{16,0},{32,16},{48,32},{1,49},{17,1},{33,17},{49,33},{2,50}... | collective-permute-start | bytes 1179656 | tf_op jit(solution)/shard_map/ppermute | solution.py:230

commit v5 on v4

--- a/solution.py
+++ b/solution.py
@@ -11,8 +11,9 @@
 R = 480
 S = 512
 M = 4
-B = 400
+B = 208
 HB = 192
+L = 17
 Q = 384
 HR = 240
 N = M * S + 128
@@ -36,7 +37,7 @@
     return total
 
 
-def first_kernel(info, x_ref, halo_ref, gain_ref, w_ref, o_ref, sq_ref, h_ref, y_ref, hy_ref, hr_ref):
+def first_kernel(info, x_ref, halo_ref, gain_ref, w_ref, o_ref, sq_ref, h_ref, y_ref, hy_ref, hr_ref, base):
     i = pl.program_id(0)
     start = pl.multiple_of(info[0] * 128, 128)
     off = info[1]
@@ -70,44 +71,46 @@
         y_ref[2 * T : 3 * T, to] += lax.dot_general(
             pick, x_ref[0, at, window], NT, preferred_element_type=jnp.float32
         )
-    y_ref[:, 0:128] = pltpu.roll(hy_ref[...], lax.rem(252 - 8 * i, 128), 1)
-    y_ref[:, 128 + S :] = pltpu.roll(hy_ref[...], lax.rem(252 - 8 * i, 128), 1)
+    b = base + i
+    y_ref[:, 0:128] = pltpu.roll(hy_ref[...], lax.rem(252 - 8 * b, 128), 1)
+    y_ref[:, 128 + S :] = pltpu.roll(hy_ref[...], lax.rem(252 - 8 * b, 128), 1)
     out = combine(y_ref[...])
     out = out.astype(jnp.bfloat16)
     o_ref[pl.ds(pl.multiple_of(i * T, 16), T), :] = out[:, 128 : 128 + S]
     out = out.astype(jnp.float32)
     squares = jnp.sum(out * out, axis=0, keepdims=True)
-    sq_ref[:, pl.ds(pl.multiple_of(i * S, 128), S)] = squares[:, 128 : 128 + S]
+    for q in range(4):
+        sq_ref[pl.ds(4 * b + q, 1), :] = squares[:, 128 + 128 * q : 256 + 128 * q]
     pad = jnp.zeros((32, 128), jnp.float32)
     left = jnp.concatenate([out[:, 0:128], pad], 0).T
     right = jnp.concatenate([out[:, 128 + S :], pad], 0).T
     keep_left = (info[2] > 0).astype(jnp.float32)
     keep_right = (info[3] > 0).astype(jnp.float32)
-    lane = lax.broadcasted_iota(jnp.int32, (1, 128), 1) - 4 * i
-    turn = lax.rem(4 * i + 2, 128)
+    lane = lax.broadcasted_iota(jnp.int32, (1, 128), 1) - 4 * b
+    turn = lax.rem(4 * b + 2, 128)
     edge = jnp.where((lane == 0) | (lane == 1), pltpu.roll(squares[:, 0:128], turn, 1) * keep_left, 0.0)
     edge += jnp.where((lane == 2) | (lane == 3), pltpu.roll(squares[:, 128 + S :], turn, 1) * keep_right, 0.0)
-    sq_ref[:, M * S :] += edge
+    sq_ref[L - 1 : L, :] += edge
     line = jnp.concatenate(
         [left[126:127] * keep_left, left[127:128] * keep_left, right[0:1] * keep_right, right[1:2] * keep_right], 1
     )
     hr_ref[pl.ds(i, 1), :] = line
-    o_ref[M * T :, :] = hr_ref[...].astype(jnp.bfloat16)
-
-
-def first(x, halo, gain, w, info):
+    o_ref[HB:, :] = hr_ref[...].astype(jnp.bfloat16)
+
+
+def first(x, halo, gain, w, info, base):
     return pl.pallas_call(
-        first_kernel,
+        functools.partial(first_kernel, base=base),
         grid_spec=pltpu.PrefetchScalarGridSpec(
             num_scalar_prefetch=1,
-            grid=(M,),
+            grid=(2,),
             in_specs=[
-                pl.BlockSpec((1, S, C), lambda i, info: (i, 0, 0)),
+                pl.BlockSpec((1, S, C), lambda i, info: (base + i, 0, 0)),
                 whole(32, C),
                 whole(1, C),
                 pl.BlockSpec((None, R, C), lambda i, info: (0, 0, 0)),
             ],
-            out_specs=[whole(B, S), whole(1, N)],
+            out_specs=[whole(B, S), whole(L, 128)],
             scratch_shapes=[
                 pltpu.VMEM((S, C), jnp.bfloat16),
                 pltpu.VMEM((R, S + 256), jnp.float32),
@@ -115,19 +118,15 @@
                 pltpu.VMEM((16, S), jnp.float32),
             ],
         ),
-        out_shape=[jax.ShapeDtypeStruct((B, S), jnp.bfloat16), jax.ShapeDtypeStruct((1, N), jnp.float32)],
+        out_shape=[jax.ShapeDtypeStruct((B, S), jnp.bfloat16), jax.ShapeDtypeStruct((L, 128), jnp.float32)],
         compiler_params=pltpu.CompilerParams(dimension_semantics=("arbitrary",), vmem_limit_bytes=32 << 20),
-        cost_estimate=pl.CostEstimate(flops=2 * M * S * R * C, bytes_accessed=2 * M * S * C, transcendentals=M * S * C),
+        cost_estimate=pl.CostEstimate(flops=4 * S * R * C, bytes_accessed=4 * S * C, transcendentals=2 * S * C),
         name="first",
     )(info, x, halo, gain, w)
 
 
 def prep_kernel(core, w_ref, o_ref):
-    for r in range(0, HR, 80):
-        v = w_ref[r : r + 80, :].astype(jnp.float32)
-        for b in range(4):
-            cols = [v[:, (a * 4 + b) * T : (a * 4 + b) * T + T] for a in range(4)]
-            o_ref[b, r : r + 80, :] = jnp.concatenate(cols, 1).astype(jnp.bfloat16)
+    o_ref[...] = w_ref[...]
 
 
 def prep(core, w):
@@ -135,12 +134,11 @@
         prep_kernel,
         grid_spec=pltpu.PrefetchScalarGridSpec(
             num_scalar_prefetch=1,
-            grid=(1,),
-            in_specs=[pl.BlockSpec((None, HR, C), lambda i, core: (1, core[0], 0))],
-            out_specs=whole(4, HR, Q),
+            grid=(4,),
+            in_specs=[pl.BlockSpec((None, HR, Q), lambda i, core: (1, core[0], i))],
+            out_specs=pl.BlockSpec((None, HR, Q), lambda i, core: (i, 0, 0)),
         ),
         out_shape=jax.ShapeDtypeStruct((4, HR, Q), jnp.bfloat16),
-        compiler_params=pltpu.CompilerParams(vmem_limit_bytes=16 << 20),
         cost_estimate=pl.CostEstimate(flops=0, bytes_accessed=4 * HR * C, transcendentals=0),
         name="prep",
     )(core, w)
@@ -159,30 +157,34 @@
     return combine(wide)[:, 128 : 128 + S]
 
 
-def far_kernel(order, a0, a1, a2, a3, a4, sq_ref, gain_ref, wa_ref, wb_ref, h_ref, far0_ref, far1_ref, y_ref, v_ref, s_ref):
+def far_kernel(order, *refs):
+    got, (sq_ref, gain_ref, wa_ref, wb_ref, h_ref, far0_ref, far1_ref, y_ref, v_ref, s_ref) = refs[:8], refs[8:]
     join(order[8], [(wa_ref, wb_ref)], v_ref)
-    s_ref[...] = jnp.broadcast_to(lax.rsqrt(sq_ref[...] * (1.0 / C) + 1e-06), s_ref.shape)
-
-    def put(piece, parts, lines):
+    total = sq_ref[0]
+    for n in range(1, 16):
+        total = total + sq_ref[n]
+    scale = lax.rsqrt(total * (1.0 / C) + 1e-06)
+    for r in range(L):
+        s_ref[:, 128 * r : 128 * r + 128] = jnp.broadcast_to(scale[r : r + 1, :], (8, 128))
+
+    for piece in range(4):
+        pair = got[2 * piece : 2 * piece + 2]
         dest = pl.multiple_of(order[piece] * T, 16)
         gain = gain_ref[pl.ds(dest, T), :]
-        lines = lines.astype(jnp.float32)
+        lines = [ref[HB:, :].astype(jnp.float32) for ref in pair]
         tile = jnp.concatenate(
-            [lines[j : j + 1, 128 * q : 128 * q + 128] for j in range(M) for q in range(4)]
+            [lines[j // 2][j % 2 : j % 2 + 1, 128 * q : 128 * q + 128] for j in range(M) for q in range(4)]
             + [jnp.zeros((112, 128), jnp.float32)],
             0,
         )
         h_ref[pl.ds(dest, T), M * S :] = gelu(tile.T[0:T] * s_ref[0:1, M * S :] * gain).astype(jnp.bfloat16)
         for j in range(M):
-            ref, row = parts[j]
+            row = j % 2 * T
             for q in range(4):
                 lane = slice(j * S + 128 * q, j * S + 128 * q + 128)
-                v = ref[row : row + T, 128 * q : 128 * q + 128].astype(jnp.float32)
+                v = pair[j // 2][row : row + T, 128 * q : 128 * q + 128].astype(jnp.float32)
                 h_ref[pl.ds(dest, T), lane] = gelu(v * s_ref[0:1, lane] * gain).astype(jnp.bfloat16)
 
-    for piece, ref in enumerate((a0, a1, a2)):
-        put(piece, [(ref, j * T) for j in range(M)], ref[M * T :, :])
-    put(3, [(a3, 0), (a3, T), (a4, 0), (a4, T)], a4[HB:, :])
     y_ref[...] = jnp.dot(v_ref[...], h_ref[...], preferred_element_type=jnp.float32)
     for j in range(2):
         far0_ref[j * T : j * T + T, :] = taps(y_ref, 0, j).astype(jnp.bfloat16)
@@ -218,12 +220,13 @@
         m_ref[j * T : j * T + T, :] = taps(y_ref, 1, j)
 
 
-def own_kernel(order, h_ref, wa_ref, wb_ref, a_ref, o_ref, y_ref, v_ref):
+def own_kernel(order, h_ref, wa_ref, wb_ref, a0_ref, a1_ref, o_ref, y_ref, v_ref):
     join(order[8], [(wa_ref, wb_ref)], v_ref)
     y_ref[...] = jnp.dot(v_ref[...], h_ref[...], preferred_element_type=jnp.float32)
     for j in range(M):
         at = slice(j * T, j * T + T)
-        o_ref[at, :] = taps(y_ref, 0, j) + a_ref[at, :].astype(jnp.float32)
+        a = (a0_ref, a1_ref)[j // 2][j % 2 * T : j % 2 * T + T, :]
+        o_ref[at, :] = taps(y_ref, 0, j) + a.astype(jnp.float32)
 
 
 def shift(value, axis, d):
@@ -245,38 +248,39 @@
     block = jnp.minimum(sec * T // 128, 10)
     info = jnp.stack([block, sec * T - block * 128, seq, 15 - seq]).astype(jnp.int32)
     info, send = lax.optimization_barrier((info, send))
-    mine = lax.all_to_all(send, "y", 0, 0, tiled=True)
-    gain = lax.dynamic_index_in_dim(gains[1].reshape(4, 4, T), y, 1, False).reshape(Q, 1)
+    mine = lax.all_to_all(send, "x", 0, 0, tiled=True)
+    gain = lax.dynamic_index_in_dim(gains[1].reshape(4, Q), x, 0, False).reshape(Q, 1)
     gain = jnp.broadcast_to(gain, (Q, 128))
-    block, sq = first(held, halo, gains[0:1], w, info)
-    block, sq, mine = lax.optimization_barrier((block, sq, mine))
+    one0, sq0 = first(held, halo, gains[0:1], w, info, 0)
+    one1, sq1 = first(held, halo, gains[0:1], w, info, 2)
+    one1, sq1, mine = lax.optimization_barrier((one1, sq1, mine))
+    below0, above0 = shift(one0, "y", 1), shift(one0, "y", -1)
+    below1, above1 = shift(one1, "y", 1), shift(one1, "y", -1)
+    got = [one0, one1, below0, below1, above0, above1, shift(below0, "y", 1), shift(above1, "y", -1)]
+    sq = jnp.broadcast_to((sq0 + sq1)[None], (16, L, 128))
+    sq = lax.all_to_all(sq, ("x", "y"), 0, 0, tiled=True)
     other = lax.ppermute(mine, "core", [(0, 1), (1, 0)])
-    below, above = shift(block, "x", 1), shift(block, "x", -1)
-    got = [block, below, above, shift(below[:HB], "x", 1), shift(above[HB:], "x", -1)]
-    for axis in ("y", "x"):
-        sq = sq + lax.ppermute(sq, axis, [(i, i ^ 1) for i in range(4)])
-        sq = sq + lax.ppermute(sq, axis, [(i, i ^ 2) for i in range(4)])
-    rel = [x, x + 3, x + 1, x + 2, y, y + 3, y + 1, y + 2]
+    rel = [y, y + 3, y + 1, y + 2, x, x + 3, x + 1, x + 2]
     order = jnp.concatenate([jnp.stack(rel) % 4, core.reshape(1)]).astype(jnp.int32)
     half = jax.ShapeDtypeStruct((HB, S), jnp.bfloat16)
     h, far0, far1 = stage(
         far_kernel,
         order,
         (*got, sq, gain, mine, other),
-        [whole(B, S)] * 3 + [whole(HB, S), whole(B - HB, S), whole(1, N), whole(Q, 128)] + picked(7),
+        [whole(B, S)] * 8 + [whole(16, L, 128), whole(Q, 128)] + picked(7),
         [jax.ShapeDtypeStruct((Q, N), jnp.bfloat16), half, half],
         [pltpu.VMEM((8, N), jnp.float32)],
         1,
         "far",
     )
-    r0, r1 = shift(far0, "y", 1), shift(far1, "y", -1)
-    one = jax.ShapeDtypeStruct((M * T, S), jnp.float32)
+    r0, r1 = shift(far0, "x", 1), shift(far1, "x", -1)
+    wide = jax.ShapeDtypeStruct((M * T, S), jnp.float32)
     plus, minus = stage(
         near_kernel,
         order,
         (h, mine, other, mine, other),
         [whole(Q, N)] + picked(6) + picked(5),
-        [one, one],
+        [wide, wide],
         [],
         2,
         "near",
@@ -288,15 +292,15 @@
     (base,) = stage(
         own_kernel,
         order,
-        (h, mine, other, block),
-        [whole(Q, N)] + picked(4) + [whole(B, S)],
-        [one],
+        (h, mine, other, one0, one1),
+        [whole(Q, N)] + picked(4) + [whole(B, S)] * 2,
+        [wide],
         [],
         1,
         "own",
     )
-    total = base + shift(plus, "y", 1).astype(jnp.float32) + shift(minus, "y", -1).astype(jnp.float32)
-    out = jnp.concatenate([block[: M * T], total.astype(jnp.bfloat16)], 0)
+    total = base + shift(plus, "x", 1).astype(jnp.float32) + shift(minus, "x", -1).astype(jnp.float32)
+    out = jnp.concatenate([one0[:HB], one1[:HB], total.astype(jnp.bfloat16)], 0)
     return out.reshape(2, M, T, S).transpose(0, 1, 3, 2)
 
 

time: 73.5 us -> 84.1 us (1.14)
  waiting for transfers between devices: 14.7 us -> 21 us
  Pallas kernels: 23.7 us -> 27.6 us
    all_to_all x1 -> x2, waiting for transfers between devices: 1.49 us -> 10.2 us  [the longest x1 5.64 us: local(): mine = lax.all_to_all(send, 'x', 0, 0, tiled=True)]
    ppermute x4 -> x0, starting transfers between devices: 8.33 us -> none  [the longest x2 6.19 us: local(): sq = sq + lax.ppermute(sq, axis, [(i, i ^ 2) for i in range(4)])]
    ppermute x4 -> x0, waiting for transfers between devices: 8.01 us -> none  [the longest x2 5.65 us: local(): sq = sq + lax.ppermute(sq, axis, [(i, i ^ 2) for i in range(4)])]
    ppermute x8 -> x10, waiting for transfers between devices: 5.21 us -> 10.8 us  [shift(): return lax.ppermute(value, axis, [(i, (i + d) % 4) for i in range(4)])]
    all_to_all x1 -> x2, starting transfers between devices: 4.46 us -> 9.11 us  [the longest x1 4.82 us: local(): sq = lax.all_to_all(sq, ('x', 'y'), 0, 0, tiled=True)]
    ppermute x8 -> x10, starting transfers between devices: 12.5 us -> 16.5 us  [shift(): return lax.ppermute(value, axis, [(i, (i + d) % 4) for i in range(4)])]
    pallas_call x1 -> x2, Pallas kernels: 11.3 us -> 14.3 us  [first(): pl.pallas_call(functools.partial(first_kernel, base=base), grid_spec=pltp...]
    pallas_call x1, Pallas kernels: 2.36 us -> 3.26 us  [prep(): pl.pallas_call(prep_kernel, grid_spec=pltpu.PrefetchScalarGridSpec(num_sc...]
  transfers between devices with their start and end apart: 16 -> 15, of which waited for: 6 -> 6; matrix products, arithmetic and copies ran while one was open for 2% -> 1% of each run, Pallas kernels for 27% -> 28%
where the time goes in v5:
time: 84.1 us; the launch traced here: 83.5 us
  starting transfers between devices  31.3 us (37%)
  Pallas kernels  27.6 us (33%)
  waiting for transfers between devices  21 us (25%)
  local copies, waits for them, and re-layouts  2.01 us (2%)
  other arithmetic  1.49 us (2%)
    ppermute x10, starting transfers between devices, shift(): return lax.ppermute(value, axis, [(i, (i + d) % 4) for i in range(4)])  16.5 us
    pallas_call x2, Pallas kernels, first(): pl.pallas_call(functools.partial(first_kernel, base=base), grid_spec=pltp...  14.3 us
    ppermute x10, waiting for transfers between devices, shift(): return lax.ppermute(value, axis, [(i, (i + d) % 4) for i in range(4)])  10.8 us
    pallas_call x3, Pallas kernels, stage(): pl.pallas_call(kernel, grid_spec=pltpu.PrefetchScalarGridSpec(num_scalar_...  10 us
    all_to_all x1, waiting for transfers between devices, local(): mine = lax.all_to_all(send, 'x', 0, 0, tiled=True)  5.64 us
    all_to_all x1, starting transfers between devices, local(): sq = lax.all_to_all(sq, ('x', 'y'), 0, 0, tiled=True)  4.82 us
    all_to_all x1, waiting for transfers between devices, local(): sq = lax.all_to_all(sq, ('x', 'y'), 0, 0, tiled=True)  4.55 us
    all_to_all x1, starting transfers between devices, local(): mine = lax.all_to_all(send, 'x', 0, 0, tiled=True)  4.29 us
  transfers between devices with their start and end apart: 15, of which 6 were waited for; matrix products, arithmetic and copies ran while one was open for 1% of the time, Pallas kernels for 28%

profile of v5, /device:TPU:96, one launch (start us, length us, event | category | flops | bytes accessed | tf_op | source)
XLA Modules:
  0.0 83.5 jit_solution(4052008252507871821)
XLA Ops:
  0.0 1.0 %fusion.1 = (bf16[4,4,1536]{2,1,0:T(4,128)(2,1)S(1)}, bf16[4,4,1536]{2,1,0:T(4,128)(2,1)S(1)}) fusion(bf16[4,512,1536]{2,1,0:T(8,128)(2,1)} %x_ref.3), kind=kLoop, calls=%fused_computation.17 | loop fusion | bytes 196608 | tf_op jit(solution)/shard_map/slice | solution.py:244
  1.0 1.9 %collective-permute-start = (bf16[4,4,1536]{2,1,0:T(4,128)(2,1)S(1)}, bf16[4,4,1536]{2,1,0:T(4,128)(2,1)S(1)}, u32[]{:S(2)}, u32[]{:S(2)}) collective-permute-start(bf16[4,4,1536]{2,1,0:T(4,128)(2,1)S(1)} %get-tuple-element.47), channel_id=1, source_target_pairs={{0,1},{1,2},{2,3},{3,4},{4,5},{5,6},{6,7},{7,8},{8,9},{9,10},{10,1... | collective-permute-start | bytes 147464 | tf_op jit(solution)/shard_map/ppermute | solution.py:244
  2.9 3.6 %collective-permute-start.1 = (bf16[4,4,1536]{2,1,0:T(4,128)(2,1)S(1)}, bf16[4,4,1536]{2,1,0:T(4,128)(2,1)S(1)}, u32[]{:S(2)}, u32[]{:S(2)}) collective-permute-start(bf16[4,4,1536]{2,1,0:T(4,128)(2,1)S(1)} %get-tuple-element.48), channel_id=1, source_target_pairs={{1,0},{2,1},{3,2},{4,3},{5,4},{6,5},{7,6},{8,7},{9,8},{10,9},{11,1... | collective-permute-start | bytes 147464 | tf_op jit(solution)/shard_map/ppermute | solution.py:245
  6.6 3.3 %prep.1 = bf16[4,240,384]{2,1,0:T(8,128)(2,1)} custom-call(s32[1]{0:T(128)} %bitcast.4.core, bf16[2,480,1536]{2,1,0:T(8,128)(2,1)} %bitcast.21), custom_call_target="tpu_custom_call" | custom-call | bytes 1474560 | tf_op jit(solution)/shard_map/prep/pallas_call | solution.py:133
  9.9 4.3 %all-to-all-start = ((bf16[4,240,384]{2,1,0:T(8,128)(2,1)}), bf16[4,240,384]{2,1,0:T(8,128)(2,1)S(1)}, u32[]{:S(2)}, u32[]{:S(2)}) async-start(bf16[4,240,384]{2,1,0:T(8,128)(2,1)} %prep.1), calls=%async_computation | async-start | bytes 1474560 | tf_op jit(solution)/shard_map/all_to_all | solution.py:251
  14.3 7.2 %first.3 = (bf16[208,512]{1,0:T(8,128)(2,1)S(1)}, f32[17,128]{1,0:T(8,128)S(1)}) custom-call(s32[4]{0:T(128)S(1)} %pad_add_fusion.info, bf16[4,512,1536]{2,1,0:T(8,128)(2,1)} %x_ref.3, bf16[32,1536]{1,0:T(8,128)(2,1)S(1)} %maximum_bitcast_fusion.halo_ref, f32[1,1536]{1,0:T(1,128)S(1)} %get-tuple-element.50.gain_ref, bf16[2,480,1536]{2,1,0:T(8,128)(2,1)} %bitcast.22), custom_call_target="tpu_custom_call" | custom-call | flops 1509949440 | bytes 3145728 | tf_op jit(solution)/shard_map/first/pallas_call | solution.py:102
  21.5 5.6 %all-to-all-done.refs_10_.pa_ref.ma_ref.wa_ref = bf16[4,240,384]{2,1,0:T(8,128)(2,1)S(1)} async-done(((bf16[4,240,384]{2,1,0:T(8,128)(2,1)}), bf16[4,240,384]{2,1,0:T(8,128)(2,1)S(1)}, u32[]{:S(2)}, u32[]{:S(2)}) %all-to-all-start) | async-done | bytes 737312 | tf_op jit(solution)/shard_map/all_to_all | solution.py:251
  27.1 0.1 collective-permute-start.8
  27.3 7.1 %first.2 = (bf16[208,512]{1,0:T(8,128)(2,1)S(1)}, f32[17,128]{1,0:T(8,128)S(1)}) custom-call(s32[4]{0:T(128)S(1)} %pad_add_fusion.info, bf16[4,512,1536]{2,1,0:T(8,128)(2,1)} %x_ref.3, bf16[32,1536]{1,0:T(8,128)(2,1)S(1)} %maximum_bitcast_fusion.halo_ref, f32[1,1536]{1,0:T(1,128)S(1)} %get-tuple-element.50.gain_ref, bf16[2,480,1536]{2,1,0:T(8,128)(2,1)} %bitcast.23), custom_call_target="tpu_custom_call" | custom-call | flops 1509949440 | bytes 3145728 | tf_op jit(solution)/shard_map/first/pallas_call | solution.py:102
  34.4 1.7 %collective-permute-start.2 = (bf16[208,512]{1,0:T(8,128)(2,1)S(1)}, bf16[208,512]{1,0:T(8,128)(2,1)S(1)}, u32[]{:S(2)}, u32[]{:S(2)}) collective-permute-start(bf16[208,512]{1,0:T(8,128)(2,1)S(1)} %get-tuple-element.27.refs_0_.a0_ref), channel_id=1, source_target_pairs={{0,16},{16,32},{32,48},{48,0},{1,17},{17,33},{33,49},{49,1},{2,18}... | collective-permute-start | bytes 638984 | tf_op jit(solution)/shard_map/ppermute | solution.py:233
  36.1 1.7 %collective-permute-start.5 = (bf16[208,512]{1,0:T(8,128)(2,1)S(1)}, bf16[208,512]{1,0:T(8,128)(2,1)S(1)}, u32[]{:S(2)}, u32[]{:S(2)}) collective-permute-start(bf16[208,512]{1,0:T(8,128)(2,1)S(1)} %get-tuple-element.31.refs_1_.a1_ref), channel_id=1, source_target_pairs={{0,48},{16,0},{32,16},{48,32},{1,49},{17,1},{33,17},{49,33},{2,50}... | collective-permute-start | bytes 638984 | tf_op jit(solution)/shard_map/ppermute | solution.py:233
  37.8 0.1 stack.55
  37.8 1.8 %collective-permute-start.4 = (bf16[208,512]{1,0:T(8,128)(2,1)S(1)}, bf16[208,512]{1,0:T(8,128)(2,1)S(1)}, u32[]{:S(2)}, u32[]{:S(2)}) collective-permute-start(bf16[208,512]{1,0:T(8,128)(2,1)S(1)} %get-tuple-element.27.refs_0_.a0_ref), channel_id=1, source_target_pairs={{0,48},{16,0},{32,16},{48,32},{1,49},{17,1},{33,17},{49,33},{2,50}... | collective-permute-start | bytes 638984 | tf_op jit(solution)/shard_map/ppermute | solution.py:233
  39.6 3.7 %collective-permute-done.2.refs_2_ = bf16[208,512]{1,0:T(8,128)(2,1)S(1)} collective-permute-done((bf16[208,512]{1,0:T(8,128)(2,1)S(1)}, bf16[208,512]{1,0:T(8,128)(2,1)S(1)}, u32[]{:S(2)}, u32[]{:S(2)}) %collective-permute-start.2) | collective-permute-done | bytes 213024 | tf_op jit(solution)/shard_map/ppermute | solution.py:233
  43.3 0.3 collective-permute-start.6
  43.6 1.6 %collective-permute-start.3 = (bf16[208,512]{1,0:T(8,128)(2,1)S(1)}, bf16[208,512]{1,0:T(8,128)(2,1)S(1)}, u32[]{:S(2)}, u32[]{:S(2)}) collective-permute-start(bf16[208,512]{1,0:T(8,128)(2,1)S(1)} %get-tuple-element.31.refs_1_.a1_ref), channel_id=1, source_target_pairs={{0,16},{16,32},{32,48},{48,0},{1,17},{17,33},{33,49},{49,1},{2,18}... | collective-permute-start | bytes 638984 | tf_op jit(solution)/shard_map/ppermute | solution.py:233
  45.2 0.7 broadcast_in_dim.6
  45.9 4.8 %all-to-all-start.1 = ((f32[16,17,128]{2,1,0:T(8,128)}), f32[16,17,128]{2,1,0:T(8,128)S(1)}, u32[]{:S(2)}, u32[]{:S(2)}) async-start(f32[16,17,128]{2,1,0:T(8,128)} %broadcast_in_dim.6), calls=%async_computation.1 | async-start | bytes 393216 | tf_op jit(solution)/shard_map/all_to_all | solution.py:261
  50.7 3.4 %collective-permute-start.7 = (bf16[208,512]{1,0:T(8,128)(2,1)S(1)}, bf16[208,512]{1,0:T(8,128)(2,1)S(1)}, u32[]{:S(2)}, u32[]{:S(2)}) collective-permute-start(bf16[208,512]{1,0:T(8,128)(2,1)S(1)} %collective-permute-done.5.refs_5_), channel_id=1, source_target_pairs={{0,48},{16,0},{32,16},{48,32},{1,49},{17,1},{33,17},{49,33},{2,50}... | collective-permute-start | bytes 638984 | tf_op jit(solution)/shard_map/ppermute | solution.py:233
  54.3 4.6 %all-to-all-done.1.refs_8_ = f32[16,17,128]{2,1,0:T(8,128)S(1)} async-done(((f32[16,17,128]{2,1,0:T(8,128)}), f32[16,17,128]{2,1,0:T(8,128)S(1)}, u32[]{:S(2)}, u32[]{:S(2)}) %all-to-all-start.1) | async-done | bytes 139296 | tf_op jit(solution)/shard_map/all_to_all | solution.py:261
  58.8 0.1 collective-permute-done.7.refs_7_
  58.9 0.1 broadcast_in_dim.15.refs_9_
  59.1 3.9 %far.1 = (bf16[384,2176]{1,0:T(8,128)(2,1)S(1)}, bf16[192,512]{1,0:T(8,128)(2,1)S(1)}, bf16[192,512]{1,0:T(8,128)(2,1)S(1)}) custom-call(s32[9]{0:T(128)S(1)} %pad_add_fusion.1.order, bf16[208,512]{1,0:T(8,128)(2,1)S(1)} %get-tuple-element.27.refs_0_.a0_ref, bf16[208,512]{1,0:T(8,128)(2,1)S(1)} %get-tuple-element.31.refs_1_.a1_ref, ...), custom_call_target="tpu_custom_call" | custom-call | flops 802160640 | bytes 3342336 | tf_op jit(solution)/shard_map/far/pallas_call | solution.py:199
  62.9 2.8 %collective-permute-start.10 = (bf16[192,512]{1,0:T(8,128)(2,1)S(1)}, bf16[192,512]{1,0:T(8,128)(2,1)S(1)}, u32[]{:S(2)}, u32[]{:S(2)}) collective-permute-start(bf16[192,512]{1,0:T(8,128)(2,1)S(1)} %get-tuple-element.39), channel_id=1, source_target_pairs={{0,192},{64,0},{128,64},{192,128},{1,193},{65,1},{129,65},{193,129... | collective-permute-start | bytes 589832 | tf_op jit(solution)/shard_map/ppermute | solution.py:233
  65.7 3.8 %near.1 = (f32[384,512]{1,0:T(8,128)S(1)}, f32[384,512]{1,0:T(8,128)S(1)}) custom-call(s32[9]{0:T(128)S(1)} %pad_add_fusion.1.order, bf16[384,2176]{1,0:T(8,128)(2,1)S(1)} %get-tuple-element.44.h_ref, bf16[4,240,384]{2,1,0:T(8,128)(2,1)S(1)} %all-to-all-done.refs_10_.pa_ref.ma_ref.wa_ref, ...), custom_call_target="tpu_custom_call" | custom-call | flops 1604321280 | bytes 3342336 | tf_op jit(solution)/shard_map/near/pallas_call | solution.py:199
  69.5 3.0 %collective-permute-done.9 = bf16[192,512]{1,0:T(8,128)(2,1)S(1)} collective-permute-done((bf16[192,512]{1,0:T(8,128)(2,1)S(1)}, bf16[192,512]{1,0:T(8,128)(2,1)S(1)}, u32[]{:S(2)}, u32[]{:S(2)}) %collective-permute-start.9) | collective-permute-done | bytes 196640 | tf_op jit(solution)/shard_map/ppermute | solution.py:233
  72.6 0.1 add_convert_fusion.1
  72.9 3.2 %collective-permute-start.12 = (bf16[384,512]{1,0:T(8,128)(2,1)S(1)}, bf16[384,512]{1,0:T(8,128)(2,1)S(1)}, u32[]{:S(2)}, u32[]{:S(2)}) collective-permute-start(bf16[384,512]{1,0:T(8,128)(2,1)S(1)} %pad_maximum_fusion.2), channel_id=1, source_target_pairs={{0,192},{64,0},{128,64},{192,128},{1,193},{65,1},{129,65},{193,129... | collective-permute-start | bytes 1179656 | tf_op jit(solution)/shard_map/ppermute | solution.py:233
  76.2 2.3 %own.1 = f32[384,512]{1,0:T(8,128)S(1)} custom-call(s32[9]{0:T(128)S(1)} %pad_add_fusion.1.order, bf16[384,2176]{1,0:T(8,128)(2,1)S(1)} %get-tuple-element.44.h_ref, bf16[4,240,384]{2,1,0:T(8,128)(2,1)S(1)} %all-to-all-done.refs_10_.pa_ref.ma_ref.wa_ref, bf16[4,240,384]{2,1,0:T(8,128)(2,1)S(1)} %collective-permute-done.8.refs_11_.pb_ref.mb_ref.wb_ref, ...), custom_call_target="tpu_custom_call" | custom-call | flops 802160640 | bytes 3342336 | tf_op jit(solution)/shard_map/own/pallas_call | solution.py:199
  78.5 3.9 %collective-permute-done.11 = bf16[384,512]{1,0:T(8,128)(2,1)S(1)} collective-permute-done((bf16[384,512]{1,0:T(8,128)(2,1)S(1)}, bf16[384,512]{1,0:T(8,128)(2,1)S(1)}, u32[]{:S(2)}, u32[]{:S(2)}) %collective-permute-start.11) | collective-permute-done | bytes 393248 | tf_op jit(solution)/shard_map/ppermute | solution.py:233
  82.4 0.2 add_convert_fusion
  82.6 0.9 %pad_maximum_fusion = bf16[768,512]{1,0:T(8,128)(2,1)} fusion(bf16[384,512]{1,0:T(8,128)(2,1)S(1)} %add_convert_fusion, bf16[192,512]{1,0:T(8,128)(2,1)S(1)} %slice.37, bf16[192,512]{1,0:T(8,128)(2,1)S(1)} %slice.36), kind=kLoop, calls=%fused_computation | loop fusion | flops 2359296 | bytes 1572864 | tf_op jit(solution)/shard_map/concatenate | solution.py:303
  (27 shorter events, 0.5 us)
Async XLA Ops:
  1.0 13.3 %collective-permute-start = (bf16[4,4,1536]{2,1,0:T(4,128)(2,1)S(1)}, bf16[4,4,1536]{2,1,0:T(4,128)(2,1)S(1)}, u32[]{:S(2)}, u32[]{:S(2)}) collective-permute-start(bf16[4,4,1536]{2,1,0:T(4,128)(2,1)S(1)} %get-tuple-element.47), channel_id=1, source_target_pairs={{0,1},{1,2},{2,3},{3,4},{4,5},{5,6},{6,7},{7,8},{8,9},{9,10},{10,1... | collective-permute-start | bytes 147464 | tf_op jit(solution)/shard_map/ppermute | solution.py:244
  2.9 11.4 %collective-permute-start.1 = (bf16[4,4,1536]{2,1,0:T(4,128)(2,1)S(1)}, bf16[4,4,1536]{2,1,0:T(4,128)(2,1)S(1)}, u32[]{:S(2)}, u32[]{:S(2)}) collective-permute-start(bf16[4,4,1536]{2,1,0:T(4,128)(2,1)S(1)} %get-tuple-element.48), channel_id=1, source_target_pairs={{1,0},{2,1},{3,2},{4,3},{5,4},{6,5},{7,6},{8,7},{9,8},{10,9},{11,1... | collective-permute-start | bytes 147464 | tf_op jit(solution)/shard_map/ppermute | solution.py:245
  6.6 7.6 %copy-start = (f32[2,1536]{1,0:T(2,128)S(1)}, f32[2,1536]{1,0:T(2,128)}, u32[]{:S(2)}) copy-start(f32[2,1536]{1,0:T(2,128)} %param.5) | copy-start | bytes 36868
  9.9 17.2 %all-to-all-start = ((bf16[4,240,384]{2,1,0:T(8,128)(2,1)}), bf16[4,240,384]{2,1,0:T(8,128)(2,1)S(1)}, u32[]{:S(2)}, u32[]{:S(2)}) async-start(bf16[4,240,384]{2,1,0:T(8,128)(2,1)} %prep.1), calls=%async_computation | async-start | bytes 1474560 | tf_op jit(solution)/shard_map/all_to_all | solution.py:251
  27.1 31.8 %collective-permute-start.8 = (bf16[4,240,384]{2,1,0:T(8,128)(2,1)S(1)}, bf16[4,240,384]{2,1,0:T(8,128)(2,1)S(1)}, u32[]{:S(2)}, u32[]{:S(2)}) collective-permute-start(bf16[4,240,384]{2,1,0:T(8,128)(2,1)S(1)} %all-to-all-done.refs_10_.pa_ref.ma_ref.wa_ref), channel_id=1, source_target_pairs={{0,1},{1,0},{2,3},{3,2},{4,5},{5,4},{6,7},{7,6},{8,9},{9,8},{10,11... | collective-permute-start | bytes 2211848 | tf_op jit(solution)/shard_map/ppermute | solution.py:262
  34.4 8.9 %collective-permute-start.2 = (bf16[208,512]{1,0:T(8,128)(2,1)S(1)}, bf16[208,512]{1,0:T(8,128)(2,1)S(1)}, u32[]{:S(2)}, u32[]{:S(2)}) collective-permute-start(bf16[208,512]{1,0:T(8,128)(2,1)S(1)} %get-tuple-element.27.refs_0_.a0_ref), channel_id=1, source_target_pairs={{0,16},{16,32},{32,48},{48,0},{1,17},{17,33},{33,49},{49,1},{2,18}... | collective-permute-start | bytes 638984 | tf_op jit(solution)/shard_map/ppermute | solution.py:233
  36.1 14.6 %collective-permute-start.5 = (bf16[208,512]{1,0:T(8,128)(2,1)S(1)}, bf16[208,512]{1,0:T(8,128)(2,1)S(1)}, u32[]{:S(2)}, u32[]{:S(2)}) collective-permute-start(bf16[208,512]{1,0:T(8,128)(2,1)S(1)} %get-tuple-element.31.refs_1_.a1_ref), channel_id=1, source_target_pairs={{0,48},{16,0},{32,16},{48,32},{1,49},{17,1},{33,17},{49,33},{2,50}... | collective-permute-start | bytes 638984 | tf_op jit(solution)/shard_map/ppermute | solution.py:233
  37.8 16.4 %collective-permute-start.4 = (bf16[208,512]{1,0:T(8,128)(2,1)S(1)}, bf16[208,512]{1,0:T(8,128)(2,1)S(1)}, u32[]{:S(2)}, u32[]{:S(2)}) collective-permute-start(bf16[208,512]{1,0:T(8,128)(2,1)S(1)} %get-tuple-element.27.refs_0_.a0_ref), channel_id=1, source_target_pairs={{0,48},{16,0},{32,16},{48,32},{1,49},{17,1},{33,17},{49,33},{2,50}... | collective-permute-start | bytes 638984 | tf_op jit(solution)/shard_map/ppermute | solution.py:233
  43.3 10.9 %collective-permute-start.6 = (bf16[208,512]{1,0:T(8,128)(2,1)S(1)}, bf16[208,512]{1,0:T(8,128)(2,1)S(1)}, u32[]{:S(2)}, u32[]{:S(2)}) collective-permute-start(bf16[208,512]{1,0:T(8,128)(2,1)S(1)} %collective-permute-done.2.refs_2_), channel_id=1, source_target_pairs={{0,16},{16,32},{32,48},{48,0},{1,17},{17,33},{33,49},{49,1},{2,18}... | collective-permute-start | bytes 638984 | tf_op jit(solution)/shard_map/ppermute | solution.py:233
  43.6 15.2 %collective-permute-start.3 = (bf16[208,512]{1,0:T(8,128)(2,1)S(1)}, bf16[208,512]{1,0:T(8,128)(2,1)S(1)}, u32[]{:S(2)}, u32[]{:S(2)}) collective-permute-start(bf16[208,512]{1,0:T(8,128)(2,1)S(1)} %get-tuple-element.31.refs_1_.a1_ref), channel_id=1, source_target_pairs={{0,16},{16,32},{32,48},{48,0},{1,17},{17,33},{33,49},{49,1},{2,18}... | collective-permute-start | bytes 638984 | tf_op jit(solution)/shard_map/ppermute | solution.py:233
  45.9 12.9 %all-to-all-start.1 = ((f32[16,17,128]{2,1,0:T(8,128)}), f32[16,17,128]{2,1,0:T(8,128)S(1)}, u32[]{:S(2)}, u32[]{:S(2)}) async-start(f32[16,17,128]{2,1,0:T(8,128)} %broadcast_in_dim.6), calls=%async_computation.1 | async-start | bytes 393216 | tf_op jit(solution)/shard_map/all_to_all | solution.py:261
  50.7 8.2 %collective-permute-start.7 = (bf16[208,512]{1,0:T(8,128)(2,1)S(1)}, bf16[208,512]{1,0:T(8,128)(2,1)S(1)}, u32[]{:S(2)}, u32[]{:S(2)}) collective-permute-start(bf16[208,512]{1,0:T(8,128)(2,1)S(1)} %collective-permute-done.5.refs_5_), channel_id=1, source_target_pairs={{0,48},{16,0},{32,16},{48,32},{1,49},{17,1},{33,17},{49,33},{2,50}... | collective-permute-start | bytes 638984 | tf_op jit(solution)/shard_map/ppermute | solution.py:233
  62.9 6.6 %collective-permute-start.10 = (bf16[192,512]{1,0:T(8,128)(2,1)S(1)}, bf16[192,512]{1,0:T(8,128)(2,1)S(1)}, u32[]{:S(2)}, u32[]{:S(2)}) collective-permute-start(bf16[192,512]{1,0:T(8,128)(2,1)S(1)} %get-tuple-element.39), channel_id=1, source_target_pairs={{0,192},{64,0},{128,64},{192,128},{1,193},{65,1},{129,65},{193,129... | collective-permute-start | bytes 589832 | tf_op jit(solution)/shard_map/ppermute | solution.py:233
  65.7 6.9 %collective-permute-start.9 = (bf16[192,512]{1,0:T(8,128)(2,1)S(1)}, bf16[192,512]{1,0:T(8,128)(2,1)S(1)}, u32[]{:S(2)}, u32[]{:S(2)}) collective-permute-start(bf16[192,512]{1,0:T(8,128)(2,1)S(1)} %get-tuple-element.38), channel_id=1, source_target_pairs={{0,64},{64,128},{128,192},{192,0},{1,65},{65,129},{129,193},{193,1... | collective-permute-start | bytes 589832 | tf_op jit(solution)/shard_map/ppermute | solution.py:233
  72.8 9.6 %collective-permute-start.11 = (bf16[384,512]{1,0:T(8,128)(2,1)S(1)}, bf16[384,512]{1,0:T(8,128)(2,1)S(1)}, u32[]{:S(2)}, u32[]{:S(2)}) collective-permute-start(bf16[384,512]{1,0:T(8,128)(2,1)S(1)} %pad_maximum_fusion.1), channel_id=1, source_target_pairs={{0,64},{64,128},{128,192},{192,0},{1,65},{65,129},{129,193},{193,1... | collective-permute-start | bytes 1179656 | tf_op jit(solution)/shard_map/ppermute | solution.py:233
  72.9 9.5 %collective-permute-start.12 = (bf16[384,512]{1,0:T(8,128)(2,1)S(1)}, bf16[384,512]{1,0:T(8,128)(2,1)S(1)}, u32[]{:S(2)}, u32[]{:S(2)}) collective-permute-start(bf16[384,512]{1,0:T(8,128)(2,1)S(1)} %pad_maximum_fusion.2), channel_id=1, source_target_pairs={{0,192},{64,0},{128,64},{192,128},{1,193},{65,1},{129,65},{193,129... | collective-permute-start | bytes 1179656 | tf_op jit(solution)/shard_map/ppermute | solution.py:233

commit v6 on v4

--- a/solution.py
+++ b/solution.py
@@ -13,6 +13,7 @@
 M = 4
 B = 400
 HB = 192
+L = 17
 Q = 384
 HR = 240
 N = M * S + 128
@@ -36,7 +37,7 @@
     return total
 
 
-def first_kernel(info, x_ref, halo_ref, gain_ref, w_ref, o_ref, sq_ref, h_ref, y_ref, hy_ref, hr_ref):
+def first_kernel(info, x_ref, up_ref, down_ref, gain_ref, w_ref, o_ref, sq_ref, h_ref, y_ref, hy_ref, hr_ref):
     i = pl.program_id(0)
     start = pl.multiple_of(info[0] * 128, 128)
     off = info[1]
@@ -51,14 +52,15 @@
 
     @pl.when(i == 0)
     def _():
-        hh = hidden(halo_ref[...])
-        hy_ref[...] = jnp.zeros_like(hy_ref)
         hr_ref[...] = jnp.zeros_like(hr_ref)
         sq_ref[...] = jnp.zeros_like(sq_ref)
-        hy = lax.dot_general(w_ref[...], hh, NT, preferred_element_type=jnp.float32)
-        hx = lax.dot_general(pick, halo_ref[:, pl.ds(start, 256)], NT, preferred_element_type=jnp.float32)
-        hy_ref[:, 0:32] = hy
-        hy_ref[2 * T : 3 * T, 0:32] += hx
+        hy_ref[...] = jnp.zeros_like(hy_ref)
+        for n, ref in enumerate((up_ref, down_ref)):
+            at = slice(32 * n, 32 * n + 32)
+            hy_ref[:, at] = lax.dot_general(w_ref[...], hidden(ref[...]), NT, preferred_element_type=jnp.float32)
+            hy_ref[2 * T : 3 * T, at] += lax.dot_general(
+                pick, ref[:, pl.ds(start, 256)], NT, preferred_element_type=jnp.float32
+            )
 
     window = pl.ds(start, 256)
     for c in range(2):
@@ -70,14 +72,15 @@
         y_ref[2 * T : 3 * T, to] += lax.dot_general(
             pick, x_ref[0, at, window], NT, preferred_element_type=jnp.float32
         )
-    y_ref[:, 0:128] = pltpu.roll(hy_ref[...], lax.rem(252 - 8 * i, 128), 1)
-    y_ref[:, 128 + S :] = pltpu.roll(hy_ref[...], lax.rem(252 - 8 * i, 128), 1)
+    y_ref[:, 0:128] = pltpu.roll(hy_ref[...], 120 - 8 * i, 1)
+    y_ref[:, 128 + S :] = pltpu.roll(hy_ref[...], 96 - 8 * i, 1)
     out = combine(y_ref[...])
     out = out.astype(jnp.bfloat16)
     o_ref[pl.ds(pl.multiple_of(i * T, 16), T), :] = out[:, 128 : 128 + S]
     out = out.astype(jnp.float32)
     squares = jnp.sum(out * out, axis=0, keepdims=True)
-    sq_ref[:, pl.ds(pl.multiple_of(i * S, 128), S)] = squares[:, 128 : 128 + S]
+    for q in range(4):
+        sq_ref[pl.ds(4 * i + q, 1), :] = squares[:, 128 + 128 * q : 256 + 128 * q]
     pad = jnp.zeros((32, 128), jnp.float32)
     left = jnp.concatenate([out[:, 0:128], pad], 0).T
     right = jnp.concatenate([out[:, 128 + S :], pad], 0).T
@@ -87,7 +90,7 @@
     turn = lax.rem(4 * i + 2, 128)
     edge = jnp.where((lane == 0) | (lane == 1), pltpu.roll(squares[:, 0:128], turn, 1) * keep_left, 0.0)
     edge += jnp.where((lane == 2) | (lane == 3), pltpu.roll(squares[:, 128 + S :], turn, 1) * keep_right, 0.0)
-    sq_ref[:, M * S :] += edge
+    sq_ref[L - 1 : L, :] += edge
     line = jnp.concatenate(
         [left[126:127] * keep_left, left[127:128] * keep_left, right[0:1] * keep_right, right[1:2] * keep_right], 1
     )
@@ -95,7 +98,8 @@
     o_ref[M * T :, :] = hr_ref[...].astype(jnp.bfloat16)
 
 
-def first(x, halo, gain, w, info):
+def first(x, up, down, gain, w, info):
+    outs = [jax.ShapeDtypeStruct((B, S), jnp.bfloat16), jax.ShapeDtypeStruct((L, 128), jnp.float32)]
     return pl.pallas_call(
         first_kernel,
         grid_spec=pltpu.PrefetchScalarGridSpec(
@@ -104,10 +108,11 @@
             in_specs=[
                 pl.BlockSpec((1, S, C), lambda i, info: (i, 0, 0)),
                 whole(32, C),
+                whole(32, C),
                 whole(1, C),
                 pl.BlockSpec((None, R, C), lambda i, info: (0, 0, 0)),
             ],
-            out_specs=[whole(B, S), whole(1, N)],
+            out_specs=[whole(*o.shape) for o in outs],
             scratch_shapes=[
                 pltpu.VMEM((S, C), jnp.bfloat16),
                 pltpu.VMEM((R, S + 256), jnp.float32),
@@ -115,35 +120,38 @@
                 pltpu.VMEM((16, S), jnp.float32),
             ],
         ),
-        out_shape=[jax.ShapeDtypeStruct((B, S), jnp.bfloat16), jax.ShapeDtypeStruct((1, N), jnp.float32)],
+        out_shape=outs,
         compiler_params=pltpu.CompilerParams(dimension_semantics=("arbitrary",), vmem_limit_bytes=32 << 20),
         cost_estimate=pl.CostEstimate(flops=2 * M * S * R * C, bytes_accessed=2 * M * S * C, transcendentals=M * S * C),
         name="first",
-    )(info, x, halo, gain, w)
-
-
-def prep_kernel(core, w_ref, o_ref):
-    for r in range(0, HR, 80):
-        v = w_ref[r : r + 80, :].astype(jnp.float32)
-        for b in range(4):
-            cols = [v[:, (a * 4 + b) * T : (a * 4 + b) * T + T] for a in range(4)]
-            o_ref[b, r : r + 80, :] = jnp.concatenate(cols, 1).astype(jnp.bfloat16)
-
-
-def prep(core, w):
+    )(info, x, up, down, gain, w)
+
+
+def prep_kernel(core, w_ref, top_ref, end_ref, o_ref, down_ref, up_ref):
+    for b in range(4):
+        o_ref[b] = w_ref[:, b * Q : b * Q + Q]
+        down_ref[b * 8 : b * 8 + 8, :] = top_ref[b]
+        up_ref[b * 8 : b * 8 + 8, :] = end_ref[b]
+
+
+def prep(core, w, x):
+    outs = [jax.ShapeDtypeStruct((4, HR, Q), jnp.bfloat16)] + [jax.ShapeDtypeStruct((32, C), jnp.bfloat16)] * 2
     return pl.pallas_call(
         prep_kernel,
         grid_spec=pltpu.PrefetchScalarGridSpec(
             num_scalar_prefetch=1,
             grid=(1,),
-            in_specs=[pl.BlockSpec((None, HR, C), lambda i, core: (1, core[0], 0))],
-            out_specs=whole(4, HR, Q),
+            in_specs=[
+                pl.BlockSpec((None, HR, C), lambda i, core: (1, core[0], 0)),
+                pl.BlockSpec((M, 8, C), lambda i, core: (0, 0, 0)),
+                pl.BlockSpec((M, 8, C), lambda i, core: (0, S // 8 - 1, 0)),
+            ],
+            out_specs=[whole(*o.shape) for o in outs],
         ),
-        out_shape=jax.ShapeDtypeStruct((4, HR, Q), jnp.bfloat16),
-        compiler_params=pltpu.CompilerParams(vmem_limit_bytes=16 << 20),
+        out_shape=outs,
         cost_estimate=pl.CostEstimate(flops=0, bytes_accessed=4 * HR * C, transcendentals=0),
         name="prep",
-    )(core, w)
+    )(core, w, x, x)
 
 
 def join(core, pairs, v_ref):
@@ -159,11 +167,19 @@
     return combine(wide)[:, 128 : 128 + S]
 
 
-def far_kernel(order, a0, a1, a2, a3, a4, sq_ref, gain_ref, wa_ref, wb_ref, h_ref, far0_ref, far1_ref, y_ref, v_ref, s_ref):
+def far_kernel(order, *refs):
+    got, (sq_ref, gain_ref, wa_ref, wb_ref, h_ref, far0_ref, far1_ref, y_ref, v_ref, s_ref) = refs[:5], refs[5:]
     join(order[8], [(wa_ref, wb_ref)], v_ref)
-    s_ref[...] = jnp.broadcast_to(lax.rsqrt(sq_ref[...] * (1.0 / C) + 1e-06), s_ref.shape)
-
-    def put(piece, parts, lines):
+    total = sq_ref[...]
+    scale = lax.rsqrt(total * (1.0 / C) + 1e-06)
+    for r in range(L):
+        s_ref[:, 128 * r : 128 * r + 128] = jnp.broadcast_to(scale[r : r + 1, :], (8, 128))
+
+    for piece in range(4):
+        if piece < 3:
+            parts, lines = [(got[piece], j * T) for j in range(M)], got[piece][M * T :, :]
+        else:
+            parts, lines = [(got[3 + j // 2], j % 2 * T) for j in range(M)], got[4][HB:, :]
         dest = pl.multiple_of(order[piece] * T, 16)
         gain = gain_ref[pl.ds(dest, T), :]
         lines = lines.astype(jnp.float32)
@@ -180,9 +196,6 @@
                 v = ref[row : row + T, 128 * q : 128 * q + 128].astype(jnp.float32)
                 h_ref[pl.ds(dest, T), lane] = gelu(v * s_ref[0:1, lane] * gain).astype(jnp.bfloat16)
 
-    for piece, ref in enumerate((a0, a1, a2)):
-        put(piece, [(ref, j * T) for j in range(M)], ref[M * T :, :])
-    put(3, [(a3, 0), (a3, T), (a4, 0), (a4, T)], a4[HB:, :])
     y_ref[...] = jnp.dot(v_ref[...], h_ref[...], preferred_element_type=jnp.float32)
     for j in range(2):
         far0_ref[j * T : j * T + T, :] = taps(y_ref, 0, j).astype(jnp.bfloat16)
@@ -238,45 +251,44 @@
     held = pltpu.with_memory_space_constraint(inputs, pltpu.HBM)
     up = [(i, i + 1) for i in range(15)]
     down = [(i + 1, i) for i in range(15)]
-    before = lax.ppermute(inputs[:, S - 4 :], ("z", "core"), up)
-    after = lax.ppermute(inputs[:, :4], ("z", "core"), down)
-    halo = jnp.concatenate([before, after], 1).reshape(32, C)
-    send = prep(core.reshape(1).astype(jnp.int32), w)
+    send, top, end = prep(core.reshape(1).astype(jnp.int32), w, held)
+    up = lax.ppermute(end, ("z", "core"), up)
+    down = lax.ppermute(top, ("z", "core"), down)
     block = jnp.minimum(sec * T // 128, 10)
     info = jnp.stack([block, sec * T - block * 128, seq, 15 - seq]).astype(jnp.int32)
     info, send = lax.optimization_barrier((info, send))
-    mine = lax.all_to_all(send, "y", 0, 0, tiled=True)
-    gain = lax.dynamic_index_in_dim(gains[1].reshape(4, 4, T), y, 1, False).reshape(Q, 1)
+    mine = lax.all_to_all(send, "x", 0, 0, tiled=True)
+    gain = lax.dynamic_index_in_dim(gains[1].reshape(4, Q), x, 0, False).reshape(Q, 1)
     gain = jnp.broadcast_to(gain, (Q, 128))
-    block, sq = first(held, halo, gains[0:1], w, info)
+    block, sq = first(held, up, down, gains[0:1], w, info)
     block, sq, mine = lax.optimization_barrier((block, sq, mine))
-    other = lax.ppermute(mine, "core", [(0, 1), (1, 0)])
-    below, above = shift(block, "x", 1), shift(block, "x", -1)
-    got = [block, below, above, shift(below[:HB], "x", 1), shift(above[HB:], "x", -1)]
-    for axis in ("y", "x"):
-        sq = sq + lax.ppermute(sq, axis, [(i, i ^ 1) for i in range(4)])
-        sq = sq + lax.ppermute(sq, axis, [(i, i ^ 2) for i in range(4)])
-    rel = [x, x + 3, x + 1, x + 2, y, y + 3, y + 1, y + 2]
+    below, above = shift(block, "y", 1), shift(block, "y", -1)
+    sq = sq + shift(sq, "x", 1) + shift(sq, "x", -1) + shift(sq, "x", 2)
+    sq = sq + shift(sq, "y", 1) + shift(sq, "y", -1) + shift(sq, "y", 2)
+    swap, below, above, sq = lax.optimization_barrier((mine, below, above, sq))
+    other = lax.ppermute(swap, "core", [(0, 1), (1, 0)])
+    got = [block, below, above, shift(below[:HB], "y", 1), shift(above[HB:], "y", -1)]
+    rel = [y, y + 3, y + 1, y + 2, x, x + 3, x + 1, x + 2]
     order = jnp.concatenate([jnp.stack(rel) % 4, core.reshape(1)]).astype(jnp.int32)
     half = jax.ShapeDtypeStruct((HB, S), jnp.bfloat16)
     h, far0, far1 = stage(
         far_kernel,
         order,
         (*got, sq, gain, mine, other),
-        [whole(B, S)] * 3 + [whole(HB, S), whole(B - HB, S), whole(1, N), whole(Q, 128)] + picked(7),
+        [whole(B, S)] * 3 + [whole(HB, S), whole(B - HB, S), whole(L, 128), whole(Q, 128)] + picked(7),
         [jax.ShapeDtypeStruct((Q, N), jnp.bfloat16), half, half],
         [pltpu.VMEM((8, N), jnp.float32)],
         1,
         "far",
     )
-    r0, r1 = shift(far0, "y", 1), shift(far1, "y", -1)
-    one = jax.ShapeDtypeStruct((M * T, S), jnp.float32)
+    r0, r1 = shift(far0, "x", 1), shift(far1, "x", -1)
+    wide = jax.ShapeDtypeStruct((M * T, S), jnp.float32)
     plus, minus = stage(
         near_kernel,
         order,
         (h, mine, other, mine, other),
         [whole(Q, N)] + picked(6) + picked(5),
-        [one, one],
+        [wide, wide],
         [],
         2,
         "near",
@@ -290,12 +302,12 @@
         order,
         (h, mine, other, block),
         [whole(Q, N)] + picked(4) + [whole(B, S)],
-        [one],
+        [wide],
         [],
         1,
         "own",
     )
-    total = base + shift(plus, "y", 1).astype(jnp.float32) + shift(minus, "y", -1).astype(jnp.float32)
+    total = base + shift(plus, "x", 1).astype(jnp.float32) + shift(minus, "x", -1).astype(jnp.float32)
     out = jnp.concatenate([block[: M * T], total.astype(jnp.bfloat16)], 0)
     return out.reshape(2, M, T, S).transpose(0, 1, 3, 2)
 

time: 73.5 us -> 82 us (1.12); the launches traced: 73.2 us -> 80.5 us
  waiting for transfers between devices: 14.7 us -> 19.4 us
  starting transfers between devices: 30.8 us -> 35.3 us
  local copies, waits for them, and re-layouts: 1.5 us -> 0.36 us
  other arithmetic: 2.29 us -> 1.45 us
    ppermute x8 -> x14, waiting for transfers between devices: 5.21 us -> 16.9 us  [shift(): return lax.ppermute(value, axis, [(i, (i + d) % 4) for i in range(4)])]
    ppermute x8 -> x14, starting transfers between devices: 12.5 us -> 22.9 us  [shift(): return lax.ppermute(value, axis, [(i, (i + d) % 4) for i in range(4)])]
    ppermute x7 -> x3, starting transfers between devices: 13.9 us -> 8.15 us  [the longest x1 3.64 us: local(): down = lax.ppermute(top, ('z', 'core'), down)]
    ppermute x7 -> x3, waiting for transfers between devices: 8.02 us -> 2.47 us  [the longest x1 1.94 us: local(): down = lax.ppermute(top, ('z', 'core'), down)]
    all_to_all x1, waiting for transfers between devices: 1.49 us -> 0.01 us  [local(): mine = lax.all_to_all(send, 'x', 0, 0, tiled=True)]
    slice x2 -> x1, local copies, waits for them, and re-layouts: 1.01 us -> 0.03 us  [local(): gains[1].reshape(4, Q)]
  transfers between devices with their start and end apart: 16 -> 18, of which waited for: 6 -> 7; matrix products, arithmetic and copies ran while one was open for 2% -> 0% of each run, Pallas kernels for 27% -> 22%
where the time goes in v6:
time: 82 us; the launch traced here: 80.5 us
  starting transfers between devices  35.3 us (43%)
  Pallas kernels  23.8 us (29%)
  waiting for transfers between devices  19.4 us (24%)
  other arithmetic  1.45 us (2%)
    ppermute x14, starting transfers between devices, shift(): return lax.ppermute(value, axis, [(i, (i + d) % 4) for i in range(4)])  22.9 us
    ppermute x14, waiting for transfers between devices, shift(): return lax.ppermute(value, axis, [(i, (i + d) % 4) for i in range(4)])  16.9 us
    pallas_call x1, Pallas kernels, first(): pl.pallas_call(first_kernel, grid_spec=pltpu.PrefetchScalarGridSpec(num_s...  11.6 us
    pallas_call x3, Pallas kernels, stage(): pl.pallas_call(kernel, grid_spec=pltpu.PrefetchScalarGridSpec(num_scalar_...  10 us
    all_to_all x1, starting transfers between devices, local(): mine = lax.all_to_all(send, 'x', 0, 0, tiled=True)  4.29 us
    ppermute x1, starting transfers between devices, local(): down = lax.ppermute(top, ('z', 'core'), down)  3.64 us
    ppermute x1, starting transfers between devices, local(): other = lax.ppermute(swap, 'core', [(0, 1), (1, 0)])  2.6 us
    pallas_call x1, Pallas kernels, prep(): pl.pallas_call(prep_kernel, grid_spec=pltpu.PrefetchScalarGridSpec(num_sc...  2.13 us
  transfers between devices with their start and end apart: 18, of which 7 were waited for; matrix products, arithmetic and copies ran while one was open for 0% of the time, Pallas kernels for 22%

profile of v6, /device:TPU:96, one launch (start us, length us, event | category | flops | bytes accessed | tf_op | source)
XLA Modules:
  0.0 80.5 jit_solution(10444462607988290923)
XLA Ops:
  0.0 2.1 %prep.1 = (bf16[4,240,384]{2,1,0:T(8,128)(2,1)}, bf16[32,1536]{1,0:T(8,128)(2,1)}, bf16[32,1536]{1,0:T(8,128)(2,1)}) custom-call(s32[1]{0:T(128)} %bitcast.4.core, bf16[2,480,1536]{2,1,0:T(8,128)(2,1)} %bitcast.19, bf16[4,512,1536]{2,1,0:T(8,128)(2,1)} %x_ref.1, bf16[4,512,1536]{2,1,0:T(8,128)(2,1)} %x_ref.1), custom_call_target="tpu_custom_call" | custom-call | bytes 1474560 | tf_op jit(solution)/shard_map/prep/pallas_call | solution.py:139
  2.2 4.3 %all-to-all-start = ((bf16[4,240,384]{2,1,0:T(8,128)(2,1)}), bf16[4,240,384]{2,1,0:T(8,128)(2,1)S(1)}, u32[]{:S(2)}, u32[]{:S(2)}) async-start(bf16[4,240,384]{2,1,0:T(8,128)(2,1)} %get-tuple-element.37), calls=%async_computation | async-start | bytes 1474560 | tf_op jit(solution)/shard_map/all_to_all | solution.py:260
  6.5 1.9 %collective-permute-start = (bf16[32,1536]{1,0:T(8,128)(2,1)}, bf16[32,1536]{1,0:T(8,128)(2,1)S(1)}, u32[]{:S(2)}, u32[]{:S(2)}) collective-permute-start(bf16[32,1536]{1,0:T(8,128)(2,1)} %get-tuple-element.33), channel_id=1, source_target_pairs={{0,1},{1,2},{2,3},{3,4},{4,5},{5,6},{6,7},{7,8},{8,9},{9,10},{10,1... | collective-permute-start | bytes 294920 | tf_op jit(solution)/shard_map/ppermute | solution.py:255
  8.4 3.6 %collective-permute-start.1 = (bf16[32,1536]{1,0:T(8,128)(2,1)}, bf16[32,1536]{1,0:T(8,128)(2,1)S(1)}, u32[]{:S(2)}, u32[]{:S(2)}) collective-permute-start(bf16[32,1536]{1,0:T(8,128)(2,1)} %get-tuple-element.34), channel_id=1, source_target_pairs={{1,0},{2,1},{3,2},{4,3},{5,4},{6,5},{7,6},{8,7},{9,8},{10,9},{11,1... | collective-permute-start | bytes 294920 | tf_op jit(solution)/shard_map/ppermute | solution.py:256
  12.1 0.5 collective-permute-done.up_ref
  12.6 1.9 %collective-permute-done.1.down_ref = bf16[32,1536]{1,0:T(8,128)(2,1)S(1)} collective-permute-done((bf16[32,1536]{1,0:T(8,128)(2,1)}, bf16[32,1536]{1,0:T(8,128)(2,1)S(1)}, u32[]{:S(2)}, u32[]{:S(2)}) %collective-permute-start.1) | collective-permute-done | bytes 98336 | tf_op jit(solution)/shard_map/ppermute | solution.py:256
  14.6 11.6 %first.1 = (bf16[400,512]{1,0:T(8,128)(2,1)S(1)}, f32[17,128]{1,0:T(8,128)S(1)}) custom-call(s32[4]{0:T(128)S(1)} %pad_add_fusion.info, bf16[4,512,1536]{2,1,0:T(8,128)(2,1)} %x_ref.1, bf16[32,1536]{1,0:T(8,128)(2,1)S(1)} %collective-permute-done.up_ref, bf16[32,1536]{1,0:T(8,128)(2,1)S(1)} %collective-permute-done.1.down_ref, ...), custom_call_target="tpu_custom_call" | custom-call | flops 3019898880 | bytes 6291456 | tf_op jit(solution)/shard_map/first/pallas_call | solution.py:103
  26.2 2.1 %collective-permute-start.4 = (f32[17,128]{1,0:T(8,128)S(1)}, f32[17,128]{1,0:T(8,128)S(1)}, u32[]{:S(2)}, u32[]{:S(2)}) collective-permute-start(f32[17,128]{1,0:T(8,128)S(1)} %get-tuple-element.40), channel_id=1, source_target_pairs={{0,64},{64,128},{128,192},{192,0},{1,65},{65,129},{129,193},{193,1... | collective-permute-start | bytes 26120 | tf_op jit(solution)/shard_map/ppermute | solution.py:243
  28.4 1.3 %collective-permute-start.5 = (f32[17,128]{1,0:T(8,128)S(1)}, f32[17,128]{1,0:T(8,128)S(1)}, u32[]{:S(2)}, u32[]{:S(2)}) collective-permute-start(f32[17,128]{1,0:T(8,128)S(1)} %get-tuple-element.40), channel_id=1, source_target_pairs={{0,192},{64,0},{128,64},{192,128},{1,193},{65,1},{129,65},{193,129... | collective-permute-start | bytes 26120 | tf_op jit(solution)/shard_map/ppermute | solution.py:243
  29.7 2.2 %collective-permute-start.6 = (f32[17,128]{1,0:T(8,128)S(1)}, f32[17,128]{1,0:T(8,128)S(1)}, u32[]{:S(2)}, u32[]{:S(2)}) collective-permute-start(f32[17,128]{1,0:T(8,128)S(1)} %get-tuple-element.40), channel_id=1, source_target_pairs={{0,128},{64,192},{128,0},{192,64},{1,129},{65,193},{129,1},{193,65... | collective-permute-start | bytes 26120 | tf_op jit(solution)/shard_map/ppermute | solution.py:243
  31.9 1.6 %collective-permute-start.2 = (bf16[400,512]{1,0:T(8,128)(2,1)S(1)}, bf16[400,512]{1,0:T(8,128)(2,1)S(1)}, u32[]{:S(2)}, u32[]{:S(2)}) collective-permute-start(bf16[400,512]{1,0:T(8,128)(2,1)S(1)} %get-tuple-element.38.refs_0_.a_ref), channel_id=1, source_target_pairs={{0,16},{16,32},{32,48},{48,0},{1,17},{17,33},{33,49},{49,1},{2,18}... | collective-permute-start | bytes 1228808 | tf_op jit(solution)/shard_map/ppermute | solution.py:243
  33.5 1.7 %collective-permute-start.3 = (bf16[400,512]{1,0:T(8,128)(2,1)S(1)}, bf16[400,512]{1,0:T(8,128)(2,1)S(1)}, u32[]{:S(2)}, u32[]{:S(2)}) collective-permute-start(bf16[400,512]{1,0:T(8,128)(2,1)S(1)} %get-tuple-element.38.refs_0_.a_ref), channel_id=1, source_target_pairs={{0,48},{16,0},{32,16},{48,32},{1,49},{17,1},{33,17},{49,33},{2,50}... | collective-permute-start | bytes 1228808 | tf_op jit(solution)/shard_map/ppermute | solution.py:243
  35.2 1.3 %collective-permute-start.7 = (f32[17,128]{1,0:T(8,128)S(1)}, f32[17,128]{1,0:T(8,128)S(1)}, u32[]{:S(2)}, u32[]{:S(2)}) collective-permute-start(f32[17,128]{1,0:T(8,128)S(1)} %add_add_fusion.1), channel_id=1, source_target_pairs={{0,16},{16,32},{32,48},{48,0},{1,17},{17,33},{33,49},{49,1},{2,18}... | collective-permute-start | bytes 26120 | tf_op jit(solution)/shard_map/ppermute | solution.py:243
  36.4 2.0 %collective-permute-start.8 = (f32[17,128]{1,0:T(8,128)S(1)}, f32[17,128]{1,0:T(8,128)S(1)}, u32[]{:S(2)}, u32[]{:S(2)}) collective-permute-start(f32[17,128]{1,0:T(8,128)S(1)} %add_add_fusion.1), channel_id=1, source_target_pairs={{0,48},{16,0},{32,16},{48,32},{1,49},{17,1},{33,17},{49,33},{2,50}... | collective-permute-start | bytes 26120 | tf_op jit(solution)/shard_map/ppermute | solution.py:243
  38.5 1.6 %collective-permute-start.9 = (f32[17,128]{1,0:T(8,128)S(1)}, f32[17,128]{1,0:T(8,128)S(1)}, u32[]{:S(2)}, u32[]{:S(2)}) collective-permute-start(f32[17,128]{1,0:T(8,128)S(1)} %add_add_fusion.1), channel_id=1, source_target_pairs={{0,32},{16,48},{32,0},{48,16},{1,33},{17,49},{33,1},{49,17},{2,34}... | collective-permute-start | bytes 26120 | tf_op jit(solution)/shard_map/ppermute | solution.py:243
  40.1 2.9 %collective-permute-done.7 = f32[17,128]{1,0:T(8,128)S(1)} collective-permute-done((f32[17,128]{1,0:T(8,128)S(1)}, f32[17,128]{1,0:T(8,128)S(1)}, u32[]{:S(2)}, u32[]{:S(2)}) %collective-permute-start.7) | collective-permute-done | bytes 8736 | tf_op jit(solution)/shard_map/ppermute | solution.py:243
  43.0 0.7 collective-permute-done.8
  43.7 0.8 collective-permute-done.9
  44.5 2.6 %collective-permute-start.12 = (bf16[4,240,384]{2,1,0:T(8,128)(2,1)S(1)}, bf16[4,240,384]{2,1,0:T(8,128)(2,1)S(1)}, u32[]{:S(2)}, u32[]{:S(2)}) collective-permute-start(bf16[4,240,384]{2,1,0:T(8,128)(2,1)S(1)} %all-to-all-done.refs_7_.pa_ref.ma_ref.wa_ref), channel_id=1, source_target_pairs={{0,1},{1,0},{2,3},{3,2},{4,5},{5,4},{6,7},{7,6},{8,9},{9,8},{10,11... | collective-permute-start | bytes 2211848 | tf_op jit(solution)/shard_map/ppermute | solution.py:269
  47.2 2.1 %collective-permute-start.11 = (bf16[208,512]{1,0:T(8,128)(2,1)S(1)}, bf16[208,512]{1,0:T(8,128)(2,1)S(1)}, u32[]{:S(2)}, u32[]{:S(2)}) collective-permute-start(bf16[208,512]{1,0:T(8,128)(2,1)S(1)} %slice.32), channel_id=1, source_target_pairs={{0,48},{16,0},{32,16},{48,32},{1,49},{17,1},{33,17},{49,33},{2,50}... | collective-permute-start | bytes 638984 | tf_op jit(solution)/shard_map/ppermute | solution.py:243
  49.4 0.3 collective-permute-start.10
  49.8 7.6 %collective-permute-done.10.refs_3_ = bf16[192,512]{1,0:T(8,128)(2,1)S(1)} collective-permute-done((bf16[192,512]{1,0:T(8,128)(2,1)S(1)}, bf16[192,512]{1,0:T(8,128)(2,1)S(1)}, u32[]{:S(2)}, u32[]{:S(2)}) %collective-permute-start.10) | collective-permute-done | bytes 196640 | tf_op jit(solution)/shard_map/ppermute | solution.py:243
  57.5 3.9 %far.1 = (bf16[384,2176]{1,0:T(8,128)(2,1)S(1)}, bf16[192,512]{1,0:T(8,128)(2,1)S(1)}, bf16[192,512]{1,0:T(8,128)(2,1)S(1)}) custom-call(s32[9]{0:T(128)S(1)} %pad_add_fusion.1.order, bf16[400,512]{1,0:T(8,128)(2,1)S(1)} %get-tuple-element.38.refs_0_.a_ref, bf16[400,512]{1,0:T(8,128)(2,1)S(1)} %collective-permute-done.2.refs_1_, ...), custom_call_target="tpu_custom_call" | custom-call | flops 802160640 | bytes 3342336 | tf_op jit(solution)/shard_map/far/pallas_call | solution.py:210
  61.4 0.6 collective-permute-start.13
  62.0 2.7 %collective-permute-start.14 = (bf16[192,512]{1,0:T(8,128)(2,1)S(1)}, bf16[192,512]{1,0:T(8,128)(2,1)S(1)}, u32[]{:S(2)}, u32[]{:S(2)}) collective-permute-start(bf16[192,512]{1,0:T(8,128)(2,1)S(1)} %get-tuple-element.49), channel_id=1, source_target_pairs={{0,192},{64,0},{128,64},{192,128},{1,193},{65,1},{129,65},{193,129... | collective-permute-start | bytes 589832 | tf_op jit(solution)/shard_map/ppermute | solution.py:243
  64.7 3.8 %near.1 = (f32[384,512]{1,0:T(8,128)S(1)}, f32[384,512]{1,0:T(8,128)S(1)}) custom-call(s32[9]{0:T(128)S(1)} %pad_add_fusion.1.order, bf16[384,2176]{1,0:T(8,128)(2,1)S(1)} %get-tuple-element.54.h_ref, bf16[4,240,384]{2,1,0:T(8,128)(2,1)S(1)} %all-to-all-done.refs_7_.pa_ref.ma_ref.wa_ref, ...), custom_call_target="tpu_custom_call" | custom-call | flops 1604321280 | bytes 3342336 | tf_op jit(solution)/shard_map/near/pallas_call | solution.py:210
  68.6 0.1 add_convert_fusion.1
  68.9 3.2 %collective-permute-start.16 = (bf16[384,512]{1,0:T(8,128)(2,1)S(1)}, bf16[384,512]{1,0:T(8,128)(2,1)S(1)}, u32[]{:S(2)}, u32[]{:S(2)}) collective-permute-start(bf16[384,512]{1,0:T(8,128)(2,1)S(1)} %pad_maximum_fusion.2), channel_id=1, source_target_pairs={{0,192},{64,0},{128,64},{192,128},{1,193},{65,1},{129,65},{193,129... | collective-permute-start | bytes 1179656 | tf_op jit(solution)/shard_map/ppermute | solution.py:243
  72.2 2.3 %own.1 = f32[384,512]{1,0:T(8,128)S(1)} custom-call(s32[9]{0:T(128)S(1)} %pad_add_fusion.1.order, bf16[384,2176]{1,0:T(8,128)(2,1)S(1)} %get-tuple-element.54.h_ref, bf16[4,240,384]{2,1,0:T(8,128)(2,1)S(1)} %all-to-all-done.refs_7_.pa_ref.ma_ref.wa_ref, bf16[4,240,384]{2,1,0:T(8,128)(2,1)S(1)} %collective-permute-done.12.refs_8_.pb_ref.mb_ref.wb_ref, ...), custom_call_target="tpu_custom_call" | custom-call | flops 802160640 | bytes 3342336 | tf_op jit(solution)/shard_map/own/pallas_call | solution.py:210
  74.5 4.9 %collective-permute-done.15 = bf16[384,512]{1,0:T(8,128)(2,1)S(1)} collective-permute-done((bf16[384,512]{1,0:T(8,128)(2,1)S(1)}, bf16[384,512]{1,0:T(8,128)(2,1)S(1)}, u32[]{:S(2)}, u32[]{:S(2)}) %collective-permute-start.15) | collective-permute-done | bytes 393248 | tf_op jit(solution)/shard_map/ppermute | solution.py:243
  79.4 0.2 add_convert_fusion
  79.6 0.9 %pad_maximum_fusion = bf16[768,512]{1,0:T(8,128)(2,1)} fusion(bf16[384,512]{1,0:T(8,128)(2,1)S(1)} %add_convert_fusion, bf16[384,512]{1,0:T(8,128)(2,1)S(1)} %slice.30), kind=kLoop, calls=%fused_computation | loop fusion | flops 1572864 | bytes 1572864 | tf_op jit(solution)/shard_map/concatenate | solution.py:311
  (31 shorter events, 0.7 us)
Async XLA Ops:
  0.0 12.1 %copy-start = (f32[2,1536]{1,0:T(2,128)S(1)}, f32[2,1536]{1,0:T(2,128)}, u32[]{:S(2)}) copy-start(f32[2,1536]{1,0:T(2,128)} %param.5) | copy-start | bytes 36868
  2.2 24.0 %all-to-all-start = ((bf16[4,240,384]{2,1,0:T(8,128)(2,1)}), bf16[4,240,384]{2,1,0:T(8,128)(2,1)S(1)}, u32[]{:S(2)}, u32[]{:S(2)}) async-start(bf16[4,240,384]{2,1,0:T(8,128)(2,1)} %get-tuple-element.37), calls=%async_computation | async-start | bytes 1474560 | tf_op jit(solution)/shard_map/all_to_all | solution.py:260
  6.5 6.1 %collective-permute-start = (bf16[32,1536]{1,0:T(8,128)(2,1)}, bf16[32,1536]{1,0:T(8,128)(2,1)S(1)}, u32[]{:S(2)}, u32[]{:S(2)}) collective-permute-start(bf16[32,1536]{1,0:T(8,128)(2,1)} %get-tuple-element.33), channel_id=1, source_target_pairs={{0,1},{1,2},{2,3},{3,4},{4,5},{5,6},{6,7},{7,8},{8,9},{9,10},{10,1... | collective-permute-start | bytes 294920 | tf_op jit(solution)/shard_map/ppermute | solution.py:255
  8.4 6.2 %collective-permute-start.1 = (bf16[32,1536]{1,0:T(8,128)(2,1)}, bf16[32,1536]{1,0:T(8,128)(2,1)S(1)}, u32[]{:S(2)}, u32[]{:S(2)}) collective-permute-start(bf16[32,1536]{1,0:T(8,128)(2,1)} %get-tuple-element.34), channel_id=1, source_target_pairs={{1,0},{2,1},{3,2},{4,3},{5,4},{6,5},{7,6},{8,7},{9,8},{10,9},{11,1... | collective-permute-start | bytes 294920 | tf_op jit(solution)/shard_map/ppermute | solution.py:256
  26.2 8.9 %collective-permute-start.4 = (f32[17,128]{1,0:T(8,128)S(1)}, f32[17,128]{1,0:T(8,128)S(1)}, u32[]{:S(2)}, u32[]{:S(2)}) collective-permute-start(f32[17,128]{1,0:T(8,128)S(1)} %get-tuple-element.40), channel_id=1, source_target_pairs={{0,64},{64,128},{128,192},{192,0},{1,65},{65,129},{129,193},{193,1... | collective-permute-start | bytes 26120 | tf_op jit(solution)/shard_map/ppermute | solution.py:243
  28.4 6.8 %collective-permute-start.5 = (f32[17,128]{1,0:T(8,128)S(1)}, f32[17,128]{1,0:T(8,128)S(1)}, u32[]{:S(2)}, u32[]{:S(2)}) collective-permute-start(f32[17,128]{1,0:T(8,128)S(1)} %get-tuple-element.40), channel_id=1, source_target_pairs={{0,192},{64,0},{128,64},{192,128},{1,193},{65,1},{129,65},{193,129... | collective-permute-start | bytes 26120 | tf_op jit(solution)/shard_map/ppermute | solution.py:243
  29.7 5.5 %collective-permute-start.6 = (f32[17,128]{1,0:T(8,128)S(1)}, f32[17,128]{1,0:T(8,128)S(1)}, u32[]{:S(2)}, u32[]{:S(2)}) collective-permute-start(f32[17,128]{1,0:T(8,128)S(1)} %get-tuple-element.40), channel_id=1, source_target_pairs={{0,128},{64,192},{128,0},{192,64},{1,129},{65,193},{129,1},{193,65... | collective-permute-start | bytes 26120 | tf_op jit(solution)/shard_map/ppermute | solution.py:243
  31.9 12.6 %collective-permute-start.2 = (bf16[400,512]{1,0:T(8,128)(2,1)S(1)}, bf16[400,512]{1,0:T(8,128)(2,1)S(1)}, u32[]{:S(2)}, u32[]{:S(2)}) collective-permute-start(bf16[400,512]{1,0:T(8,128)(2,1)S(1)} %get-tuple-element.38.refs_0_.a_ref), channel_id=1, source_target_pairs={{0,16},{16,32},{32,48},{48,0},{1,17},{17,33},{33,49},{49,1},{2,18}... | collective-permute-start | bytes 1228808 | tf_op jit(solution)/shard_map/ppermute | solution.py:243
  33.5 11.0 %collective-permute-start.3 = (bf16[400,512]{1,0:T(8,128)(2,1)S(1)}, bf16[400,512]{1,0:T(8,128)(2,1)S(1)}, u32[]{:S(2)}, u32[]{:S(2)}) collective-permute-start(bf16[400,512]{1,0:T(8,128)(2,1)S(1)} %get-tuple-element.38.refs_0_.a_ref), channel_id=1, source_target_pairs={{0,48},{16,0},{32,16},{48,32},{1,49},{17,1},{33,17},{49,33},{2,50}... | collective-permute-start | bytes 1228808 | tf_op jit(solution)/shard_map/ppermute | solution.py:243
  35.2 7.8 %collective-permute-start.7 = (f32[17,128]{1,0:T(8,128)S(1)}, f32[17,128]{1,0:T(8,128)S(1)}, u32[]{:S(2)}, u32[]{:S(2)}) collective-permute-start(f32[17,128]{1,0:T(8,128)S(1)} %add_add_fusion.1), channel_id=1, source_target_pairs={{0,16},{16,32},{32,48},{48,0},{1,17},{17,33},{33,49},{49,1},{2,18}... | collective-permute-start | bytes 26120 | tf_op jit(solution)/shard_map/ppermute | solution.py:243
  36.4 7.2 %collective-permute-start.8 = (f32[17,128]{1,0:T(8,128)S(1)}, f32[17,128]{1,0:T(8,128)S(1)}, u32[]{:S(2)}, u32[]{:S(2)}) collective-permute-start(f32[17,128]{1,0:T(8,128)S(1)} %add_add_fusion.1), channel_id=1, source_target_pairs={{0,48},{16,0},{32,16},{48,32},{1,49},{17,1},{33,17},{49,33},{2,50}... | collective-permute-start | bytes 26120 | tf_op jit(solution)/shard_map/ppermute | solution.py:243
  38.5 6.0 %collective-permute-start.9 = (f32[17,128]{1,0:T(8,128)S(1)}, f32[17,128]{1,0:T(8,128)S(1)}, u32[]{:S(2)}, u32[]{:S(2)}) collective-permute-start(f32[17,128]{1,0:T(8,128)S(1)} %add_add_fusion.1), channel_id=1, source_target_pairs={{0,32},{16,48},{32,0},{48,16},{1,33},{17,49},{33,1},{49,17},{2,34}... | collective-permute-start | bytes 26120 | tf_op jit(solution)/shard_map/ppermute | solution.py:243
  44.5 12.9 %collective-permute-start.12 = (bf16[4,240,384]{2,1,0:T(8,128)(2,1)S(1)}, bf16[4,240,384]{2,1,0:T(8,128)(2,1)S(1)}, u32[]{:S(2)}, u32[]{:S(2)}) collective-permute-start(bf16[4,240,384]{2,1,0:T(8,128)(2,1)S(1)} %all-to-all-done.refs_7_.pa_ref.ma_ref.wa_ref), channel_id=1, source_target_pairs={{0,1},{1,0},{2,3},{3,2},{4,5},{5,4},{6,7},{7,6},{8,9},{9,8},{10,11... | collective-permute-start | bytes 2211848 | tf_op jit(solution)/shard_map/ppermute | solution.py:269
  47.2 10.2 %collective-permute-start.11 = (bf16[208,512]{1,0:T(8,128)(2,1)S(1)}, bf16[208,512]{1,0:T(8,128)(2,1)S(1)}, u32[]{:S(2)}, u32[]{:S(2)}) collective-permute-start(bf16[208,512]{1,0:T(8,128)(2,1)S(1)} %slice.32), channel_id=1, source_target_pairs={{0,48},{16,0},{32,16},{48,32},{1,49},{17,1},{33,17},{49,33},{2,50}... | collective-permute-start | bytes 638984 | tf_op jit(solution)/shard_map/ppermute | solution.py:243
  49.4 8.0 %collective-permute-start.10 = (bf16[192,512]{1,0:T(8,128)(2,1)S(1)}, bf16[192,512]{1,0:T(8,128)(2,1)S(1)}, u32[]{:S(2)}, u32[]{:S(2)}) collective-permute-start(bf16[192,512]{1,0:T(8,128)(2,1)S(1)} %slice.31), channel_id=1, source_target_pairs={{0,16},{16,32},{32,48},{48,0},{1,17},{17,33},{33,49},{49,1},{2,18}... | collective-permute-start | bytes 589832 | tf_op jit(solution)/shard_map/ppermute | solution.py:243
  61.4 7.2 %collective-permute-start.13 = (bf16[192,512]{1,0:T(8,128)(2,1)S(1)}, bf16[192,512]{1,0:T(8,128)(2,1)S(1)}, u32[]{:S(2)}, u32[]{:S(2)}) collective-permute-start(bf16[192,512]{1,0:T(8,128)(2,1)S(1)} %get-tuple-element.48), channel_id=1, source_target_pairs={{0,64},{64,128},{128,192},{192,0},{1,65},{65,129},{129,193},{193,1... | collective-permute-start | bytes 589832 | tf_op jit(solution)/shard_map/ppermute | solution.py:243
  62.0 6.5 %collective-permute-start.14 = (bf16[192,512]{1,0:T(8,128)(2,1)S(1)}, bf16[192,512]{1,0:T(8,128)(2,1)S(1)}, u32[]{:S(2)}, u32[]{:S(2)}) collective-permute-start(bf16[192,512]{1,0:T(8,128)(2,1)S(1)} %get-tuple-element.49), channel_id=1, source_target_pairs={{0,192},{64,0},{128,64},{192,128},{1,193},{65,1},{129,65},{193,129... | collective-permute-start | bytes 589832 | tf_op jit(solution)/shard_map/ppermute | solution.py:243
  68.8 10.6 %collective-permute-start.15 = (bf16[384,512]{1,0:T(8,128)(2,1)S(1)}, bf16[384,512]{1,0:T(8,128)(2,1)S(1)}, u32[]{:S(2)}, u32[]{:S(2)}) collective-permute-start(bf16[384,512]{1,0:T(8,128)(2,1)S(1)} %pad_maximum_fusion.1), channel_id=1, source_target_pairs={{0,64},{64,128},{128,192},{192,0},{1,65},{65,129},{129,193},{193,1... | collective-permute-start | bytes 1179656 | tf_op jit(solution)/shard_map/ppermute | solution.py:243
  68.9 10.5 %collective-permute-start.16 = (bf16[384,512]{1,0:T(8,128)(2,1)S(1)}, bf16[384,512]{1,0:T(8,128)(2,1)S(1)}, u32[]{:S(2)}, u32[]{:S(2)}) collective-permute-start(bf16[384,512]{1,0:T(8,128)(2,1)S(1)} %pad_maximum_fusion.2), channel_id=1, source_target_pairs={{0,192},{64,0},{128,64},{192,128},{1,193},{65,1},{129,65},{193,129... | collective-permute-start | bytes 1179656 | tf_op jit(solution)/shard_map/ppermute | solution.py:243

commit v7 on v4

--- a/solution.py
+++ b/solution.py
@@ -250,12 +250,14 @@
     gain = jnp.broadcast_to(gain, (Q, 128))
     block, sq = first(held, halo, gains[0:1], w, info)
     block, sq, mine = lax.optimization_barrier((block, sq, mine))
-    other = lax.ppermute(mine, "core", [(0, 1), (1, 0)])
     below, above = shift(block, "x", 1), shift(block, "x", -1)
+    sq = sq + lax.ppermute(sq, "y", [(i, i ^ 1) for i in range(4)])
+    sq = sq + lax.ppermute(sq, "y", [(i, i ^ 2) for i in range(4)])
+    sq, swap = lax.optimization_barrier((sq, mine))
+    sq = sq + lax.ppermute(sq, "x", [(i, i ^ 1) for i in range(4)])
+    other = lax.ppermute(swap, "core", [(0, 1), (1, 0)])
     got = [block, below, above, shift(below[:HB], "x", 1), shift(above[HB:], "x", -1)]
-    for axis in ("y", "x"):
-        sq = sq + lax.ppermute(sq, axis, [(i, i ^ 1) for i in range(4)])
-        sq = sq + lax.ppermute(sq, axis, [(i, i ^ 2) for i in range(4)])
+    sq = sq + lax.ppermute(sq, "x", [(i, i ^ 2) for i in range(4)])
     rel = [x, x + 3, x + 1, x + 2, y, y + 3, y + 1, y + 2]
     order = jnp.concatenate([jnp.stack(rel) % 4, core.reshape(1)]).astype(jnp.int32)
     half = jax.ShapeDtypeStruct((HB, S), jnp.bfloat16)

time: 73.5 us -> 74.2 us (level)
  waiting for transfers between devices: 14.7 us -> 16.5 us
  starting transfers between devices: 30.8 us -> 29.8 us
    ppermute x8, waiting for transfers between devices: 5.21 us -> 7.58 us  [shift(): return lax.ppermute(value, axis, [(i, (i + d) % 4) for i in range(4)])]
    ppermute x5, starting transfers between devices: 8.33 us -> 6.5 us  [the longest x1 2.54 us: local(): sq = sq + lax.ppermute(sq, 'y', [(i, i ^ 2) for i in range(4)])]
    ppermute x8, starting transfers between devices: 12.5 us -> 13.3 us  [shift(): return lax.ppermute(value, axis, [(i, (i + d) % 4) for i in range(4)])]
  transfers between devices with their start and end apart: 16 -> 16, of which waited for: 6 -> 7; matrix products, arithmetic and copies ran while one was open for 2% -> 2% of each run, Pallas kernels for 27% -> 27%
where the time goes in v7:
time: 74.2 us; the launch traced here: 73.9 us
  starting transfers between devices  29.8 us (40%)
  Pallas kernels  23.7 us (32%)
  waiting for transfers between devices  16.5 us (22%)
  other arithmetic  2.23 us (3%)
  local copies, waits for them, and re-layouts  1.5 us (2%)
    ppermute x8, starting transfers between devices, shift(): return lax.ppermute(value, axis, [(i, (i + d) % 4) for i in range(4)])  13.3 us
    pallas_call x1, Pallas kernels, first(): pl.pallas_call(first_kernel, grid_spec=pltpu.PrefetchScalarGridSpec(num_s...  11.3 us
    pallas_call x3, Pallas kernels, stage(): pl.pallas_call(kernel, grid_spec=pltpu.PrefetchScalarGridSpec(num_scalar_...  10 us
    ppermute x8, waiting for transfers between devices, shift(): return lax.ppermute(value, axis, [(i, (i + d) % 4) for i in range(4)])  7.58 us
    all_to_all x1, starting transfers between devices, local(): mine = lax.all_to_all(send, 'y', 0, 0, tiled=True)  4.46 us
    ppermute x1, waiting for transfers between devices, local(): sq = sq + lax.ppermute(sq, 'x', [(i, i ^ 2) for i in range(4)])  4.42 us
    ppermute x1, starting transfers between devices, local(): after = lax.ppermute(inputs[:, :4], ('z', 'core'), down)  3.64 us
    ppermute x1, waiting for transfers between devices, local(): sq = sq + lax.ppermute(sq, 'y', [(i, i ^ 2) for i in range(4)])  2.7 us
  transfers between devices with their start and end apart: 16, of which 7 were waited for; matrix products, arithmetic and copies ran while one was open for 2% of the time, Pallas kernels for 27%

profile of v7, /device:TPU:96, one launch (start us, length us, event | category | flops | bytes accessed | tf_op | source)
XLA Modules:
  0.0 73.9 jit_solution(5932584235588369475)
XLA Ops:
  0.0 1.0 %fusion.1 = (bf16[4,4,1536]{2,1,0:T(4,128)(2,1)S(1)}, bf16[4,4,1536]{2,1,0:T(4,128)(2,1)S(1)}) fusion(bf16[4,512,1536]{2,1,0:T(8,128)(2,1)} %x_ref.1), kind=kLoop, calls=%fused_computation.17 | loop fusion | bytes 196608 | tf_op jit(solution)/shard_map/slice | solution.py:241
  1.0 1.9 %collective-permute-start = (bf16[4,4,1536]{2,1,0:T(4,128)(2,1)S(1)}, bf16[4,4,1536]{2,1,0:T(4,128)(2,1)S(1)}, u32[]{:S(2)}, u32[]{:S(2)}) collective-permute-start(bf16[4,4,1536]{2,1,0:T(4,128)(2,1)S(1)} %get-tuple-element.47), channel_id=1, source_target_pairs={{0,1},{1,2},{2,3},{3,4},{4,5},{5,6},{6,7},{7,8},{8,9},{9,10},{10,1... | collective-permute-start | bytes 147464 | tf_op jit(solution)/shard_map/ppermute | solution.py:241
  2.9 3.6 %collective-permute-start.1 = (bf16[4,4,1536]{2,1,0:T(4,128)(2,1)S(1)}, bf16[4,4,1536]{2,1,0:T(4,128)(2,1)S(1)}, u32[]{:S(2)}, u32[]{:S(2)}) collective-permute-start(bf16[4,4,1536]{2,1,0:T(4,128)(2,1)S(1)} %get-tuple-element.48), channel_id=1, source_target_pairs={{1,0},{2,1},{3,2},{4,3},{5,4},{6,5},{7,6},{8,7},{9,8},{10,9},{11,1... | collective-permute-start | bytes 147464 | tf_op jit(solution)/shard_map/ppermute | solution.py:242
  6.6 2.4 %prep.1 = bf16[4,240,384]{2,1,0:T(8,128)(2,1)} custom-call(s32[1]{0:T(128)} %bitcast.4.core, bf16[2,480,1536]{2,1,0:T(8,128)(2,1)} %bitcast.21), custom_call_target="tpu_custom_call" | custom-call | bytes 1474560 | tf_op jit(solution)/shard_map/prep/pallas_call | solution.py:134
  9.0 4.5 %all-to-all-start = ((bf16[4,240,384]{2,1,0:T(8,128)(2,1)}), bf16[4,240,384]{2,1,0:T(8,128)(2,1)S(1)}, u32[]{:S(2)}, u32[]{:S(2)}) async-start(bf16[4,240,384]{2,1,0:T(8,128)(2,1)} %prep.1), calls=%async_computation | async-start | bytes 1474560 | tf_op jit(solution)/shard_map/all_to_all | solution.py:248
  13.6 11.3 %first.1 = (bf16[400,512]{1,0:T(8,128)(2,1)S(1)}, f32[1,2176]{1,0:T(1,128)S(1)}) custom-call(s32[4]{0:T(128)S(1)} %pad_add_fusion.info, bf16[4,512,1536]{2,1,0:T(8,128)(2,1)} %x_ref.1, bf16[32,1536]{1,0:T(8,128)(2,1)S(1)} %maximum_bitcast_fusion.halo_ref, f32[1,1536]{1,0:T(1,128)S(1)} %get-tuple-element.50.gain_ref, bf16[2,480,1536]{2,1,0:T(8,128)(2,1)} %bitcast.22), custom_call_target="tpu_custom_call" | custom-call | flops 3019898880 | bytes 6291456 | tf_op jit(solution)/shard_map/first/pallas_call | solution.py:99
  24.9 1.5 %all-to-all-done.wa_ref.pa_ref.ma_ref = bf16[4,240,384]{2,1,0:T(8,128)(2,1)S(1)} async-done(((bf16[4,240,384]{2,1,0:T(8,128)(2,1)}), bf16[4,240,384]{2,1,0:T(8,128)(2,1)S(1)}, u32[]{:S(2)}, u32[]{:S(2)}) %all-to-all-start) | async-done | bytes 737312 | tf_op jit(solution)/shard_map/all_to_all | solution.py:248
  26.4 0.6 collective-permute-start.6
  27.0 2.8 %collective-permute-start.3 = (bf16[400,512]{1,0:T(8,128)(2,1)S(1)}, bf16[400,512]{1,0:T(8,128)(2,1)S(1)}, u32[]{:S(2)}, u32[]{:S(2)}) collective-permute-start(bf16[400,512]{1,0:T(8,128)(2,1)S(1)} %get-tuple-element.30.a0.a_ref), channel_id=1, source_target_pairs={{0,192},{64,0},{128,64},{192,128},{1,193},{65,1},{129,65},{193,129... | collective-permute-start | bytes 1228808 | tf_op jit(solution)/shard_map/ppermute | solution.py:230
  29.8 0.3 collective-permute-done.6
  30.1 2.5 %collective-permute-start.7 = (f32[1,2176]{1,0:T(1,128)S(1)}, f32[1,2176]{1,0:T(1,128)S(1)}, u32[]{:S(2)}, u32[]{:S(2)}) collective-permute-start(f32[1,2176]{1,0:T(1,128)S(1)} %add.68), channel_id=1, source_target_pairs={{0,32},{16,48},{32,0},{48,16},{1,33},{17,49},{33,1},{49,17},{2,34}... | collective-permute-start | bytes 26120 | tf_op jit(solution)/shard_map/ppermute | solution.py:255
  32.6 2.7 %collective-permute-done.7 = f32[1,2176]{1,0:T(1,128)S(1)} collective-permute-done((f32[1,2176]{1,0:T(1,128)S(1)}, f32[1,2176]{1,0:T(1,128)S(1)}, u32[]{:S(2)}, u32[]{:S(2)}) %collective-permute-start.7) | collective-permute-done | bytes 8736 | tf_op jit(solution)/shard_map/ppermute | solution.py:255
  35.4 0.1 collective-permute-start.10
  35.5 1.5 %collective-permute-start.8 = (f32[1,2176]{1,0:T(1,128)S(1)}, f32[1,2176]{1,0:T(1,128)S(1)}, u32[]{:S(2)}, u32[]{:S(2)}) collective-permute-start(f32[1,2176]{1,0:T(1,128)S(1)} %add.69), channel_id=1, source_target_pairs={{0,64},{64,0},{128,192},{192,128},{1,65},{65,1},{129,193},{193,129... | collective-permute-start | bytes 26120 | tf_op jit(solution)/shard_map/ppermute | solution.py:257
  37.1 2.3 %collective-permute-done.3.a2 = bf16[400,512]{1,0:T(8,128)(2,1)S(1)} collective-permute-done((bf16[400,512]{1,0:T(8,128)(2,1)S(1)}, bf16[400,512]{1,0:T(8,128)(2,1)S(1)}, u32[]{:S(2)}, u32[]{:S(2)}) %collective-permute-start.3) | collective-permute-done | bytes 409632 | tf_op jit(solution)/shard_map/ppermute | solution.py:230
  39.4 3.8 %collective-permute-start.5 = (bf16[208,512]{1,0:T(8,128)(2,1)S(1)}, bf16[208,512]{1,0:T(8,128)(2,1)S(1)}, u32[]{:S(2)}, u32[]{:S(2)}) collective-permute-start(bf16[208,512]{1,0:T(8,128)(2,1)S(1)} %slice.47), channel_id=1, source_target_pairs={{0,192},{64,0},{128,64},{192,128},{1,193},{65,1},{129,65},{193,129... | collective-permute-start | bytes 638984 | tf_op jit(solution)/shard_map/ppermute | solution.py:230
  43.3 1.7 %collective-permute-start.9 = (f32[1,2176]{1,0:T(1,128)S(1)}, f32[1,2176]{1,0:T(1,128)}, u32[]{:S(2)}, u32[]{:S(2)}) collective-permute-start(f32[1,2176]{1,0:T(1,128)S(1)} %add.70), channel_id=1, source_target_pairs={{0,128},{64,192},{128,0},{192,64},{1,129},{65,193},{129,1},{193,65... | collective-permute-start | bytes 26120 | tf_op jit(solution)/shard_map/ppermute | solution.py:260
  45.2 0.1 broadcast_in_dim.7
  45.3 4.4 %collective-permute-done.9 = f32[1,2176]{1,0:T(1,128)} collective-permute-done((f32[1,2176]{1,0:T(1,128)S(1)}, f32[1,2176]{1,0:T(1,128)}, u32[]{:S(2)}, u32[]{:S(2)}) %collective-permute-start.9) | collective-permute-done | bytes 8736 | tf_op jit(solution)/shard_map/ppermute | solution.py:260
  49.7 0.7 add.71.sq_ref
  50.4 0.5 collective-permute-done.4.a3
  51.0 0.1 broadcast_in_dim.8.gain_ref
  51.1 3.9 %far.1 = (bf16[384,2176]{1,0:T(8,128)(2,1)S(1)}, bf16[192,512]{1,0:T(8,128)(2,1)S(1)}, bf16[192,512]{1,0:T(8,128)(2,1)S(1)}) custom-call(s32[9]{0:T(128)S(1)} %pad_add_fusion.1.order, bf16[400,512]{1,0:T(8,128)(2,1)S(1)} %get-tuple-element.30.a0.a_ref, bf16[400,512]{1,0:T(8,128)(2,1)S(1)} %collective-permute-done.2.a1, ...), custom_call_target="tpu_custom_call" | custom-call | flops 802160640 | bytes 3342336 | tf_op jit(solution)/shard_map/far/pallas_call | solution.py:197
  55.1 3.2 %collective-permute-start.12 = (bf16[192,512]{1,0:T(8,128)(2,1)S(1)}, bf16[192,512]{1,0:T(8,128)(2,1)S(1)}, u32[]{:S(2)}, u32[]{:S(2)}) collective-permute-start(bf16[192,512]{1,0:T(8,128)(2,1)S(1)} %get-tuple-element.39), channel_id=1, source_target_pairs={{0,48},{16,0},{32,16},{48,32},{1,49},{17,1},{33,17},{49,33},{2,50}... | collective-permute-start | bytes 589832 | tf_op jit(solution)/shard_map/ppermute | solution.py:230
  58.3 3.8 %near.1 = (f32[384,512]{1,0:T(8,128)S(1)}, f32[384,512]{1,0:T(8,128)S(1)}) custom-call(s32[9]{0:T(128)S(1)} %pad_add_fusion.1.order, bf16[384,2176]{1,0:T(8,128)(2,1)S(1)} %get-tuple-element.44.h_ref, bf16[4,240,384]{2,1,0:T(8,128)(2,1)S(1)} %all-to-all-done.wa_ref.pa_ref.ma_ref, bf16[4,240,384]{2,1,0:T(8,128)(2,1)S(1)} %collective-permute-done.10.wb_ref.pb_ref.mb_ref, ...), custom_call_target="tpu_custom_call" | custom-call | flops 1604321280 | bytes 3342336 | tf_op jit(solution)/shard_map/near/pallas_call | solution.py:197
  62.2 0.1 add_convert_fusion.1
  62.4 1.3 %collective-permute-start.13 = (bf16[384,512]{1,0:T(8,128)(2,1)S(1)}, bf16[384,512]{1,0:T(8,128)(2,1)S(1)}, u32[]{:S(2)}, u32[]{:S(2)}) collective-permute-start(bf16[384,512]{1,0:T(8,128)(2,1)S(1)} %pad_maximum_fusion.1), channel_id=1, source_target_pairs={{0,16},{16,32},{32,48},{48,0},{1,17},{17,33},{33,49},{49,1},{2,18}... | collective-permute-start | bytes 1179656 | tf_op jit(solution)/shard_map/ppermute | solution.py:230
  63.7 2.0 %collective-permute-start.14 = (bf16[384,512]{1,0:T(8,128)(2,1)S(1)}, bf16[384,512]{1,0:T(8,128)(2,1)S(1)}, u32[]{:S(2)}, u32[]{:S(2)}) collective-permute-start(bf16[384,512]{1,0:T(8,128)(2,1)S(1)} %pad_maximum_fusion.2), channel_id=1, source_target_pairs={{0,48},{16,0},{32,16},{48,32},{1,49},{17,1},{33,17},{49,33},{2,50}... | collective-permute-start | bytes 1179656 | tf_op jit(solution)/shard_map/ppermute | solution.py:230
  65.8 2.3 %own.1 = f32[384,512]{1,0:T(8,128)S(1)} custom-call(s32[9]{0:T(128)S(1)} %pad_add_fusion.1.order, bf16[384,2176]{1,0:T(8,128)(2,1)S(1)} %get-tuple-element.44.h_ref, bf16[4,240,384]{2,1,0:T(8,128)(2,1)S(1)} %all-to-all-done.wa_ref.pa_ref.ma_ref, bf16[4,240,384]{2,1,0:T(8,128)(2,1)S(1)} %collective-permute-done.10.wb_ref.pb_ref.mb_ref, ...), custom_call_target="tpu_custom_call" | custom-call | flops 802160640 | bytes 3342336 | tf_op jit(solution)/shard_map/own/pallas_call | solution.py:197
  68.1 4.7 %collective-permute-done.13 = bf16[384,512]{1,0:T(8,128)(2,1)S(1)} collective-permute-done((bf16[384,512]{1,0:T(8,128)(2,1)S(1)}, bf16[384,512]{1,0:T(8,128)(2,1)S(1)}, u32[]{:S(2)}, u32[]{:S(2)}) %collective-permute-start.13) | collective-permute-done | bytes 393248 | tf_op jit(solution)/shard_map/ppermute | solution.py:230
  72.8 0.2 add_convert_fusion
  73.0 0.9 %pad_maximum_fusion = bf16[768,512]{1,0:T(8,128)(2,1)} fusion(bf16[384,512]{1,0:T(8,128)(2,1)S(1)} %add_convert_fusion, bf16[384,512]{1,0:T(8,128)(2,1)S(1)} %slice.38), kind=kLoop, calls=%fused_computation | loop fusion | flops 1572864 | bytes 1572864 | tf_op jit(solution)/shard_map/concatenate | solution.py:301
  (32 shorter events, 0.8 us)
Async XLA Ops:
  1.0 12.6 %collective-permute-start = (bf16[4,4,1536]{2,1,0:T(4,128)(2,1)S(1)}, bf16[4,4,1536]{2,1,0:T(4,128)(2,1)S(1)}, u32[]{:S(2)}, u32[]{:S(2)}) collective-permute-start(bf16[4,4,1536]{2,1,0:T(4,128)(2,1)S(1)} %get-tuple-element.47), channel_id=1, source_target_pairs={{0,1},{1,2},{2,3},{3,4},{4,5},{5,6},{6,7},{7,8},{8,9},{9,10},{10,1... | collective-permute-start | bytes 147464 | tf_op jit(solution)/shard_map/ppermute | solution.py:241
  2.9 10.6 %collective-permute-start.1 = (bf16[4,4,1536]{2,1,0:T(4,128)(2,1)S(1)}, bf16[4,4,1536]{2,1,0:T(4,128)(2,1)S(1)}, u32[]{:S(2)}, u32[]{:S(2)}) collective-permute-start(bf16[4,4,1536]{2,1,0:T(4,128)(2,1)S(1)} %get-tuple-element.48), channel_id=1, source_target_pairs={{1,0},{2,1},{3,2},{4,3},{5,4},{6,5},{7,6},{8,7},{9,8},{10,9},{11,1... | collective-permute-start | bytes 147464 | tf_op jit(solution)/shard_map/ppermute | solution.py:242
  6.6 6.9 %copy-start = (f32[2,1536]{1,0:T(2,128)S(1)}, f32[2,1536]{1,0:T(2,128)}, u32[]{:S(2)}) copy-start(f32[2,1536]{1,0:T(2,128)} %param.5) | copy-start | bytes 36868
  9.0 17.4 %all-to-all-start = ((bf16[4,240,384]{2,1,0:T(8,128)(2,1)}), bf16[4,240,384]{2,1,0:T(8,128)(2,1)S(1)}, u32[]{:S(2)}, u32[]{:S(2)}) async-start(bf16[4,240,384]{2,1,0:T(8,128)(2,1)} %prep.1), calls=%async_computation | async-start | bytes 1474560 | tf_op jit(solution)/shard_map/all_to_all | solution.py:248
  26.4 3.7 %collective-permute-start.6 = (f32[1,2176]{1,0:T(1,128)S(1)}, f32[1,2176]{1,0:T(1,128)S(1)}, u32[]{:S(2)}, u32[]{:S(2)}) collective-permute-start(f32[1,2176]{1,0:T(1,128)S(1)} %get-tuple-element.31), channel_id=1, source_target_pairs={{0,16},{16,0},{32,48},{48,32},{1,17},{17,1},{33,49},{49,33},{2,18}... | collective-permute-start | bytes 26120 | tf_op jit(solution)/shard_map/ppermute | solution.py:254
  27.0 12.3 %collective-permute-start.3 = (bf16[400,512]{1,0:T(8,128)(2,1)S(1)}, bf16[400,512]{1,0:T(8,128)(2,1)S(1)}, u32[]{:S(2)}, u32[]{:S(2)}) collective-permute-start(bf16[400,512]{1,0:T(8,128)(2,1)S(1)} %get-tuple-element.30.a0.a_ref), channel_id=1, source_target_pairs={{0,192},{64,0},{128,64},{192,128},{1,193},{65,1},{129,65},{193,129... | collective-permute-start | bytes 1228808 | tf_op jit(solution)/shard_map/ppermute | solution.py:230
  29.8 13.3 %collective-permute-start.2 = (bf16[400,512]{1,0:T(8,128)(2,1)S(1)}, bf16[400,512]{1,0:T(8,128)(2,1)S(1)}, u32[]{:S(2)}, u32[]{:S(2)}) collective-permute-start(bf16[400,512]{1,0:T(8,128)(2,1)S(1)} %get-tuple-element.30.a0.a_ref), channel_id=1, source_target_pairs={{0,64},{64,128},{128,192},{192,0},{1,65},{65,129},{129,193},{193,1... | collective-permute-start | bytes 1228808 | tf_op jit(solution)/shard_map/ppermute | solution.py:230
  30.1 5.2 %collective-permute-start.7 = (f32[1,2176]{1,0:T(1,128)S(1)}, f32[1,2176]{1,0:T(1,128)S(1)}, u32[]{:S(2)}, u32[]{:S(2)}) collective-permute-start(f32[1,2176]{1,0:T(1,128)S(1)} %add.68), channel_id=1, source_target_pairs={{0,32},{16,48},{32,0},{48,16},{1,33},{17,49},{33,1},{49,17},{2,34}... | collective-permute-start | bytes 26120 | tf_op jit(solution)/shard_map/ppermute | solution.py:255
  35.4 15.6 %collective-permute-start.10 = (bf16[4,240,384]{2,1,0:T(8,128)(2,1)S(1)}, bf16[4,240,384]{2,1,0:T(8,128)(2,1)S(1)}, u32[]{:S(2)}, u32[]{:S(2)}) collective-permute-start(bf16[4,240,384]{2,1,0:T(8,128)(2,1)S(1)} %all-to-all-done.wa_ref.pa_ref.ma_ref), channel_id=1, source_target_pairs={{0,1},{1,0},{2,3},{3,2},{4,5},{5,4},{6,7},{7,6},{8,9},{9,8},{10,11... | collective-permute-start | bytes 2211848 | tf_op jit(solution)/shard_map/ppermute | solution.py:258
  35.5 7.7 %collective-permute-start.8 = (f32[1,2176]{1,0:T(1,128)S(1)}, f32[1,2176]{1,0:T(1,128)S(1)}, u32[]{:S(2)}, u32[]{:S(2)}) collective-permute-start(f32[1,2176]{1,0:T(1,128)S(1)} %add.69), channel_id=1, source_target_pairs={{0,64},{64,0},{128,192},{192,128},{1,65},{65,1},{129,193},{193,129... | collective-permute-start | bytes 26120 | tf_op jit(solution)/shard_map/ppermute | solution.py:257
  39.4 11.6 %collective-permute-start.5 = (bf16[208,512]{1,0:T(8,128)(2,1)S(1)}, bf16[208,512]{1,0:T(8,128)(2,1)S(1)}, u32[]{:S(2)}, u32[]{:S(2)}) collective-permute-start(bf16[208,512]{1,0:T(8,128)(2,1)S(1)} %slice.47), channel_id=1, source_target_pairs={{0,192},{64,0},{128,64},{192,128},{1,193},{65,1},{129,65},{193,129... | collective-permute-start | bytes 638984 | tf_op jit(solution)/shard_map/ppermute | solution.py:230
  43.2 7.8 %collective-permute-start.4 = (bf16[192,512]{1,0:T(8,128)(2,1)S(1)}, bf16[192,512]{1,0:T(8,128)(2,1)S(1)}, u32[]{:S(2)}, u32[]{:S(2)}) collective-permute-start(bf16[192,512]{1,0:T(8,128)(2,1)S(1)} %slice.46), channel_id=1, source_target_pairs={{0,64},{64,128},{128,192},{192,0},{1,65},{65,129},{129,193},{193,1... | collective-permute-start | bytes 589832 | tf_op jit(solution)/shard_map/ppermute | solution.py:230
  43.3 6.4 %collective-permute-start.9 = (f32[1,2176]{1,0:T(1,128)S(1)}, f32[1,2176]{1,0:T(1,128)}, u32[]{:S(2)}, u32[]{:S(2)}) collective-permute-start(f32[1,2176]{1,0:T(1,128)S(1)} %add.70), channel_id=1, source_target_pairs={{0,128},{64,192},{128,0},{192,64},{1,129},{65,193},{129,1},{193,65... | collective-permute-start | bytes 26120 | tf_op jit(solution)/shard_map/ppermute | solution.py:260
  55.0 7.2 %collective-permute-start.11 = (bf16[192,512]{1,0:T(8,128)(2,1)S(1)}, bf16[192,512]{1,0:T(8,128)(2,1)S(1)}, u32[]{:S(2)}, u32[]{:S(2)}) collective-permute-start(bf16[192,512]{1,0:T(8,128)(2,1)S(1)} %get-tuple-element.38), channel_id=1, source_target_pairs={{0,16},{16,32},{32,48},{48,0},{1,17},{17,33},{33,49},{49,1},{2,18}... | collective-permute-start | bytes 589832 | tf_op jit(solution)/shard_map/ppermute | solution.py:230
  55.1 7.1 %collective-permute-start.12 = (bf16[192,512]{1,0:T(8,128)(2,1)S(1)}, bf16[192,512]{1,0:T(8,128)(2,1)S(1)}, u32[]{:S(2)}, u32[]{:S(2)}) collective-permute-start(bf16[192,512]{1,0:T(8,128)(2,1)S(1)} %get-tuple-element.39), channel_id=1, source_target_pairs={{0,48},{16,0},{32,16},{48,32},{1,49},{17,1},{33,17},{49,33},{2,50}... | collective-permute-start | bytes 589832 | tf_op jit(solution)/shard_map/ppermute | solution.py:230
  62.4 10.4 %collective-permute-start.13 = (bf16[384,512]{1,0:T(8,128)(2,1)S(1)}, bf16[384,512]{1,0:T(8,128)(2,1)S(1)}, u32[]{:S(2)}, u32[]{:S(2)}) collective-permute-start(bf16[384,512]{1,0:T(8,128)(2,1)S(1)} %pad_maximum_fusion.1), channel_id=1, source_target_pairs={{0,16},{16,32},{32,48},{48,0},{1,17},{17,33},{33,49},{49,1},{2,18}... | collective-permute-start | bytes 1179656 | tf_op jit(solution)/shard_map/ppermute | solution.py:230
  63.7 9.1 %collective-permute-start.14 = (bf16[384,512]{1,0:T(8,128)(2,1)S(1)}, bf16[384,512]{1,0:T(8,128)(2,1)S(1)}, u32[]{:S(2)}, u32[]{:S(2)}) collective-permute-start(bf16[384,512]{1,0:T(8,128)(2,1)S(1)} %pad_maximum_fusion.2), channel_id=1, source_target_pairs={{0,48},{16,0},{32,16},{48,32},{1,49},{17,1},{33,17},{49,33},{2,50}... | collective-permute-start | bytes 1179656 | tf_op jit(solution)/shard_map/ppermute | solution.py:230

commit v8 on v4

--- a/solution.py
+++ b/solution.py
@@ -253,9 +253,8 @@
     other = lax.ppermute(mine, "core", [(0, 1), (1, 0)])
     below, above = shift(block, "x", 1), shift(block, "x", -1)
     got = [block, below, above, shift(below[:HB], "x", 1), shift(above[HB:], "x", -1)]
-    for axis in ("y", "x"):
-        sq = sq + lax.ppermute(sq, axis, [(i, i ^ 1) for i in range(4)])
-        sq = sq + lax.ppermute(sq, axis, [(i, i ^ 2) for i in range(4)])
+    for axis, bit in (("y", 1), ("y", 2), ("x", 2), ("x", 1)):
+        sq = sq + lax.ppermute(sq, axis, [(i, i ^ bit) for i in range(4)])
     rel = [x, x + 3, x + 1, x + 2, y, y + 3, y + 1, y + 2]
     order = jnp.concatenate([jnp.stack(rel) % 4, core.reshape(1)]).astype(jnp.int32)
     half = jax.ShapeDtypeStruct((HB, S), jnp.bfloat16)

time: 73.5 us -> 73.2 us (level)
  starting transfers between devices: 30.8 us -> 29.9 us
    ppermute x8, waiting for transfers between devices: 5.21 us -> 6.29 us  [shift(): return lax.ppermute(value, axis, [(i, (i + d) % 4) for i in range(4)])]
  transfers between devices with their start and end apart: 16 -> 16, of which waited for: 6 -> 9; matrix products, arithmetic and copies ran while one was open for 2% -> 2% of each run, Pallas kernels for 27% -> 27%
where the time goes in v8:
time: 73.2 us; the launch traced here: 73 us
  starting transfers between devices  29.9 us (41%)
  Pallas kernels  23.7 us (32%)
  waiting for transfers between devices  15.4 us (21%)
  other arithmetic  2.29 us (3%)
  local copies, waits for them, and re-layouts  1.5 us (2%)
    ppermute x8, starting transfers between devices, shift(): return lax.ppermute(value, axis, [(i, (i + d) % 4) for i in range(4)])  11.9 us
    pallas_call x1, Pallas kernels, first(): pl.pallas_call(first_kernel, grid_spec=pltpu.PrefetchScalarGridSpec(num_s...  11.3 us
    pallas_call x3, Pallas kernels, stage(): pl.pallas_call(kernel, grid_spec=pltpu.PrefetchScalarGridSpec(num_scalar_...  10 us
    ppermute x4, starting transfers between devices, local(): sq = sq + lax.ppermute(sq, axis, [(i, i ^ bit) for i in range(4)])  8 us
    ppermute x4, waiting for transfers between devices, local(): sq = sq + lax.ppermute(sq, axis, [(i, i ^ bit) for i in range(4)])  7.59 us
    ppermute x8, waiting for transfers between devices, shift(): return lax.ppermute(value, axis, [(i, (i + d) % 4) for i in range(4)])  6.29 us
    all_to_all x1, starting transfers between devices, local(): mine = lax.all_to_all(send, 'y', 0, 0, tiled=True)  4.46 us
    ppermute x1, starting transfers between devices, local(): after = lax.ppermute(inputs[:, :4], ('z', 'core'), down)  3.64 us
  transfers between devices with their start and end apart: 16, of which 9 were waited for; matrix products, arithmetic and copies ran while one was open for 2% of the time, Pallas kernels for 27%

profile of v8, /device:TPU:96, one launch (start us, length us, event | category | flops | bytes accessed | tf_op | source)
XLA Modules:
  0.0 73.0 jit_solution(17425396620691111488)
XLA Ops:
  0.0 1.0 %fusion.1 = (bf16[4,4,1536]{2,1,0:T(4,128)(2,1)S(1)}, bf16[4,4,1536]{2,1,0:T(4,128)(2,1)S(1)}) fusion(bf16[4,512,1536]{2,1,0:T(8,128)(2,1)} %x_ref.1), kind=kLoop, calls=%fused_computation.17 | loop fusion | bytes 196608 | tf_op jit(solution)/shard_map/slice | solution.py:241
  1.0 1.9 %collective-permute-start = (bf16[4,4,1536]{2,1,0:T(4,128)(2,1)S(1)}, bf16[4,4,1536]{2,1,0:T(4,128)(2,1)S(1)}, u32[]{:S(2)}, u32[]{:S(2)}) collective-permute-start(bf16[4,4,1536]{2,1,0:T(4,128)(2,1)S(1)} %get-tuple-element.43), channel_id=1, source_target_pairs={{0,1},{1,2},{2,3},{3,4},{4,5},{5,6},{6,7},{7,8},{8,9},{9,10},{10,1... | collective-permute-start | bytes 147464 | tf_op jit(solution)/shard_map/ppermute | solution.py:241
  2.9 3.6 %collective-permute-start.1 = (bf16[4,4,1536]{2,1,0:T(4,128)(2,1)S(1)}, bf16[4,4,1536]{2,1,0:T(4,128)(2,1)S(1)}, u32[]{:S(2)}, u32[]{:S(2)}) collective-permute-start(bf16[4,4,1536]{2,1,0:T(4,128)(2,1)S(1)} %get-tuple-element.44), channel_id=1, source_target_pairs={{1,0},{2,1},{3,2},{4,3},{5,4},{6,5},{7,6},{8,7},{9,8},{10,9},{11,1... | collective-permute-start | bytes 147464 | tf_op jit(solution)/shard_map/ppermute | solution.py:242
  6.6 2.4 %prep.1 = bf16[4,240,384]{2,1,0:T(8,128)(2,1)} custom-call(s32[1]{0:T(128)} %bitcast.4.core, bf16[2,480,1536]{2,1,0:T(8,128)(2,1)} %bitcast.21), custom_call_target="tpu_custom_call" | custom-call | bytes 1474560 | tf_op jit(solution)/shard_map/prep/pallas_call | solution.py:134
  9.0 4.5 %all-to-all-start = ((bf16[4,240,384]{2,1,0:T(8,128)(2,1)}), bf16[4,240,384]{2,1,0:T(8,128)(2,1)S(1)}, u32[]{:S(2)}, u32[]{:S(2)}) async-start(bf16[4,240,384]{2,1,0:T(8,128)(2,1)} %prep.1), calls=%async_computation | async-start | bytes 1474560 | tf_op jit(solution)/shard_map/all_to_all | solution.py:248
  13.6 11.3 %first.1 = (bf16[400,512]{1,0:T(8,128)(2,1)S(1)}, f32[1,2176]{1,0:T(1,128)S(1)}) custom-call(s32[4]{0:T(128)S(1)} %pad_add_fusion.info, bf16[4,512,1536]{2,1,0:T(8,128)(2,1)} %x_ref.1, bf16[32,1536]{1,0:T(8,128)(2,1)S(1)} %maximum_bitcast_fusion.halo_ref, f32[1,1536]{1,0:T(1,128)S(1)} %get-tuple-element.46.gain_ref, bf16[2,480,1536]{2,1,0:T(8,128)(2,1)} %bitcast.22), custom_call_target="tpu_custom_call" | custom-call | flops 3019898880 | bytes 6291456 | tf_op jit(solution)/shard_map/first/pallas_call | solution.py:99
  24.9 1.5 %all-to-all-done.wa_ref.pa_ref.ma_ref = bf16[4,240,384]{2,1,0:T(8,128)(2,1)S(1)} async-done(((bf16[4,240,384]{2,1,0:T(8,128)(2,1)}), bf16[4,240,384]{2,1,0:T(8,128)(2,1)S(1)}, u32[]{:S(2)}, u32[]{:S(2)}) %all-to-all-start) | async-done | bytes 737312 | tf_op jit(solution)/shard_map/all_to_all | solution.py:248
  26.4 2.8 %collective-permute-start.3 = (bf16[400,512]{1,0:T(8,128)(2,1)S(1)}, bf16[400,512]{1,0:T(8,128)(2,1)S(1)}, u32[]{:S(2)}, u32[]{:S(2)}) collective-permute-start(bf16[400,512]{1,0:T(8,128)(2,1)S(1)} %get-tuple-element.28.a0.a_ref), channel_id=1, source_target_pairs={{0,192},{64,0},{128,64},{192,128},{1,193},{65,1},{129,65},{193,129... | collective-permute-start | bytes 1228808 | tf_op jit(solution)/shard_map/ppermute | solution.py:230
  29.2 1.3 %collective-permute-start.6 = (f32[1,2176]{1,0:T(1,128)S(1)}, f32[1,2176]{1,0:T(1,128)S(1)}, u32[]{:S(2)}, u32[]{:S(2)}) collective-permute-start(f32[1,2176]{1,0:T(1,128)S(1)} %get-tuple-element.29), channel_id=1, source_target_pairs={{0,16},{16,0},{32,48},{48,32},{1,17},{17,1},{33,49},{49,33},{2,18}... | collective-permute-start | bytes 26120 | tf_op jit(solution)/shard_map/ppermute | solution.py:257
  30.5 2.4 %collective-permute-done.6 = f32[1,2176]{1,0:T(1,128)S(1)} collective-permute-done((f32[1,2176]{1,0:T(1,128)S(1)}, f32[1,2176]{1,0:T(1,128)S(1)}, u32[]{:S(2)}, u32[]{:S(2)}) %collective-permute-start.6) | collective-permute-done | bytes 8736 | tf_op jit(solution)/shard_map/ppermute | solution.py:257
  32.9 2.9 %collective-permute-start.7 = (f32[1,2176]{1,0:T(1,128)S(1)}, f32[1,2176]{1,0:T(1,128)S(1)}, u32[]{:S(2)}, u32[]{:S(2)}) collective-permute-start(f32[1,2176]{1,0:T(1,128)S(1)} %add.68), channel_id=1, source_target_pairs={{0,32},{16,48},{32,0},{48,16},{1,33},{17,49},{33,1},{49,17},{2,34}... | collective-permute-start | bytes 26120 | tf_op jit(solution)/shard_map/ppermute | solution.py:257
  35.8 2.3 %collective-permute-done.7 = f32[1,2176]{1,0:T(1,128)S(1)} collective-permute-done((f32[1,2176]{1,0:T(1,128)S(1)}, f32[1,2176]{1,0:T(1,128)S(1)}, u32[]{:S(2)}, u32[]{:S(2)}) %collective-permute-start.7) | collective-permute-done | bytes 8736 | tf_op jit(solution)/shard_map/ppermute | solution.py:257
  38.1 2.4 %collective-permute-start.8 = (f32[1,2176]{1,0:T(1,128)S(1)}, f32[1,2176]{1,0:T(1,128)S(1)}, u32[]{:S(2)}, u32[]{:S(2)}) collective-permute-start(f32[1,2176]{1,0:T(1,128)S(1)} %add.69), channel_id=1, source_target_pairs={{0,128},{64,192},{128,0},{192,64},{1,129},{65,193},{129,1},{193,65... | collective-permute-start | bytes 26120 | tf_op jit(solution)/shard_map/ppermute | solution.py:257
  40.5 1.5 %collective-permute-start.5 = (bf16[208,512]{1,0:T(8,128)(2,1)S(1)}, bf16[208,512]{1,0:T(8,128)(2,1)S(1)}, u32[]{:S(2)}, u32[]{:S(2)}) collective-permute-start(bf16[208,512]{1,0:T(8,128)(2,1)S(1)} %slice.47), channel_id=1, source_target_pairs={{0,192},{64,0},{128,64},{192,128},{1,193},{65,1},{129,65},{193,129... | collective-permute-start | bytes 638984 | tf_op jit(solution)/shard_map/ppermute | solution.py:230
  42.0 0.7 collective-permute-start.4
  42.7 0.6 collective-permute-done.8
  43.4 1.4 %collective-permute-start.9 = (f32[1,2176]{1,0:T(1,128)S(1)}, f32[1,2176]{1,0:T(1,128)}, u32[]{:S(2)}, u32[]{:S(2)}) collective-permute-start(f32[1,2176]{1,0:T(1,128)S(1)} %add.70), channel_id=1, source_target_pairs={{0,64},{64,0},{128,192},{192,128},{1,65},{65,1},{129,193},{193,129... | collective-permute-start | bytes 26120 | tf_op jit(solution)/shard_map/ppermute | solution.py:257
  45.1 2.3 %collective-permute-done.9 = f32[1,2176]{1,0:T(1,128)} collective-permute-done((f32[1,2176]{1,0:T(1,128)S(1)}, f32[1,2176]{1,0:T(1,128)}, u32[]{:S(2)}, u32[]{:S(2)}) %collective-permute-start.9) | collective-permute-done | bytes 8736 | tf_op jit(solution)/shard_map/ppermute | solution.py:257
  47.4 0.7 add.71.sq_ref
  48.1 1.0 %collective-permute-done.4.a3 = bf16[192,512]{1,0:T(8,128)(2,1)S(1)} collective-permute-done((bf16[192,512]{1,0:T(8,128)(2,1)S(1)}, bf16[192,512]{1,0:T(8,128)(2,1)S(1)}, u32[]{:S(2)}, u32[]{:S(2)}) %collective-permute-start.4) | collective-permute-done | bytes 196640 | tf_op jit(solution)/shard_map/ppermute | solution.py:230
  49.2 3.9 %far.1 = (bf16[384,2176]{1,0:T(8,128)(2,1)S(1)}, bf16[192,512]{1,0:T(8,128)(2,1)S(1)}, bf16[192,512]{1,0:T(8,128)(2,1)S(1)}) custom-call(s32[9]{0:T(128)S(1)} %pad_add_fusion.1.order, bf16[400,512]{1,0:T(8,128)(2,1)S(1)} %get-tuple-element.28.a0.a_ref, bf16[400,512]{1,0:T(8,128)(2,1)S(1)} %collective-permute-done.2.a1, ...), custom_call_target="tpu_custom_call" | custom-call | flops 802160640 | bytes 3342336 | tf_op jit(solution)/shard_map/far/pallas_call | solution.py:197
  53.1 2.3 %collective-permute-start.11 = (bf16[192,512]{1,0:T(8,128)(2,1)S(1)}, bf16[192,512]{1,0:T(8,128)(2,1)S(1)}, u32[]{:S(2)}, u32[]{:S(2)}) collective-permute-start(bf16[192,512]{1,0:T(8,128)(2,1)S(1)} %get-tuple-element.34), channel_id=1, source_target_pairs={{0,16},{16,32},{32,48},{48,0},{1,17},{17,33},{33,49},{49,1},{2,18}... | collective-permute-start | bytes 589832 | tf_op jit(solution)/shard_map/ppermute | solution.py:230
  55.4 1.3 %collective-permute-start.12 = (bf16[192,512]{1,0:T(8,128)(2,1)S(1)}, bf16[192,512]{1,0:T(8,128)(2,1)S(1)}, u32[]{:S(2)}, u32[]{:S(2)}) collective-permute-start(bf16[192,512]{1,0:T(8,128)(2,1)S(1)} %get-tuple-element.35), channel_id=1, source_target_pairs={{0,48},{16,0},{32,16},{48,32},{1,49},{17,1},{33,17},{49,33},{2,50}... | collective-permute-start | bytes 589832 | tf_op jit(solution)/shard_map/ppermute | solution.py:230
  56.7 3.8 %near.1 = (f32[384,512]{1,0:T(8,128)S(1)}, f32[384,512]{1,0:T(8,128)S(1)}) custom-call(s32[9]{0:T(128)S(1)} %pad_add_fusion.1.order, bf16[384,2176]{1,0:T(8,128)(2,1)S(1)} %get-tuple-element.40.h_ref, bf16[4,240,384]{2,1,0:T(8,128)(2,1)S(1)} %all-to-all-done.wa_ref.pa_ref.ma_ref, bf16[4,240,384]{2,1,0:T(8,128)(2,1)S(1)} %collective-permute-done.10.wb_ref.pb_ref.mb_ref, ...), custom_call_target="tpu_custom_call" | custom-call | flops 1604321280 | bytes 3342336 | tf_op jit(solution)/shard_map/near/pallas_call | solution.py:197
  60.6 0.5 collective-permute-done.12
  61.2 0.1 add_convert_fusion.1
  61.4 1.5 %collective-permute-start.13 = (bf16[384,512]{1,0:T(8,128)(2,1)S(1)}, bf16[384,512]{1,0:T(8,128)(2,1)S(1)}, u32[]{:S(2)}, u32[]{:S(2)}) collective-permute-start(bf16[384,512]{1,0:T(8,128)(2,1)S(1)} %pad_maximum_fusion.1), channel_id=1, source_target_pairs={{0,16},{16,32},{32,48},{48,0},{1,17},{17,33},{33,49},{49,1},{2,18}... | collective-permute-start | bytes 1179656 | tf_op jit(solution)/shard_map/ppermute | solution.py:230
  62.9 1.8 %collective-permute-start.14 = (bf16[384,512]{1,0:T(8,128)(2,1)S(1)}, bf16[384,512]{1,0:T(8,128)(2,1)S(1)}, u32[]{:S(2)}, u32[]{:S(2)}) collective-permute-start(bf16[384,512]{1,0:T(8,128)(2,1)S(1)} %pad_maximum_fusion.2), channel_id=1, source_target_pairs={{0,48},{16,0},{32,16},{48,32},{1,49},{17,1},{33,17},{49,33},{2,50}... | collective-permute-start | bytes 1179656 | tf_op jit(solution)/shard_map/ppermute | solution.py:230
  64.7 2.3 %own.1 = f32[384,512]{1,0:T(8,128)S(1)} custom-call(s32[9]{0:T(128)S(1)} %pad_add_fusion.1.order, bf16[384,2176]{1,0:T(8,128)(2,1)S(1)} %get-tuple-element.40.h_ref, bf16[4,240,384]{2,1,0:T(8,128)(2,1)S(1)} %all-to-all-done.wa_ref.pa_ref.ma_ref, bf16[4,240,384]{2,1,0:T(8,128)(2,1)S(1)} %collective-permute-done.10.wb_ref.pb_ref.mb_ref, ...), custom_call_target="tpu_custom_call" | custom-call | flops 802160640 | bytes 3342336 | tf_op jit(solution)/shard_map/own/pallas_call | solution.py:197
  67.0 4.8 %collective-permute-done.13 = bf16[384,512]{1,0:T(8,128)(2,1)S(1)} collective-permute-done((bf16[384,512]{1,0:T(8,128)(2,1)S(1)}, bf16[384,512]{1,0:T(8,128)(2,1)S(1)}, u32[]{:S(2)}, u32[]{:S(2)}) %collective-permute-start.13) | collective-permute-done | bytes 393248 | tf_op jit(solution)/shard_map/ppermute | solution.py:230
  71.8 0.2 add_convert_fusion
  72.0 0.9 %pad_maximum_fusion = bf16[768,512]{1,0:T(8,128)(2,1)} fusion(bf16[384,512]{1,0:T(8,128)(2,1)S(1)} %add_convert_fusion, bf16[384,512]{1,0:T(8,128)(2,1)S(1)} %slice.38), kind=kLoop, calls=%fused_computation | loop fusion | flops 1572864 | bytes 1572864 | tf_op jit(solution)/shard_map/concatenate | solution.py:298
  (32 shorter events, 0.9 us)
Async XLA Ops:
  1.0 12.6 %collective-permute-start = (bf16[4,4,1536]{2,1,0:T(4,128)(2,1)S(1)}, bf16[4,4,1536]{2,1,0:T(4,128)(2,1)S(1)}, u32[]{:S(2)}, u32[]{:S(2)}) collective-permute-start(bf16[4,4,1536]{2,1,0:T(4,128)(2,1)S(1)} %get-tuple-element.43), channel_id=1, source_target_pairs={{0,1},{1,2},{2,3},{3,4},{4,5},{5,6},{6,7},{7,8},{8,9},{9,10},{10,1... | collective-permute-start | bytes 147464 | tf_op jit(solution)/shard_map/ppermute | solution.py:241
  2.9 10.6 %collective-permute-start.1 = (bf16[4,4,1536]{2,1,0:T(4,128)(2,1)S(1)}, bf16[4,4,1536]{2,1,0:T(4,128)(2,1)S(1)}, u32[]{:S(2)}, u32[]{:S(2)}) collective-permute-start(bf16[4,4,1536]{2,1,0:T(4,128)(2,1)S(1)} %get-tuple-element.44), channel_id=1, source_target_pairs={{1,0},{2,1},{3,2},{4,3},{5,4},{6,5},{7,6},{8,7},{9,8},{10,9},{11,1... | collective-permute-start | bytes 147464 | tf_op jit(solution)/shard_map/ppermute | solution.py:242
  6.6 6.9 %copy-start = (f32[2,1536]{1,0:T(2,128)S(1)}, f32[2,1536]{1,0:T(2,128)}, u32[]{:S(2)}) copy-start(f32[2,1536]{1,0:T(2,128)} %param.5) | copy-start | bytes 36868
  9.0 17.4 %all-to-all-start = ((bf16[4,240,384]{2,1,0:T(8,128)(2,1)}), bf16[4,240,384]{2,1,0:T(8,128)(2,1)S(1)}, u32[]{:S(2)}, u32[]{:S(2)}) async-start(bf16[4,240,384]{2,1,0:T(8,128)(2,1)} %prep.1), calls=%async_computation | async-start | bytes 1474560 | tf_op jit(solution)/shard_map/all_to_all | solution.py:248
  26.4 14.1 %collective-permute-start.3 = (bf16[400,512]{1,0:T(8,128)(2,1)S(1)}, bf16[400,512]{1,0:T(8,128)(2,1)S(1)}, u32[]{:S(2)}, u32[]{:S(2)}) collective-permute-start(bf16[400,512]{1,0:T(8,128)(2,1)S(1)} %get-tuple-element.28.a0.a_ref), channel_id=1, source_target_pairs={{0,192},{64,0},{128,64},{192,128},{1,193},{65,1},{129,65},{193,129... | collective-permute-start | bytes 1228808 | tf_op jit(solution)/shard_map/ppermute | solution.py:230
  29.2 12.8 %collective-permute-start.2 = (bf16[400,512]{1,0:T(8,128)(2,1)S(1)}, bf16[400,512]{1,0:T(8,128)(2,1)S(1)}, u32[]{:S(2)}, u32[]{:S(2)}) collective-permute-start(bf16[400,512]{1,0:T(8,128)(2,1)S(1)} %get-tuple-element.28.a0.a_ref), channel_id=1, source_target_pairs={{0,64},{64,128},{128,192},{192,0},{1,65},{65,129},{129,193},{193,1... | collective-permute-start | bytes 1228808 | tf_op jit(solution)/shard_map/ppermute | solution.py:230
  29.2 19.9 %collective-permute-start.10 = (bf16[4,240,384]{2,1,0:T(8,128)(2,1)S(1)}, bf16[4,240,384]{2,1,0:T(8,128)(2,1)S(1)}, u32[]{:S(2)}, u32[]{:S(2)}) collective-permute-start(bf16[4,240,384]{2,1,0:T(8,128)(2,1)S(1)} %all-to-all-done.wa_ref.pa_ref.ma_ref), channel_id=1, source_target_pairs={{0,1},{1,0},{2,3},{3,2},{4,5},{5,4},{6,7},{7,6},{8,9},{9,8},{10,11... | collective-permute-start | bytes 2211848 | tf_op jit(solution)/shard_map/ppermute | solution.py:253
  29.2 3.7 %collective-permute-start.6 = (f32[1,2176]{1,0:T(1,128)S(1)}, f32[1,2176]{1,0:T(1,128)S(1)}, u32[]{:S(2)}, u32[]{:S(2)}) collective-permute-start(f32[1,2176]{1,0:T(1,128)S(1)} %get-tuple-element.29), channel_id=1, source_target_pairs={{0,16},{16,0},{32,48},{48,32},{1,17},{17,1},{33,49},{49,33},{2,18}... | collective-permute-start | bytes 26120 | tf_op jit(solution)/shard_map/ppermute | solution.py:257
  32.9 5.2 %collective-permute-start.7 = (f32[1,2176]{1,0:T(1,128)S(1)}, f32[1,2176]{1,0:T(1,128)S(1)}, u32[]{:S(2)}, u32[]{:S(2)}) collective-permute-start(f32[1,2176]{1,0:T(1,128)S(1)} %add.68), channel_id=1, source_target_pairs={{0,32},{16,48},{32,0},{48,16},{1,33},{17,49},{33,1},{49,17},{2,34}... | collective-permute-start | bytes 26120 | tf_op jit(solution)/shard_map/ppermute | solution.py:257
  38.1 5.2 %collective-permute-start.8 = (f32[1,2176]{1,0:T(1,128)S(1)}, f32[1,2176]{1,0:T(1,128)S(1)}, u32[]{:S(2)}, u32[]{:S(2)}) collective-permute-start(f32[1,2176]{1,0:T(1,128)S(1)} %add.69), channel_id=1, source_target_pairs={{0,128},{64,192},{128,0},{192,64},{1,129},{65,193},{129,1},{193,65... | collective-permute-start | bytes 26120 | tf_op jit(solution)/shard_map/ppermute | solution.py:257
  40.5 8.6 %collective-permute-start.5 = (bf16[208,512]{1,0:T(8,128)(2,1)S(1)}, bf16[208,512]{1,0:T(8,128)(2,1)S(1)}, u32[]{:S(2)}, u32[]{:S(2)}) collective-permute-start(bf16[208,512]{1,0:T(8,128)(2,1)S(1)} %slice.47), channel_id=1, source_target_pairs={{0,192},{64,0},{128,64},{192,128},{1,193},{65,1},{129,65},{193,129... | collective-permute-start | bytes 638984 | tf_op jit(solution)/shard_map/ppermute | solution.py:230
  42.0 7.1 %collective-permute-start.4 = (bf16[192,512]{1,0:T(8,128)(2,1)S(1)}, bf16[192,512]{1,0:T(8,128)(2,1)S(1)}, u32[]{:S(2)}, u32[]{:S(2)}) collective-permute-start(bf16[192,512]{1,0:T(8,128)(2,1)S(1)} %slice.46), channel_id=1, source_target_pairs={{0,64},{64,128},{128,192},{192,0},{1,65},{65,129},{129,193},{193,1... | collective-permute-start | bytes 589832 | tf_op jit(solution)/shard_map/ppermute | solution.py:230
  43.4 4.0 %collective-permute-start.9 = (f32[1,2176]{1,0:T(1,128)S(1)}, f32[1,2176]{1,0:T(1,128)}, u32[]{:S(2)}, u32[]{:S(2)}) collective-permute-start(f32[1,2176]{1,0:T(1,128)S(1)} %add.70), channel_id=1, source_target_pairs={{0,64},{64,0},{128,192},{192,128},{1,65},{65,1},{129,193},{193,129... | collective-permute-start | bytes 26120 | tf_op jit(solution)/shard_map/ppermute | solution.py:257
  53.1 7.5 %collective-permute-start.11 = (bf16[192,512]{1,0:T(8,128)(2,1)S(1)}, bf16[192,512]{1,0:T(8,128)(2,1)S(1)}, u32[]{:S(2)}, u32[]{:S(2)}) collective-permute-start(bf16[192,512]{1,0:T(8,128)(2,1)S(1)} %get-tuple-element.34), channel_id=1, source_target_pairs={{0,16},{16,32},{32,48},{48,0},{1,17},{17,33},{33,49},{49,1},{2,18}... | collective-permute-start | bytes 589832 | tf_op jit(solution)/shard_map/ppermute | solution.py:230
  55.4 5.7 %collective-permute-start.12 = (bf16[192,512]{1,0:T(8,128)(2,1)S(1)}, bf16[192,512]{1,0:T(8,128)(2,1)S(1)}, u32[]{:S(2)}, u32[]{:S(2)}) collective-permute-start(bf16[192,512]{1,0:T(8,128)(2,1)S(1)} %get-tuple-element.35), channel_id=1, source_target_pairs={{0,48},{16,0},{32,16},{48,32},{1,49},{17,1},{33,17},{49,33},{2,50}... | collective-permute-start | bytes 589832 | tf_op jit(solution)/shard_map/ppermute | solution.py:230
  61.4 10.4 %collective-permute-start.13 = (bf16[384,512]{1,0:T(8,128)(2,1)S(1)}, bf16[384,512]{1,0:T(8,128)(2,1)S(1)}, u32[]{:S(2)}, u32[]{:S(2)}) collective-permute-start(bf16[384,512]{1,0:T(8,128)(2,1)S(1)} %pad_maximum_fusion.1), channel_id=1, source_target_pairs={{0,16},{16,32},{32,48},{48,0},{1,17},{17,33},{33,49},{49,1},{2,18}... | collective-permute-start | bytes 1179656 | tf_op jit(solution)/shard_map/ppermute | solution.py:230
  62.9 8.9 %collective-permute-start.14 = (bf16[384,512]{1,0:T(8,128)(2,1)S(1)}, bf16[384,512]{1,0:T(8,128)(2,1)S(1)}, u32[]{:S(2)}, u32[]{:S(2)}) collective-permute-start(bf16[384,512]{1,0:T(8,128)(2,1)S(1)} %pad_maximum_fusion.2), channel_id=1, source_target_pairs={{0,48},{16,0},{32,16},{48,32},{1,49},{17,1},{33,17},{49,33},{2,50}... | collective-permute-start | bytes 1179656 | tf_op jit(solution)/shard_map/ppermute | solution.py:230
